TPU v7x, 256 devices: a whole 4x4x8 slice. The times are simulated.
256 devices in a mesh: ctx: 32 (over y, x, core), head: 8 (over z).
Axes of the slice: x: 4, y: 4, z: 8, core: 2. Of those that a mesh axis runs over, the one named last changes fastest.
Arguments:
- x_raw: bfloat16 [8192, 8192], P('ctx', 'head'), may hold values from -6 to 6
- bc_raw: bfloat16 [8192, 256], P('ctx'), may hold values from -6 to 6
- dt_raw: float32 [8192, 128], P('ctx', 'head')
- conv_x: float32 [4, 8192], P(None, 'head'), may hold values from -3 to 3
- conv_bc: float32 [4, 256], replicated, may hold values from -1.5 to 1.5
- a_log: float32 [128], P('head')
- dt_bias: float32 [128], P('head'), may hold values from -5 to -3
- skip_weight: float32 [128], P('head'), may hold values from 0.5 to 1.5
- segment: int32 [8192], replicated, may hold values from 0 to 7, as said below
- grad_y: bfloat16 [8192, 8192], P('ctx', 'head'), may hold values from -6 to 6
Outputs:
- ssd_out: bfloat16 [8192, 8192], P('ctx', 'head')
- grad_x: bfloat16 [8192, 8192], P('ctx', 'head')
- grad_bc: float32 [8192, 256], P(('ctx', 'head'))
- grad_dt: float32 [8192, 128], P('ctx', 'head')
- grad_conv_x: float32 [4, 8192], P(None, 'head')
- grad_conv_bc: float32 [4, 256], replicated
- grad_heads: float32 [3, 128], P(None, 'head')
Inputs may be any that keep to these rules, and one draw needn't show every extreme that they name: `segment`: ids of 8 packed documents: 0 at the first token, never falling, rising by at most one from a token to the next.
All inputs are finite; a program needn't handle non-finite values.
Results may differ from a plain program's by a relative error of at most 0.008.
Values may be sent and summed in bfloat16 or wider, within the bound.
No kernel may reach another device: no remote copies, remote signals or barrier semaphores. Data moves between devices by JAX's collectives and lax.ppermute only.
A program may use at most 192 MiB of HBM per device.

v0:
```python
import jax
import jax.numpy as jnp
from jax import lax
from jax.sharding import PartitionSpec as P


def passed_along(value, axis, by):
    peers = lax.axis_size(axis)
    pairs = [(i, i + by) for i in range(peers) if 0 <= i + by < peers]
    return lax.ppermute(value, axis, pairs)


def carried_in(value, axis, combine, identity, reverse):
    peers, here = (lax.axis_size(axis), lax.axis_index(axis))
    everything = jax.tree.map(lambda part: lax.all_gather(part, axis), value)
    start = jax.tree.map(
        lambda part, zero: jnp.broadcast_to(jnp.asarray(zero, part.dtype), part.shape),
        value,
        identity,
    )

    def hop(k, before):
        at = peers - 1 - k if reverse else k
        reached = at > here if reverse else at < here
        new = combine(before, jax.tree.map(lambda part: part[at], everything))
        return jax.tree.map(lambda a, b: jnp.where(reached, a, b), new, before)

    return lax.fori_loop(0, peers, hop, start)


def round_values(values):
    low = lax.optimization_barrier(lax.stop_gradient(values).astype(jnp.bfloat16))
    return values + (low.astype(jnp.float32) - lax.stop_gradient(values))


def conv_activate(extended, weight, seg_ext):
    tap_count = weight.shape[0]
    row_count = extended.shape[0] - tap_count + 1
    target = seg_ext[tap_count - 1 :]
    total = jnp.zeros((row_count, extended.shape[1]), jnp.float32)
    for tap_index in range(tap_count):
        match = (seg_ext[tap_index : tap_index + row_count] == target)[:, None]
        total = total + jnp.where(
            match, extended[tap_index : tap_index + row_count] * weight[tap_index][None, :], 0.0
        )
    return jax.nn.silu(total)


def window_parts(x_head, dt_head, rate, scores, b_vals, c_vals, seg_rows, continues):
    block_count = scores.shape[0]
    block_rows = scores.shape[1]
    head_dim = x_head.shape[1]
    state_width = b_vals.shape[1]
    log_decay = (-rate * dt_head).reshape(block_count, block_rows)
    cumul = jnp.cumsum(log_decay, axis=1)
    seg_blocks = seg_rows.reshape(block_count, block_rows)
    joins = jnp.concatenate(
        [
            jnp.reshape(continues, (1,)),
            (seg_blocks[1:, 0] == seg_blocks[:-1, -1]).astype(jnp.float32),
        ]
    )
    lower = jnp.tril(jnp.ones((block_rows, block_rows), jnp.bool_))
    linked = lower[None] & (seg_blocks[:, :, None] == seg_blocks[:, None, :])
    spread = jnp.where(linked, cumul[:, :, None] - cumul[:, None, :], 0.0)
    decay_mat = jnp.where(linked, jnp.exp(spread), 0.0)
    inputs = (dt_head[:, None] * x_head).reshape(block_count, block_rows, head_dim)
    y_diag = jnp.einsum("bts,bsp->btp", decay_mat * scores, inputs)
    same_end = seg_blocks == seg_blocks[:, -1:]
    end_weight = jnp.where(same_end, jnp.exp(jnp.where(same_end, cumul[:, -1:] - cumul, 0.0)), 0.0)
    b_blocks = b_vals.reshape(block_count, block_rows, state_width)
    block_states = jnp.einsum("bsp,bsn->bpn", end_weight[:, :, None] * inputs, b_blocks)
    keep = joins[:, None] * (seg_blocks == seg_blocks[:, :1]).astype(jnp.float32)
    in_weight = keep * jnp.exp(cumul)
    passes = in_weight[:, -1]

    def advance(carry, item):
        state_now, through = carry
        pass_now, block_state = item
        return ((pass_now * state_now + block_state, through * pass_now), (state_now, through))

    start_carry = (jnp.zeros((head_dim, state_width), jnp.float32), jnp.ones((), jnp.float32))
    (last_state, through), (incoming, before) = lax.scan(
        advance, start_carry, (passes, block_states)
    )
    c_blocks = c_vals.reshape(block_count, block_rows, state_width)
    y_inter = in_weight[:, :, None] * jnp.einsum("btn,bpn->btp", c_blocks, incoming)
    carry_weight = (in_weight * before[:, None]).reshape(-1)
    return ((y_diag + y_inter).reshape(-1, head_dim), last_state, carry_weight, through)


def combine(earlier, later_part):
    return (earlier[0] * later_part[0], later_part[0][:, None, None] * earlier[1] + later_part[1])


def local(x_raw, bc_raw, dt_raw, conv_x, conv_bc, a_log, dt_bias, skip_weight, segment, grad_y):
    row_count, channels = x_raw.shape
    state_width = bc_raw.shape[1] // 2
    head_count = dt_raw.shape[1]
    head_dim = channels // head_count
    margin = conv_x.shape[0] - 1
    block_rows = min(256, row_count)
    block_count = row_count // block_rows
    rim_rows = passed_along(
        jnp.concatenate([x_raw[row_count - margin :], bc_raw[row_count - margin :]], axis=1),
        "ctx",
        1,
    )
    first_row = lax.axis_index("ctx") * row_count
    padded_seg = jnp.concatenate([jnp.full((margin,), -1, jnp.int32), segment])
    seg_ext = lax.dynamic_slice_in_dim(padded_seg, first_row, row_count + margin)
    seg_own = seg_ext[margin:]
    continues = (seg_ext[margin] == seg_ext[margin - 1]).astype(jnp.float32)
    x_ext = jnp.concatenate([rim_rows[:, :channels], x_raw], axis=0).astype(jnp.float32)
    bc_ext = jnp.concatenate([rim_rows[:, channels:], bc_raw], axis=0).astype(jnp.float32)
    x_act = round_values(conv_activate(x_ext, conv_x, seg_ext))
    bc_act = round_values(conv_activate(bc_ext, conv_bc, seg_ext))
    b_vals = bc_act[:, :state_width]
    c_vals = bc_act[:, state_width:]
    b_low = b_vals.astype(jnp.bfloat16).reshape(block_count, block_rows, state_width)
    c_low = c_vals.astype(jnp.bfloat16).reshape(block_count, block_rows, state_width)
    scores = jnp.einsum("btn,bsn->bts", c_low, b_low, preferred_element_type=jnp.float32)
    pre_step = dt_raw + dt_bias[None, :]
    step_size = jax.nn.softplus(pre_step)
    rates = jnp.exp(a_log)
    x_heads = x_act.reshape(row_count, head_count, head_dim).transpose(1, 0, 2)
    dy_heads = (
        grad_y.astype(jnp.float32).reshape(row_count, head_count, head_dim).transpose(1, 0, 2)
    )
    dt_heads = step_size.T

    def all_heads(x_all, dt_all, rate_all, score_vals, b_part, c_part):

        def local_head(item):
            return window_parts(
                item[0], item[1], item[2], score_vals, b_part, c_part, seg_own, continues
            )

        return lax.map(local_head, (x_all, dt_all, rate_all))

    (y_local, state_local, carry_weight, through), pull_local = jax.vjp(
        all_heads, x_heads, dt_heads, rates, scores, b_vals, c_vals
    )
    weighted_dy = carry_weight[:, :, None] * dy_heads
    grad_terms = jnp.einsum("hrp,rn->hpn", weighted_dy, c_vals)
    identity = (
        jnp.ones((head_count,), jnp.float32),
        jnp.zeros((head_count, head_dim, state_width), jnp.float32),
    )
    state_in = carried_in((through, state_local), "ctx", combine, identity, False)[1]
    state_back = carried_in((through, grad_terms), "ctx", combine, identity, True)[1]
    carried = jnp.einsum("rn,hpn->hrp", c_vals, state_in)
    y_heads = y_local + carry_weight[:, :, None] * carried + skip_weight[:, None, None] * x_heads
    ssd_out = y_heads.transpose(1, 0, 2).reshape(row_count, channels).astype(jnp.bfloat16)
    grad_carry = jnp.sum(dy_heads * carried, axis=2)
    grad_through = jnp.sum(state_back * state_in, axis=(1, 2))
    grad_x_local, grad_dt_heads, grad_rates, grad_scores, grad_b, grad_c = pull_local(
        (dy_heads, state_back, grad_carry, grad_through)
    )
    grad_c = grad_c + jnp.einsum("hrp,hpn->rn", weighted_dy, state_in)
    grad_x_heads = grad_x_local + skip_weight[:, None, None] * dy_heads
    grad_skips = jnp.sum(dy_heads * x_heads, axis=(1, 2))
    b_blocks = b_vals.reshape(block_count, block_rows, state_width)
    c_blocks = c_vals.reshape(block_count, block_rows, state_width)
    grad_c = grad_c + jnp.einsum("bts,bsn->btn", grad_scores, b_blocks).reshape(
        row_count, state_width
    )
    grad_b = grad_b + jnp.einsum("bts,btn->bsn", grad_scores, c_blocks).reshape(
        row_count, state_width
    )
    grad_bc_act = jnp.concatenate([grad_b, grad_c], axis=1)
    grad_x_act = grad_x_heads.transpose(1, 0, 2).reshape(row_count, channels)
    _, pull_x = jax.vjp(
        lambda extended, weight: conv_activate(extended, weight, seg_ext), x_ext, conv_x
    )
    grad_x_ext, grad_wx = pull_x(grad_x_act)
    grad_dt = grad_dt_heads.T * jax.nn.sigmoid(pre_step)
    head_terms = jnp.stack([grad_rates * rates, jnp.sum(grad_dt, axis=0), grad_skips])
    share_rows = row_count // lax.axis_size("head")
    grad_bc_full = lax.psum(grad_bc_act, "head")
    _, pull_bc = jax.vjp(
        lambda extended, weight: conv_activate(extended, weight, seg_ext), bc_ext, conv_bc
    )
    grad_bc_ext, grad_wbc = pull_bc(grad_bc_full)
    spill = passed_along(
        jnp.concatenate([grad_x_ext[:margin], grad_bc_ext[:margin]], axis=1), "ctx", -1
    )
    spill_x = spill[:, :channels]
    bc_rows = grad_bc_ext[margin:] + jnp.pad(spill[:, channels:], ((row_count - margin, 0), (0, 0)))
    grad_bc = lax.dynamic_slice_in_dim(bc_rows, lax.axis_index("head") * share_rows, share_rows)
    grad_x = (grad_x_ext[margin:] + jnp.pad(spill_x, ((row_count - margin, 0), (0, 0)))).astype(
        jnp.bfloat16
    )
    sums = lax.psum((grad_wx, head_terms, grad_wbc), "ctx")
    grad_conv_bc = sums[2]
    return (ssd_out, grad_x, grad_bc, grad_dt, sums[0], grad_conv_bc, sums[1])


def solution(mesh):
    in_specs = (
        P("ctx", "head"),
        P("ctx", None),
        P("ctx", "head"),
        P(None, "head"),
        P(),
        P("head"),
        P("head"),
        P("head"),
        P(),
        P("ctx", "head"),
    )
    out_specs = (
        P("ctx", "head"),
        P("ctx", "head"),
        P(("ctx", "head"), None),
        P("ctx", "head"),
        P(None, "head"),
        P(),
        P(None, "head"),
    )
    return jax.shard_map(local, mesh=mesh, in_specs=in_specs, out_specs=out_specs, check_vma=False)
```

profile of v0, /device:TPU:1, one launch (start us, length us, event | category | flops | bytes accessed | tf_op | source)
XLA Modules:
  0.0 1214.0 jit_solution(13573260130482668698)
XLA Ops:
  8.6 4.5 collective-permute-start
  27.9 2.5 copy.44
  31.5 253.9 %while.128 = (s32[]{:T(128)}, f32[16,256,64]{1,2,0:T(8,128)}, f32[16,64,128]{2,1,0:T(8,128)}, f32[16,256]{1,0:T(8,128)S(1)}, f32[16]{0:T(128)S(1)}, /*index=5*/f...) while((s32[]{:T(128)}, f32[16,256,64]{1,2,0:T(8,128)}, ...), condition=%wide.region_3.4_spmd.clone, body=%wide.region_0.3_spmd.clone.sunk | while | flops 13676295 | bytes 2807126 | solution.py:139
  288.9 63.2 %all-reduce.21 = f32[512]{0:T(512)S(1)} all-reduce(f32[512]{0:T(512)S(1)} %dynamic-update-slice), channel_id=2, replica_groups=mesh['ctx'=32,'head'=8] {'ctx'}, use_global_device_ids=true, to_apply=%add.21 | all-reduce | flops 512 | bytes 4096
  354.2 12.9 %all-gather.8.cloned.1.call-done = f32[512,64,128]{2,1,0:T(8,128)} async-done(((f32[16,64,128]{2,1,0:T(8,128)}), f32[512,64,128]{2,1,0:T(8,128)}) %all-gather.8.cloned.1.call-update) | async-done | bytes 16777232 | tf_op jit(solution)/shard_map/all_gather | solution.py:15
  367.1 68.9 %while.130 = (s32[]{:T(128)}, f32[16,64,128]{2,1,0:T(8,128)}, s32[]{:T(128)}, f32[32,16]{1,0:T(8,128)S(1)}, f32[32,16,64,128]{3,2,1,0:T(8,128)}, /*index=5*/s32[]{:T(128)}, s32[]{:T(128)}, s32[]{:T(128)}, s32[]{:T(128)}) while((s32[]{:T(128)}, f32[16,64,128]{2,1,0:T(8,128)}, s32[]{:T(128)}, f32[32,16]{1,0:T(8,128)S(1)}, ...), condition=%wide.region_7.8_spmd.clone, body=%wide.region_6.7_spmd.clone.sunk | while | flops 524296 | bytes 1573223 | solution.py:28
  369.1 2.1 fusion.167
  373.4 2.1 fusion.167
  379.8 2.1 fusion.167
  381.9 2.2 fusion.167
  386.2 2.1 fusion.167
  388.3 2.1 fusion.167
  390.5 2.1 fusion.167
  392.6 2.2 fusion.167
  407.6 2.4 fusion.167
  414.3 2.2 fusion.167
  416.5 2.2 fusion.167
  420.7 2.2 fusion.167
  422.9 2.2 fusion.167
  425.1 2.4 fusion.167
  431.7 2.2 fusion.167
  433.9 2.2 fusion.167
  436.1 11.0 all-gather.6.cloned.1.call-done
  447.0 38.8 %while.129 = (s32[]{:T(128)}, f32[16,64,128]{2,1,0:T(8,128)S(1)}, s32[]{:T(128)}, f32[32,16]{1,0:T(8,128)S(1)}, f32[32,16,64,128]{3,2,1,0:T(8,128)}, /*index=5*/s32[]{:T(128)}, s32[]{:T(128)}) while((s32[]{:T(128)}, f32[16,64,128]{2,1,0:T(8,128)S(1)}, s32[]{:T(128)}, f32[32,16]{1,0:T(8,128)S(1)}, f32[32,16,64,128]{3,2,1,0:T(8,128)}, ...), condition=%wide.region_5.6_spmd.clone, body=%wide.region_4.5_spmd.clone.sunk | while | flops 524292 | bytes 1573161 | solution.py:28
  487.7 3.4 multiply_reduce_fusion.6
  493.4 505.8 %while.131 = (s32[]{:T(128)}, f32[1,256,256]{2,1,0:T(8,128)}, f32[256,128]{0,1:T(8,128)}, f32[256,128]{1,0:T(8,128)}, f32[16,256,64]{1,2,0:T(8,128)}, /*index=5*...) while((s32[]{:T(128)}, f32[1,256,256]{2,1,0:T(8,128)}, ...), condition=%wide.region_21.22_spmd.clone, body=%wide.region_10.21_spmd.clone.sunk | while | flops 30494472 | bytes 3932991 | solution.py:139
  1006.8 2.5 multiply_add_fusion.1
  1009.2 2.6 copy.51
  1011.9 2.3 multiply_reduce_fusion.5
  1020.1 53.9 %all-reduce.25.cloned.1.call-done = f32[256,256]{1,0:T(8,128)} async-done(((f32[256,256]{1,0:T(8,128)}), f32[256,256]{1,0:T(8,128)}) %all-reduce.25.cloned.1.call-update) | async-done | bytes 262160 | tf_op jit(solution)/shard_map/psum | solution.py:180
  1075.5 7.2 collective-permute-start.1
  1082.8 123.1 %all-reduce.22 = (f32[4,1024]{1,0:T(4,128)}, f32[4,256]{1,0:T(4,128)}, f32[3,16]{1,0:T(4,128)}) all-reduce(f32[4,1024]{1,0:T(4,128)S(1)} %pad_add_fusion.2, f32[4,256]{1,0:T(4,128)S(1)} %pad_add_fusion.4, f32[3,16]{1,0:T(4,128)S(1)} %pad_maximum_fusion.3), channel_id=1, replica_groups=mesh['ctx'=32,'head'=8] {'ctx'}, use_global_device_ids=true, to_apply=%region_27.28 | all-reduce | flops 5168 | bytes 41344 | tf_op jit(solution)/shard_map/psum | solution.py:194
  (1226 shorter events, 823.5 us)
Async XLA Ops:
  7.2 360.0 %all-gather.8.cloned.1.call-start = ((), (), s32[]{:S(2)}) async-start(), calls=%async_computation.2 | async-start | bytes 17301504 | tf_op jit(solution)/shard_map/all_gather | solution.py:15
  8.6 14.0 %collective-permute-start = (bf16[3,1280]{1,0:T(4,128)(2,1)S(1)}, bf16[3,1280]{1,0:T(4,128)(2,1)S(1)}, u32[]{:S(2)}, u32[]{:S(2)}) collective-permute-start(bf16[3,1280]{1,0:T(4,128)(2,1)S(1)} %pad_maximum_fusion.2), channel_id=1, source_target_pairs={{0,8},{8,16},{16,24},{24,32},{32,40},{40,48},{48,56},{56,64},{64,7... | collective-permute-start | bytes 23048 | tf_op jit(solution)/shard_map/ppermute | solution.py:10
  15.9 8.8 copy-start.20
  15.9 8.8 copy-start.22
  15.9 8.8 copy-start.24
  16.8 7.9 copy-start.12
  16.8 7.9 copy-start.14
  16.8 7.9 copy-start.16
  16.9 7.9 copy-start.18
  17.7 6.4 copy-start.26
  17.7 6.5 copy-start.28
  17.7 6.5 copy-start.30
  17.7 6.5 copy-start.32
  24.0 463.8 %copy-start.5 = (bf16[256,256]{1,0:T(8,128)(2,1)}, bf16[256,256]{1,0:T(8,128)(2,1)S(1)}, u32[]{:S(2)}) copy-start(bf16[256,256]{1,0:T(8,128)(2,1)S(1)} %subtract_add_fusion.1) | copy-start | bytes 393220
  286.5 160.5 %all-gather.6.cloned.1.call-start = ((), (), s32[]{:S(2)}) async-start(), calls=%async_computation.1 | async-start | bytes 17301504 | tf_op jit(solution)/shard_map/all_gather | solution.py:15
  287.3 786.8 %all-reduce.25.cloned.1.call-start = ((), (), s32[]{:S(2)}) async-start(), calls=%async_computation | async-start | bytes 524288 | tf_op jit(solution)/shard_map/psum | solution.py:180
  447.0 40.7 %copy-start.35 = (f32[16]{0:T(128)S(1)}, f32[16]{0:T(128)}, u32[]{:S(2)}) copy-start(f32[16]{0:T(128)} %param.25) | copy-start | bytes 196
  999.1 4.5 copy-start.6
  999.1 7.6 copy-start.36
  1006.7 5.1 copy-start.21
  1006.7 5.1 copy-start.23
  1006.8 5.1 copy-start.25
  1009.2 2.7 copy-start.1
  1011.9 2.4 copy-start.13
  1011.9 2.4 copy-start.15
  1018.6 55.4 %copy-start.8 = (f32[256,256]{1,0:T(8,128)S(1)}, f32[256,256]{1,0:T(8,128)}, u32[]{:S(2)}) copy-start(f32[256,256]{1,0:T(8,128)} %copy-done.7) | copy-start | bytes 786436
  1018.6 56.6 %copy-start.27 = (f32[1,256]{1,0:T(1,128)S(1)}, f32[1,256]{1,0:T(1,128)}, u32[]{:S(2)}) copy-start(f32[1,256]{1,0:T(1,128)} %copy-done.26) | copy-start | bytes 3076
  1018.6 56.6 %copy-start.29 = (f32[1,256]{1,0:T(1,128)S(1)}, f32[1,256]{1,0:T(1,128)}, u32[]{:S(2)}) copy-start(f32[1,256]{1,0:T(1,128)} %copy-done.28) | copy-start | bytes 3076
  1018.6 56.7 %copy-start.31 = (f32[1,256]{1,0:T(1,128)S(1)}, f32[1,256]{1,0:T(1,128)}, u32[]{:S(2)}) copy-start(f32[1,256]{1,0:T(1,128)} %copy-done.30) | copy-start | bytes 3076
  1018.6 56.7 %copy-start.33 = (f32[1,256]{1,0:T(1,128)S(1)}, f32[1,256]{1,0:T(1,128)}, u32[]{:S(2)}) copy-start(f32[1,256]{1,0:T(1,128)} %copy-done.32) | copy-start | bytes 3076
  1075.3 131.3 %copy-start.4 = (f32[259,1024]{1,0:T(8,128)S(1)}, f32[259,1024]{1,0:T(8,128)}, u32[]{:S(2)}) copy-start(f32[259,1024]{1,0:T(8,128)} %pad_add_fusion) | copy-start | bytes 3182596
  1075.5 130.3 %collective-permute-start.1 = (f32[3,1280]{1,0:T(4,128)S(1)}, f32[3,1280]{1,0:T(4,128)S(1)}, u32[]{:S(2)}, u32[]{:S(2)}) collective-permute-start(f32[3,1280]{1,0:T(4,128)S(1)} %pad_maximum_fusion.1), channel_id=1, source_target_pairs={{8,0},{16,8},{24,16},{32,24},{40,32},{48,40},{56,48},{64,56},{72,6... | collective-permute-start | bytes 46088 | tf_op jit(solution)/shard_map/ppermute | solution.py:10
  (13 other events, 22.6 us)
Sparse Core Ops, SparseCore 0:
  286.6 80.4 all-gather.7
  370.3 76.7 all-gather.5
  1006.8 67.1 all-reduce.24
where the time goes:
time: 1230 us; the launch traced here: 1210 us
  other arithmetic  376 us (31%)
  local copies, waits for them, and re-layouts  314 us (26%)
  blocking collectives  186 us (15%)
  matrix products  181 us (15%)
  waiting for transfers between devices  78.5 us (6%)
  loops' own time  50 us (4%)
  between operations  16.4 us (1%)
    dynamic_slice x192, local copies, waits for them, and re-layouts, all_heads(): return lax.map(local_head, (x_all, dt_all, rate_all))  158 us
    psum x1, blocking collectives, local(): sums = lax.psum((grad_wx, head_terms, grad_wbc), 'ctx')  123 us
    select_n x64, other arithmetic, hop(): return jax.tree.map(lambda a, b: jnp.where(reached, a, b), new, before)  106 us
    dynamic_update_slice x160, local copies, waits for them, and re-layouts, all_heads(): return lax.map(local_head, (x_all, dt_all, rate_all))  106 us
    dynamic_update_slice x80, other arithmetic, all_heads(): return lax.map(local_head, (x_all, dt_all, rate_all))  77.7 us
    dot_general x48, matrix products, window_parts(): y_diag = jnp.einsum('bts,bsp->btp', decay_mat * scores, inputs)  74.7 us
    dot_general x48, matrix products, window_parts(): jnp.einsum('bsp,bsn->bpn', end_weight[:, :, None] * inputs, b_blocks)  69.8 us
    unnamed x1, blocking collectives  63.2 us
  transfers between devices with their start and end apart: 5, of which 3 were waited for; matrix products, arithmetic and copies ran while one was open for 8% of the time, Pallas kernels for 0%

commit v1 on v0

v1 whole, which is shorter than its diff:
```python
import jax
import jax.numpy as jnp
from jax import lax
from jax.experimental import pallas as pl
from jax.experimental.pallas import tpu as pltpu
from jax.sharding import PartitionSpec as P

F32 = jnp.float32
BF16 = jnp.bfloat16
HIGH = lax.Precision.HIGHEST

BLK = 256
HD = 64
NS = 128
RIM = 16
VMEM = 48 * 1024 * 1024


def mm(a, b, precision=None):
    return lax.dot_general(
        a, b, (((1,), (0,)), ((), ())), precision=precision, preferred_element_type=F32
    )


def mm_nt(a, b, precision=None):
    return lax.dot_general(
        a, b, (((1,), (1,)), ((), ())), precision=precision, preferred_element_type=F32
    )


def iota(shape, dim):
    return lax.broadcasted_iota(jnp.int32, shape, dim)


def eye(n, dtype):
    return (iota((n, n), 0) == iota((n, n), 1)).astype(dtype)


def silu_and_slope(pre):
    sig = 1.0 / (1.0 + jnp.exp(-pre))
    return pre * sig, sig * (1.0 + pre * (1.0 - sig))


def tap_masks(seg_ref):
    target = seg_ref[3:4, :]
    return [(seg_ref[k : k + 1, :] == target).astype(F32) for k in range(4)]


def conv_rows(raw, rim, taps, masks):
    lane = iota((raw.shape[0], 128), 1)
    total = taps[:, 3:4] * raw
    for j in range(1, 4):
        rolled = pltpu.roll(raw, j, 1)
        before = pltpu.roll(rim, j, 1)
        shifted = jnp.concatenate(
            [jnp.where(lane < j, before, rolled[:, :128]), rolled[:, 128:]], axis=1
        )
        total = total + shifted * (taps[:, 3 - j : 4 - j] * masks[3 - j])
    return total


def conv_back(g, raw, rim, taps, masks):
    lane = iota((g.shape[0], 128), 1)
    grad = taps[:, 3:4] * g
    spill = jnp.zeros((g.shape[0], 128), F32)
    width = g.shape[1]
    row = iota((8, width), 0)
    weights = mm_nt((row == 3).astype(F32), g * raw, HIGH)
    for j in range(1, 4):
        masked = g * masks[3 - j]
        rolled = pltpu.roll(masked, width - j, 1)
        inner = jnp.concatenate(
            [rolled[:, :128], jnp.where(lane >= 128 - j, 0.0, rolled[:, 128:])], axis=1
        )
        outer = jnp.where(lane >= 128 - j, rolled[:, 128:], 0.0)
        tap = taps[:, 3 - j : 4 - j]
        grad = grad + tap * inner
        spill = spill + tap * outer
        weights = weights + mm_nt((row == 3 - j).astype(F32), inner * raw, HIGH)
        weights = weights + mm_nt((row[:, :128] == 3 - j).astype(F32), outer * rim, HIGH)
    return grad, spill, weights


def wide_rim(rim):
    return jnp.concatenate([jnp.zeros((128 - RIM, rim.shape[1]), BF16), rim], axis=0)


def local_kernel(
    x_ref, rim_ref, gy_ref, wx_ref, bc_ref, rimbc_ref, wbc_ref, dt_ref, hv_ref, seg_ref,
    pay_ref, xa_ref, slope_ref, y_ref, du_ref, rows_ref, dbc_ref, bcslope_ref, bctok_ref,
    scores_ref, link_ref, bct_ref, acol_ref, dg_ref,
):
    step = pl.program_id(0)
    ident = eye(BLK, BF16)

    @pl.when(step == 0)
    def _():
        masks = tap_masks(seg_ref)
        raw = mm_nt(ident, bc_ref[...])
        rim = mm_nt(ident, wide_rim(rimbc_ref[...]))
        taps = mm_nt(eye(BLK, F32), wbc_ref[...], HIGH)
        act, slope = silu_and_slope(conv_rows(raw, rim, taps, masks))
        bcslope_ref[...] = slope
        act = act.astype(BF16)
        bct_ref[...] = act
        token = mm_nt(ident, act).astype(BF16)
        bctok_ref[...] = token
        scores_ref[...] = mm_nt(token[:, NS:], token[:, :NS])
        seg_row = seg_ref[3:4, :]
        seg_col = mm_nt(ident, seg_ref[...].astype(BF16))[:, 3:4]
        later = iota((BLK, BLK), 0) >= iota((BLK, BLK), 1)
        linked = jnp.logical_and(later, seg_col == seg_row)
        link_ref[...] = jnp.where(linked, 0.0, -jnp.inf)
        heads = dt_ref.shape[1]
        head_eye = eye(heads, F32)
        per_head = mm_nt(head_eye, hv_ref[...], HIGH)
        rate = jnp.exp(per_head[:, 0:1])
        pre = mm_nt(head_eye, dt_ref[...], HIGH) + per_head[:, 1:2]
        dt = jnp.maximum(pre, 0.0) + jnp.log1p(jnp.exp(-jnp.abs(pre)))
        log_decay = -rate * dt
        upto = (iota((BLK, BLK), 0) <= iota((BLK, BLK), 1)).astype(F32)
        cumul = mm(log_decay, upto, HIGH)
        keep = (seg_row == seg_ref[2:3, 0:1]).astype(F32)
        same_end = seg_row == seg_row[:, BLK - 1 :]
        rows_ref[0] = dt
        rows_ref[1] = cumul
        rows_ref[2] = keep * jnp.exp(cumul)
        rows_ref[3] = jnp.exp(jnp.where(same_end, cumul[:, BLK - 1 :] - cumul, -jnp.inf))
        rows_ref[4] = 1.0 / (1.0 + jnp.exp(-pre))
        dg_ref[...] = jnp.zeros_like(dg_ref)

    masks = tap_masks(seg_ref)
    raw = mm_nt(ident, x_ref[...])
    rim = mm_nt(ident, wide_rim(rim_ref[...]))
    taps = mm_nt(eye(BLK, F32), wx_ref[...], HIGH)
    act, slope = silu_and_slope(conv_rows(raw, rim, taps, masks))
    slope_ref[...] = slope
    act = act.astype(BF16)
    xa_ref[...] = act
    act = act.astype(F32)
    gy = gy_ref[...]
    dy = mm_nt(ident, gy)
    dy_low = dy.astype(BF16)
    b_tok = bctok_ref[:, :NS]
    c_tok = bctok_ref[:, NS:]
    per_step = BLK // HD
    cumul_all = rows_ref[1]
    acol_ref[...] = mm_nt(eye(BLK, F32), cumul_all, HIGH)
    step_heads = step * per_step
    pick = (iota((cumul_all.shape[0], per_step), 0) == step_heads + iota(
        (cumul_all.shape[0], per_step), 1)).astype(F32)
    acols = mm(acol_ref[...], pick, HIGH)
    for k in range(per_step):
        head = step_heads + k
        lo, hi = k * HD, (k + 1) * HD
        dt = rows_ref[0, pl.ds(head, 1), :]
        arow = rows_ref[1, pl.ds(head, 1), :]
        carry = rows_ref[2, pl.ds(head, 1), :]
        end = rows_ref[3, pl.ds(head, 1), :]
        u = dt * act[lo:hi]
        u_low = u.astype(BF16)
        state = mm((end * u).astype(BF16), b_tok)
        back = mm((carry * dy[lo:hi]).astype(BF16), c_tok)
        through = carry[:, BLK - 1 :]
        t_hi = through.astype(BF16)
        t_rest = through - t_hi.astype(F32)
        t_mid = t_rest.astype(BF16)
        t_low = (t_rest - t_mid.astype(F32)).astype(BF16)
        which = iota((16, NS), 0)
        thr = jnp.where(
            which == 0, t_hi.astype(F32), jnp.where(which == 1, t_mid.astype(F32), t_low.astype(F32))
        ).astype(BF16)
        for half in range(2):
            j = 2 * k + half
            pay_ref[j, 0:32, :] = state[half * 32 : half * 32 + 32].astype(BF16)
            pay_ref[j, 32:64, :] = back[half * 32 : half * 32 + 32].astype(BF16)
            pay_ref[j, 64:80, :] = thr
        du_first = None
        for tb in range(2):
            t0, t1 = tb * 128, tb * 128 + 128
            decay = jnp.exp(acols[t0:t1, k : k + 1] - arow[:, :t1] + link_ref[t0:t1, :t1])
            mixed = (decay * scores_ref[t0:t1, :t1]).astype(BF16)
            y_ref[lo:hi, t0:t1] = mm_nt(u_low[:, :t1], mixed)
            du = mm(dy_low[lo:hi, t0:t1], mixed)
            if tb == 0:
                du_first = du
            else:
                du_ref[lo:hi, :128] = du_first + du[:, :128]
                du_ref[lo:hi, 128:] = du[:, 128:]
            dmix = mm(gy[t0:t1, lo:hi], u_low[:, :t1])
            dg_ref[t0:t1, :t1] += decay * dmix

    @pl.when(step == pl.num_programs(0) - 1)
    def _():
        dg = dg_ref[...].astype(BF16)
        dbc_ref[:NS, :] = mm(bct_ref[NS:, :], dg)
        dbc_ref[NS:, :] = mm_nt(bct_ref[:NS, :], dg)


def scan_kernel(peers, in_ref, out_ref):
    ahead = jnp.zeros((32, NS), F32)
    behind = jnp.zeros((32, NS), F32)
    for i in range(peers):
        def through(at):
            parts = in_ref[at, 64:80, :].astype(F32)
            return parts[0:1] + parts[1:2] + parts[2:3]

        out_ref[i, 0:32, :] = ahead.astype(BF16)
        ahead = through(i) * ahead + in_ref[i, 0:32, :].astype(F32)
        at = peers - 1 - i
        out_ref[at, 32:64, :] = behind.astype(BF16)
        behind = through(at) * behind + in_ref[at, 32:64, :].astype(F32)


def final_kernel(
    x_ref, rim_ref, gy_ref, wx_ref, bc_ref, rimbc_ref, wbc_ref, hv_ref, seg_ref,
    state_ref, xa_ref, slope_ref, y_ref, du_ref, rows_ref, dbc_ref, bcslope_ref, bctok_ref,
    out_ref, gx_ref, last_ref, spill_ref, gw_ref, gdt_ref, gh_ref, pay_ref,
    red_ref, acc_ref,
):
    step = pl.program_id(0)
    ident = eye(BLK, BF16)
    per_step = BLK // HD
    step_heads = step * per_step
    masks = tap_masks(seg_ref)
    heads = rows_ref.shape[1]

    @pl.when(step == 0)
    def _():
        acc_ref[...] = dbc_ref[...]

    state_in = state_ref[:, 0:32, :].reshape(BLK, NS)
    state_back = state_ref[:, 32:64, :].reshape(BLK, NS)
    b_tok = bctok_ref[:, :NS]
    c_tok = bctok_ref[:, NS:]
    dy = mm_nt(ident, gy_ref[...])
    carried = mm_nt(state_in, c_tok)
    from_end = mm_nt(state_back, b_tok)
    act = xa_ref[...].astype(F32)
    skips = mm_nt(eye(heads, F32), hv_ref[...], HIGH)[:, 2:3]
    skip_wide = jnp.broadcast_to(skips, (heads, BLK))
    both = state_in.astype(F32) * state_back.astype(F32)
    y_parts, g_parts, cdy_parts, eu_parts = [], [], [], []
    for k in range(per_step):
        head = step_heads + k
        lo, hi = k * HD, (k + 1) * HD
        dt = rows_ref[0, pl.ds(head, 1), :]
        carry = rows_ref[2, pl.ds(head, 1), :]
        end = rows_ref[3, pl.ds(head, 1), :]
        is_head = iota((heads, BLK), 0) == head
        skip = jnp.sum(jnp.where(is_head, skip_wide, 0.0), axis=0, keepdims=True)
        x_h = act[lo:hi]
        dy_h = dy[lo:hi]
        y_h = y_ref[lo:hi, :] + carry * carried[lo:hi]
        ext = end * from_end[lo:hi]
        du = du_ref[lo:hi, :] + ext
        u = dt * x_h
        u_low = u.astype(BF16).astype(F32)
        last_lane = iota((1, BLK), 1) == BLK - 1
        at_end = jnp.sum(jnp.sum(u_low * ext, axis=0, keepdims=True), axis=1, keepdims=True)
        joint = jnp.sum(jnp.sum(both[lo:hi], axis=0, keepdims=True), axis=1, keepdims=True)
        at_end = at_end + carry[:, BLK - 1 :] * joint
        ga = jnp.sum(dy_h * y_h - u_low * du, axis=0, keepdims=True)
        red_ref[0, pl.ds(head, 1), :] = ga + jnp.where(last_lane, at_end, 0.0)
        red_ref[1, pl.ds(head, 1), :] = jnp.sum(x_h * du, axis=0, keepdims=True)
        red_ref[2, pl.ds(head, 1), :] = jnp.sum(x_h * dy_h, axis=0, keepdims=True)
        y_parts.append((y_h + skip * x_h).astype(BF16))
        g_parts.append(dt * du + skip * dy_h)
        cdy_parts.append((carry * dy_h).astype(BF16))
        eu_parts.append((end * u).astype(BF16))
    out_ref[...] = mm_nt(ident, jnp.concatenate(y_parts, axis=0)).astype(BF16)
    small = eye(NS, BF16)
    acc_ref[:NS, :] += mm(mm_nt(small, state_back).astype(BF16), jnp.concatenate(eu_parts, axis=0))
    acc_ref[NS:, :] += mm(mm_nt(small, state_in).astype(BF16), jnp.concatenate(cdy_parts, axis=0))
    g = jnp.concatenate(g_parts, axis=0) * slope_ref[...]
    raw = mm_nt(ident, x_ref[...])
    rim = mm_nt(ident, wide_rim(rim_ref[...]))
    taps = mm_nt(eye(BLK, F32), wx_ref[...], HIGH)
    grad, spill, weights = conv_back(g, raw, rim, taps, masks)
    gx_ref[...] = mm_nt(ident, grad.astype(BF16)).astype(BF16)
    tail = (iota((RIM, BLK), 0) + (BLK - RIM) == iota((RIM, BLK), 1)).astype(F32)
    last_ref[...] = mm_nt(tail, grad, HIGH)
    rim_pick = (iota((RIM, 128), 0) + (128 - RIM) == iota((RIM, 128), 1)).astype(F32)
    spill_ref[...] = mm_nt(rim_pick, spill, HIGH)
    gw_ref[...] = weights

    @pl.when(step == pl.num_programs(0) - 1)
    def _():
        per_head = mm_nt(eye(heads, F32), hv_ref[...], HIGH)
        rate = jnp.exp(per_head[:, 0:1])
        later = (iota((BLK, BLK), 0) >= iota((BLK, BLK), 1)).astype(F32)
        grad_log = mm(red_ref[0], later, HIGH)
        grad_step = (red_ref[1] - rate * grad_log) * rows_ref[4]
        gdt_ref[...] = mm_nt(eye(BLK, F32), grad_step, HIGH)
        which = iota((8, BLK), 0)
        gh = mm_nt((which == 0).astype(F32), -rate * rows_ref[0] * grad_log, HIGH)
        gh = gh + mm_nt((which == 1).astype(F32), grad_step, HIGH)
        gh_ref[...] = gh + mm_nt((which == 2).astype(F32), red_ref[2], HIGH)
        g_bc = acc_ref[...] * bcslope_ref[...]
        raw_bc = mm_nt(ident, bc_ref[...])
        rim_bc = mm_nt(ident, wide_rim(rimbc_ref[...]))
        taps_bc = mm_nt(eye(BLK, F32), wbc_ref[...], HIGH)
        grad_bc, spill_bc, weights_bc = conv_back(g_bc, raw_bc, rim_bc, taps_bc, masks)
        token = mm_nt(eye(BLK, F32), grad_bc, HIGH)
        shares = pay_ref.shape[0]
        share = BLK // shares
        last8 = (iota((8, 128), 0) + 120 == iota((8, 128), 1)).astype(F32)
        spill8 = mm_nt(last8, spill_bc, HIGH)
        for j in range(shares):
            pay_ref[j, 0:share, :] = token[j * share : (j + 1) * share]
            pay_ref[j, share : share + 8, :] = weights_bc
            pay_ref[j, share + 8 : share + 16, :] = spill8


def patch_kernel(gx_ref, last_ref, spill_ref, out_ref):
    del gx_ref
    out_ref[...] = (last_ref[...] + spill_ref[...]).astype(BF16)


def whole(shape):
    zeros = (0,) * len(shape)
    return pl.BlockSpec(shape, lambda *_: zeros)


def columns(rows):
    return pl.BlockSpec((rows, BLK), lambda i: (0, i))


def channel_rows(width):
    return pl.BlockSpec((BLK, width), lambda i: (i, 0))


def shaped(shape, dtype):
    return jax.ShapeDtypeStruct(shape, dtype)


def passed_along(value, by):
    peers = lax.axis_size("ctx")
    pairs = [(i, i + by) for i in range(peers) if 0 <= i + by < peers]
    return lax.ppermute(value, "ctx", pairs)


def summed_over_ctx(value):
    peers = lax.axis_size("ctx")
    value = value + lax.ppermute(value, "ctx", [(i, i ^ 1) for i in range(peers)])
    for stride in (2, 8):
        def turned(i, by):
            at = i // stride % 4
            return i + ((at + by) % 4 - at) * stride

        got = [
            lax.ppermute(value, "ctx", [(i, turned(i, by)) for i in range(peers)])
            for by in (1, 2, 3)
        ]
        value = (value + got[0]) + (got[1] + got[2])
    return value


def local(x_raw, bc_raw, dt_raw, conv_x, conv_bc, a_log, dt_bias, skip_weight, segment, grad_y):
    rows, channels = x_raw.shape
    heads = dt_raw.shape[1]
    steps = channels // BLK
    peers = lax.axis_size("ctx")
    shares = lax.axis_size("head")
    share = rows // shares
    rim = passed_along(jnp.concatenate([x_raw[rows - RIM :], bc_raw[rows - RIM :]], axis=1), 1)
    rim_x = rim[:, :channels]
    rim_bc = rim[:, channels:]
    padded = jnp.concatenate([jnp.full((3,), -1, jnp.int32), segment])
    seg_ext = lax.dynamic_slice_in_dim(padded, lax.axis_index("ctx") * rows, rows + 3)
    seg = jnp.stack([seg_ext[min(k, 3) : min(k, 3) + rows] for k in range(8)]).astype(F32)
    hv = jnp.stack([a_log, dt_bias, skip_weight, skip_weight])

    pay, xa, slope, y_loc, du_loc, head_rows, dbc, bcslope, bctok = pl.pallas_call(
        local_kernel,
        grid=(steps,),
        in_specs=[
            columns(rows), columns(RIM), columns(rows), columns(4),
            whole((rows, 256)), whole((RIM, 256)), whole((4, 256)),
            whole((rows, heads)), whole((4, heads)), whole((8, rows)),
        ],
        out_specs=[
            pl.BlockSpec((8, 80, NS), lambda i: (i, 0, 0)),
            channel_rows(rows), channel_rows(rows), channel_rows(rows), channel_rows(rows),
            whole((5, heads, rows)), whole((256, rows)), whole((256, rows)), whole((rows, 256)),
        ],
        out_shape=[
            shaped((peers, 80, NS), BF16),
            shaped((channels, rows), BF16), shaped((channels, rows), F32),
            shaped((channels, rows), F32), shaped((channels, rows), F32),
            shaped((5, heads, rows), F32), shaped((256, rows), F32),
            shaped((256, rows), F32), shaped((rows, 256), BF16),
        ],
        scratch_shapes=[
            pltpu.VMEM((rows, rows), F32), pltpu.VMEM((rows, rows), F32),
            pltpu.VMEM((256, rows), BF16), pltpu.VMEM((rows, heads), F32),
            pltpu.VMEM((rows, rows), F32),
        ],
        compiler_params=pltpu.CompilerParams(vmem_limit_bytes=VMEM),
        name="local_part",
    )(x_raw, rim_x, grad_y, conv_x, bc_raw, rim_bc, conv_bc, dt_raw, hv, seg)

    got = lax.all_to_all(pay, "ctx", 0, 0, tiled=True)
    carried = pl.pallas_call(
        lambda *refs: scan_kernel(peers, *refs),
        in_specs=[pl.BlockSpec(memory_space=pltpu.VMEM)],
        out_specs=pl.BlockSpec(memory_space=pltpu.VMEM),
        out_shape=shaped((peers, 64, NS), BF16),
        name="state_scan",
    )(got)
    states = lax.all_to_all(carried, "ctx", 0, 0, tiled=True)

    ssd_out, gx, last, spill, gw, grad_dt, gh, pay_bc = pl.pallas_call(
        final_kernel,
        grid=(steps,),
        in_specs=[
            columns(rows), columns(RIM), columns(rows), columns(4),
            whole((rows, 256)), whole((RIM, 256)), whole((4, 256)),
            whole((4, heads)), whole((8, rows)),
            pl.BlockSpec((8, 64, NS), lambda i: (i, 0, 0)),
            channel_rows(rows), channel_rows(rows), channel_rows(rows), channel_rows(rows),
            whole((5, heads, rows)), whole((256, rows)), whole((256, rows)), whole((rows, 256)),
        ],
        out_specs=[
            columns(rows), columns(rows), columns(RIM), columns(RIM), columns(8),
            whole((rows, heads)), whole((8, heads)), whole((shares, share + 16, 256)),
        ],
        out_shape=[
            shaped((rows, channels), BF16), shaped((rows, channels), BF16),
            shaped((RIM, channels), F32), shaped((RIM, channels), F32), shaped((8, channels), F32),
            shaped((rows, heads), F32), shaped((8, heads), F32),
            shaped((shares, share + 16, 256), F32),
        ],
        scratch_shapes=[
            pltpu.VMEM((3, heads, rows), F32), pltpu.VMEM((256, rows), F32),
        ],
        compiler_params=pltpu.CompilerParams(vmem_limit_bytes=VMEM),
        name="final_part",
    )(
        x_raw, rim_x, grad_y, conv_x, bc_raw, rim_bc, conv_bc, hv, seg,
        states, xa, slope, y_loc, du_loc, head_rows, dbc, bcslope, bctok,
    )

    spill_x = passed_along(spill, -1)
    grad_x = pl.pallas_call(
        patch_kernel,
        grid=(1,),
        in_specs=[
            pl.BlockSpec(memory_space=pl.ANY), whole((RIM, channels)), whole((RIM, channels)),
        ],
        out_specs=pl.BlockSpec((RIM, channels), lambda i: (rows // RIM - 1, 0)),
        out_shape=shaped((rows, channels), BF16),
        input_output_aliases={0: 0},
        name="last_rows",
    )(gx, last, spill_x)

    got_bc = jnp.sum(lax.all_to_all(pay_bc, "head", 0, 0, tiled=True), axis=0)
    spill_bc = passed_along(got_bc[share + 8 :], -1)
    sums = summed_over_ctx(
        jnp.concatenate([gw, got_bc[share : share + 8], jnp.pad(gh, ((0, 0), (0, 112)))], axis=1)
    )
    is_last = lax.axis_index("head") == shares - 1
    grad_bc = got_bc[:share] + jnp.pad(
        jnp.where(is_last, spill_bc, 0.0), ((share - 8, 0), (0, 0))
    )
    return (
        ssd_out, grad_x, grad_bc, grad_dt,
        sums[:4, :channels], sums[:4, channels : channels + 256],
        sums[:3, channels + 256 : channels + 256 + heads],
    )


def solution(mesh):
    in_specs = (
        P("ctx", "head"), P("ctx", None), P("ctx", "head"), P(None, "head"), P(),
        P("head"), P("head"), P("head"), P(), P("ctx", "head"),
    )
    out_specs = (
        P("ctx", "head"), P("ctx", "head"), P(("ctx", "head"), None), P("ctx", "head"),
        P(None, "head"), P(), P(None, "head"),
    )
    return jax.shard_map(local, mesh=mesh, in_specs=in_specs, out_specs=out_specs, check_vma=False)
```

time: 1230 us -> 130 us (0.11)
  the two profiles are of different devices: /device:TPU:1 before, /device:TPU:2 now
where the time goes in v1:
time: 130 us; the launch traced here: 129 us
  blocking collectives  35.2 us (27%)
  Pallas kernels  31.8 us (24%)
  starting transfers between devices  23.8 us (18%)
  waiting for transfers between devices  22.1 us (17%)
  local copies, waits for them, and re-layouts  14.4 us (11%)
    all_to_all x1, blocking collectives, local(): got = lax.all_to_all(pay, 'ctx', 0, 0, tiled=True)  19.4 us
    pallas_call x1, Pallas kernels, local(): pl.pallas_call(final_kernel, grid=(steps,), in_specs=[columns(rows), colu...  18.2 us
    all_to_all x1, blocking collectives, local(): states = lax.all_to_all(carried, 'ctx', 0, 0, tiled=True)  15.8 us
    all_to_all x1, waiting for transfers between devices, local(): got_bc = jnp.sum(lax.all_to_all(pay_bc, 'head', 0, 0, tiled=True), axis=0)  12.4 us
    unnamed x62, local copies, waits for them, and re-layouts  11.6 us
    pallas_call x1, Pallas kernels, local(): pl.pallas_call(local_kernel, grid=(steps,), in_specs=[columns(rows), colu...  10 us
    all_to_all x1, starting transfers between devices, local(): got_bc = jnp.sum(lax.all_to_all(pay_bc, 'head', 0, 0, tiled=True), axis=0)  8.61 us
    ppermute x6, waiting for transfers between devices, summed_over_ctx(): lax.ppermute(value, 'ctx', [(i, turned(i, by)) for i in range(peers)])  8 us
  transfers between devices with their start and end apart: 11, of which 7 were waited for; matrix products, arithmetic and copies ran while one was open for 1% of the time, Pallas kernels for 1%

profile of v1, /device:TPU:2, one launch (start us, length us, event | category | flops | bytes accessed | tf_op | source)
XLA Modules:
  0.0 128.9 jit_solution(17227876050665900787)
XLA Ops:
  0.7 0.7 slice-done
  1.4 1.9 %collective-permute-start = (bf16[16,1280]{1,0:T(8,128)(2,1)S(1)}, bf16[16,1280]{1,0:T(8,128)(2,1)S(1)}, u32[]{:S(2)}, u32[]{:S(2)}) collective-permute-start(bf16[16,1280]{1,0:T(8,128)(2,1)S(1)} %pad_maximum_fusion), channel_id=1, source_target_pairs={{0,8},{8,16},{16,24},{24,32},{32,40},{40,48},{48,56},{56,64},{64,7... | collective-permute-start | bytes 122888 | tf_op jit(solution)/shard_map/ppermute | solution.py:340
  3.5 0.7 copy-done.27
  4.3 0.7 copy-done.26
  5.0 1.7 %collective-permute-done = bf16[16,1280]{1,0:T(8,128)(2,1)S(1)} collective-permute-done((bf16[16,1280]{1,0:T(8,128)(2,1)S(1)}, bf16[16,1280]{1,0:T(8,128)(2,1)S(1)}, u32[]{:S(2)}, u32[]{:S(2)}) %collective-permute-start) | collective-permute-done | bytes 40992 | tf_op jit(solution)/shard_map/ppermute | solution.py:340
  7.5 1.0 copy-done
  8.5 1.0 copy-done.2
  9.5 10.0 %local_part.1 = (bf16[32,80,128]{2,1,0:T(8,128)(2,1)S(1)}, bf16[1024,256]{1,0:T(8,128)(2,1)S(1)}, f32[1024,256]{1,0:T(8,128)S(1)}, f32[1024,256]{1,0:T(8,128)S(1...) custom-call(bf16[256,1024]{1,0:T(8,128)(2,1)S(1)} %copy-done, ...), custom_call_target="tpu_custom_call" | custom-call | tf_op jit(solution)/shard_map/local_part/pallas_call | solution.py:374
  19.6 0.7 copy-done.5
  20.2 19.4 %all_to_all.15.refs_0_ = bf16[32,80,128]{2,1,0:T(8,128)(2,1)} all-to-all(bf16[32,80,128]{2,1,0:T(8,128)(2,1)S(1)} %get-tuple-element.24), channel_id=1, replica_groups=mesh['ctx'=32,'head'=8] {'ctx'}, dimensions={0} | all-to-all | bytes 1310720 | tf_op jit(solution)/shard_map/all_to_all | solution.py:403
  39.7 2.1 %state_scan.1 = bf16[32,64,128]{2,1,0:T(8,128)(2,1)} custom-call(bf16[32,80,128]{2,1,0:T(8,128)(2,1)} %all_to_all.15.refs_0_), custom_call_target="tpu_custom_call" | custom-call | tf_op jit(solution)/shard_map/state_scan/pallas_call | solution.py:404
  41.7 15.8 %all_to_all.16.state_ref = bf16[32,64,128]{2,1,0:T(8,128)(2,1)S(1)} all-to-all(bf16[32,64,128]{2,1,0:T(8,128)(2,1)} %state_scan.1), channel_id=1, replica_groups=mesh['ctx'=32,'head'=8] {'ctx'}, dimensions={0} | all-to-all | bytes 1048576 | tf_op jit(solution)/shard_map/all_to_all | solution.py:411
  57.6 0.7 copy-done.10
  58.3 0.7 copy-done.12
  59.0 0.7 copy-done.14
  59.7 18.2 %final_part.1 = (bf16[256,1024]{1,0:T(8,128)(2,1)}, bf16[256,1024]{1,0:T(8,128)(2,1)}, f32[16,1024]{1,0:T(8,128)S(1)}, f32[16,1024]{1,0:T(8,128)S(1)}, f32[8,102...) custom-call(bf16[256,1024]{1,0:T(8,128)(2,1)S(1)} %copy-done.1, ...), custom_call_target="tpu_custom_call" | custom-call | tf_op jit(solution)/shard_map/final_part/pallas_call | solution.py:413
  77.9 0.6 copy-done.7
  80.4 8.6 %all-to-all-start.2 = ((f32[8,48,256]{2,1,0:T(8,128)}), f32[8,48,256]{2,1,0:T(8,128)S(1)}, u32[]{:S(2)}, u32[]{:S(2)}) async-start(f32[8,48,256]{2,1,0:T(8,128)} %get-tuple-element.37), calls=%async_computation.2 | async-start | bytes 786432 | tf_op jit(solution)/shard_map/all_to_all | solution.py:457
  89.0 2.8 %collective-permute-start.1 = (f32[16,1024]{1,0:T(8,128)S(1)}, f32[16,1024]{1,0:T(8,128)S(1)}, u32[]{:S(2)}, u32[]{:S(2)}) collective-permute-start(f32[16,1024]{1,0:T(8,128)S(1)} %copy-done.23), channel_id=1, source_target_pairs={{8,0},{16,8},{24,16},{32,24},{40,32},{48,40},{56,48},{64,56},{72,6... | collective-permute-start | bytes 196616 | tf_op jit(solution)/shard_map/ppermute | solution.py:340
  91.8 12.4 %all-to-all-done.2 = f32[8,48,256]{2,1,0:T(8,128)S(1)} async-done(((f32[8,48,256]{2,1,0:T(8,128)}), f32[8,48,256]{2,1,0:T(8,128)S(1)}, u32[]{:S(2)}, u32[]{:S(2)}) %all-to-all-start.2) | async-done | bytes 393248 | tf_op jit(solution)/shard_map/all_to_all | solution.py:457
  105.1 0.7 copy.19
  106.4 1.5 %last_rows.1 = bf16[256,1024]{1,0:T(8,128)(2,1)} custom-call(bf16[256,1024]{1,0:T(8,128)(2,1)} %get-tuple-element.34.gx_ref, f32[16,1024]{1,0:T(8,128)} %copy-done.15, f32[16,1024]{1,0:T(8,128)} %copy-done.24), custom_call_target="tpu_custom_call", output_to_operand_aliasing={{}: (0, {})} | custom-call | tf_op jit(solution)/shard_map/last_rows/pallas_call | solution.py:445
  107.9 3.0 %collective-permute-start.2 = (f32[8,256]{1,0:T(8,128)S(1)}, f32[8,256]{1,0:T(8,128)S(1)}, u32[]{:S(2)}, u32[]{:S(2)}) collective-permute-start(f32[8,256]{1,0:T(8,128)S(1)} %get-tuple-element.49), channel_id=1, source_target_pairs={{8,0},{16,8},{24,16},{32,24},{40,32},{48,40},{56,48},{64,56},{72,6... | collective-permute-start | bytes 24584 | tf_op jit(solution)/shard_map/ppermute | solution.py:340
  111.0 2.3 %collective-permute-start.5 = (f32[8,1408]{1,0:T(8,128)S(1)}, f32[8,1408]{1,0:T(8,128)S(1)}, u32[]{:S(2)}, u32[]{:S(2)}) collective-permute-start(f32[8,1408]{1,0:T(8,128)S(1)} %fusion), channel_id=1, source_target_pairs={{0,32},{8,40},{16,48},{24,56},{32,0},{40,8},{48,16},{56,24},{64,96... | collective-permute-start | bytes 135176 | tf_op jit(solution)/shard_map/ppermute | solution.py:352
  113.3 0.9 collective-permute-start.4
  114.2 0.8 collective-permute-done.6
  115.1 1.6 %collective-permute-done.5 = f32[8,1408]{1,0:T(8,128)S(1)} collective-permute-done((f32[8,1408]{1,0:T(8,128)S(1)}, f32[8,1408]{1,0:T(8,128)S(1)}, u32[]{:S(2)}, u32[]{:S(2)}) %collective-permute-start.5) | collective-permute-done | bytes 45088 | tf_op jit(solution)/shard_map/ppermute | solution.py:352
  116.7 0.9 collective-permute-done.4
  117.6 1.1 collective-permute-start.9
  118.7 3.1 %collective-permute-start.8 = (f32[8,1408]{1,0:T(8,128)S(1)}, f32[8,1408]{1,0:T(8,128)S(1)}, u32[]{:S(2)}, u32[]{:S(2)}) collective-permute-start(f32[8,1408]{1,0:T(8,128)S(1)} %add_add_fusion.1), channel_id=1, source_target_pairs={{0,128},{8,136},{16,144},{24,152},{32,160},{40,168},{48,176},{56,1... | collective-permute-start | bytes 135176 | tf_op jit(solution)/shard_map/ppermute | solution.py:352
  122.4 1.9 %collective-permute-done.8 = f32[8,1408]{1,0:T(8,128)S(1)} collective-permute-done((f32[8,1408]{1,0:T(8,128)S(1)}, f32[8,1408]{1,0:T(8,128)S(1)}, u32[]{:S(2)}, u32[]{:S(2)}) %collective-permute-start.8) | collective-permute-done | bytes 45088 | tf_op jit(solution)/shard_map/ppermute | solution.py:352
  124.3 2.8 %collective-permute-done.7 = f32[8,1408]{1,0:T(8,128)S(1)} collective-permute-done((f32[8,1408]{1,0:T(8,128)S(1)}, f32[8,1408]{1,0:T(8,128)S(1)}, u32[]{:S(2)}, u32[]{:S(2)}) %collective-permute-start.7) | collective-permute-done | bytes 45088 | tf_op jit(solution)/shard_map/ppermute | solution.py:352
  (81 shorter events, 7.0 us)
Async XLA Ops:
  0.6 0.8 slice-start
  0.6 0.8 slice-start.1
  1.4 1.9 %copy-start.25 = (s32[8192]{0:T(1024)S(1)}, s32[8192]{0:T(1024)}, u32[]{:S(2)}) copy-start(s32[8192]{0:T(1024)} %param.18) | copy-start | bytes 98308
  1.4 5.3 %collective-permute-start = (bf16[16,1280]{1,0:T(8,128)(2,1)S(1)}, bf16[16,1280]{1,0:T(8,128)(2,1)S(1)}, u32[]{:S(2)}, u32[]{:S(2)}) collective-permute-start(bf16[16,1280]{1,0:T(8,128)(2,1)S(1)} %pad_maximum_fusion), channel_id=1, source_target_pairs={{0,8},{8,16},{16,24},{24,32},{32,40},{40,48},{48,56},{56,64},{64,7... | collective-permute-start | bytes 122888 | tf_op jit(solution)/shard_map/ppermute | solution.py:340
  4.2 2.5 %copy-start.16 = (f32[4,16]{1,0:T(4,128)}, f32[4,16]{1,0:T(4,128)S(1)}, u32[]{:S(2)}) copy-start(f32[4,16]{1,0:T(4,128)S(1)} %pad_maximum_fusion.1.hv_ref) | copy-start | bytes 772
  4.2 0.7 copy-start.26
  4.2 3.1 %copy-start.4 = (bf16[256,256]{1,0:T(8,128)(2,1)S(1)}, bf16[256,256]{1,0:T(8,128)(2,1)}, u32[]{:S(2)}) copy-start(bf16[256,256]{1,0:T(8,128)(2,1)} %bc_ref.3) | copy-start | bytes 393220
  4.9 1.8 %copy-start.9 = (f32[8,256]{1,0:T(8,128)}, f32[8,256]{1,0:T(8,128)S(1)}, u32[]{:S(2)}) copy-start(f32[8,256]{1,0:T(8,128)S(1)} %convert_element_type.7.seg_ref) | copy-start | bytes 24580
  6.7 0.7 copy-start.13
  6.7 0.7 copy-start.18
  7.5 1.0 copy-start
  8.5 1.0 copy-start.2
  39.7 17.9 %copy-start.6 = (bf16[256,256]{1,0:T(8,128)(2,1)S(1)}, bf16[256,256]{1,0:T(8,128)(2,1)}, u32[]{:S(2)}) copy-start(bf16[256,256]{1,0:T(8,128)(2,1)} %copy-done.5) | copy-start | bytes 393220
  41.7 15.8 %copy-start.1 = (bf16[256,1024]{1,0:T(8,128)(2,1)S(1)}, bf16[256,1024]{1,0:T(8,128)(2,1)}, u32[]{:S(2)}) copy-start(bf16[256,1024]{1,0:T(8,128)(2,1)} %x_ref.3) | copy-start | bytes 1572868
  41.7 15.8 %copy-start.3 = (bf16[256,1024]{1,0:T(8,128)(2,1)S(1)}, bf16[256,1024]{1,0:T(8,128)(2,1)}, u32[]{:S(2)}) copy-start(bf16[256,1024]{1,0:T(8,128)(2,1)} %gy_ref.3) | copy-start | bytes 1572868
  57.6 0.7 copy-start.10
  57.6 0.7 copy-start.19
  57.6 0.7 copy-start.17
  58.3 0.7 copy-start.12
  59.0 0.7 copy-start.14
  80.4 8.6 %copy-start.23 = (f32[16,1024]{1,0:T(8,128)S(1)}, f32[16,1024]{1,0:T(8,128)}, u32[]{:S(2)}) copy-start(f32[16,1024]{1,0:T(8,128)} %copy-done.22) | copy-start | bytes 196612
  80.4 23.8 %all-to-all-start.2 = ((f32[8,48,256]{2,1,0:T(8,128)}), f32[8,48,256]{2,1,0:T(8,128)S(1)}, u32[]{:S(2)}, u32[]{:S(2)}) async-start(f32[8,48,256]{2,1,0:T(8,128)} %get-tuple-element.37), calls=%async_computation.2 | async-start | bytes 786432 | tf_op jit(solution)/shard_map/all_to_all | solution.py:457
  89.0 16.8 %collective-permute-start.1 = (f32[16,1024]{1,0:T(8,128)S(1)}, f32[16,1024]{1,0:T(8,128)S(1)}, u32[]{:S(2)}, u32[]{:S(2)}) collective-permute-start(f32[16,1024]{1,0:T(8,128)S(1)} %copy-done.23), channel_id=1, source_target_pairs={{8,0},{16,8},{24,16},{32,24},{40,32},{48,40},{56,48},{64,56},{72,6... | collective-permute-start | bytes 196616 | tf_op jit(solution)/shard_map/ppermute | solution.py:340
  104.2 0.9 copy-start.8
  104.9 6.0 %collective-permute-start.3 = (f32[8,1408]{1,0:T(8,128)S(1)}, f32[8,1408]{1,0:T(8,128)S(1)}, u32[]{:S(2)}, u32[]{:S(2)}) collective-permute-start(f32[8,1408]{1,0:T(8,128)S(1)} %select_maximum_fusion), channel_id=1, source_target_pairs={{0,8},{8,0},{16,24},{24,16},{32,40},{40,32},{48,56},{56,48},{64,72... | collective-permute-start | bytes 135176 | tf_op jit(solution)/shard_map/ppermute | solution.py:345
  107.9 6.3 %collective-permute-start.2 = (f32[8,256]{1,0:T(8,128)S(1)}, f32[8,256]{1,0:T(8,128)S(1)}, u32[]{:S(2)}, u32[]{:S(2)}) collective-permute-start(f32[8,256]{1,0:T(8,128)S(1)} %get-tuple-element.49), channel_id=1, source_target_pairs={{8,0},{16,8},{24,16},{32,24},{40,32},{48,40},{56,48},{64,56},{72,6... | collective-permute-start | bytes 24584 | tf_op jit(solution)/shard_map/ppermute | solution.py:340
  110.9 4.1 %collective-permute-start.6 = (f32[8,1408]{1,0:T(8,128)S(1)}, f32[8,1408]{1,0:T(8,128)S(1)}, u32[]{:S(2)}, u32[]{:S(2)}) collective-permute-start(f32[8,1408]{1,0:T(8,128)S(1)} %fusion), channel_id=1, source_target_pairs={{0,48},{8,56},{16,0},{24,8},{32,16},{40,24},{48,32},{56,40},{64,11... | collective-permute-start | bytes 135176 | tf_op jit(solution)/shard_map/ppermute | solution.py:352
  111.0 5.6 %collective-permute-start.5 = (f32[8,1408]{1,0:T(8,128)S(1)}, f32[8,1408]{1,0:T(8,128)S(1)}, u32[]{:S(2)}, u32[]{:S(2)}) collective-permute-start(f32[8,1408]{1,0:T(8,128)S(1)} %fusion), channel_id=1, source_target_pairs={{0,32},{8,40},{16,48},{24,56},{32,0},{40,8},{48,16},{56,24},{64,96... | collective-permute-start | bytes 135176 | tf_op jit(solution)/shard_map/ppermute | solution.py:352
  113.3 4.3 %collective-permute-start.4 = (f32[8,1408]{1,0:T(8,128)S(1)}, f32[8,1408]{1,0:T(8,128)S(1)}, u32[]{:S(2)}, u32[]{:S(2)}) collective-permute-start(f32[8,1408]{1,0:T(8,128)S(1)} %fusion), channel_id=1, source_target_pairs={{0,16},{8,24},{16,32},{24,40},{32,48},{40,56},{48,0},{56,8},{64,80... | collective-permute-start | bytes 135176 | tf_op jit(solution)/shard_map/ppermute | solution.py:352
  117.6 4.8 %collective-permute-start.9 = (f32[8,1408]{1,0:T(8,128)S(1)}, f32[8,1408]{1,0:T(8,128)S(1)}, u32[]{:S(2)}, u32[]{:S(2)}) collective-permute-start(f32[8,1408]{1,0:T(8,128)S(1)} %add_add_fusion.1), channel_id=1, source_target_pairs={{0,192},{8,200},{16,208},{24,216},{32,224},{40,232},{48,240},{56,2... | collective-permute-start | bytes 135176 | tf_op jit(solution)/shard_map/ppermute | solution.py:352
  118.7 5.6 %collective-permute-start.8 = (f32[8,1408]{1,0:T(8,128)S(1)}, f32[8,1408]{1,0:T(8,128)S(1)}, u32[]{:S(2)}, u32[]{:S(2)}) collective-permute-start(f32[8,1408]{1,0:T(8,128)S(1)} %add_add_fusion.1), channel_id=1, source_target_pairs={{0,128},{8,136},{16,144},{24,152},{32,160},{40,168},{48,176},{56,1... | collective-permute-start | bytes 135176 | tf_op jit(solution)/shard_map/ppermute | solution.py:352
  121.8 5.3 %collective-permute-start.7 = (f32[8,1408]{1,0:T(8,128)S(1)}, f32[8,1408]{1,0:T(8,128)S(1)}, u32[]{:S(2)}, u32[]{:S(2)}) collective-permute-start(f32[8,1408]{1,0:T(8,128)S(1)} %add_add_fusion.1), channel_id=1, source_target_pairs={{0,64},{8,72},{16,80},{24,88},{32,96},{40,104},{48,112},{56,120},{... | collective-permute-start | bytes 135176 | tf_op jit(solution)/shard_map/ppermute | solution.py:352
  (11 other events, 7.1 us)

commit v2 on v1

v2 whole, which is shorter than its diff:
```python
import jax
import jax.numpy as jnp
from jax import lax
from jax.experimental import pallas as pl
from jax.experimental.pallas import tpu as pltpu
from jax.sharding import PartitionSpec as P

F32 = jnp.float32
BF16 = jnp.bfloat16

BLK = 256
HD = 64
NS = 128
RIM = 16
PER = BLK // HD
VMEM = 24 * 1024 * 1024

DT, CUMUL, CARRY, END, SIG, SKIP, RATE, MASK = range(8)


def mm(a, b):
    return lax.dot_general(a, b, (((1,), (0,)), ((), ())), preferred_element_type=F32)


def mm_nt(a, b):
    return lax.dot_general(a, b, (((1,), (1,)), ((), ())), preferred_element_type=F32)


def split(value, count):
    parts = []
    for _ in range(count):
        part = value.astype(BF16)
        parts.append(part)
        value = value - part.astype(F32)
    return parts


def pick_nt(pick, value, count):
    return sum(mm_nt(pick, part) for part in split(value, count))


def pick_right(value, pick, count):
    return sum(mm(part, pick) for part in split(value, count))


def iota(shape, dim):
    return lax.broadcasted_iota(jnp.int32, shape, dim)


def eye(n, dtype):
    return (iota((n, n), 0) == iota((n, n), 1)).astype(dtype)


def silu_and_slope(pre):
    sig = 1.0 / (1.0 + jnp.exp(-pre))
    return pre * sig, sig * (1.0 + pre * (1.0 - sig))


def conv_own(raw, taps, masks):
    lane = iota((raw.shape[0], 128), 1)
    total = taps[:, 3:4] * raw
    for j in range(1, 4):
        rolled = pltpu.roll(raw, j, 1)
        shifted = jnp.concatenate(
            [jnp.where(lane < j, 0.0, rolled[:, :128]), rolled[:, 128:]], axis=1
        )
        total = total + shifted * (taps[:, 3 - j : 4 - j] * masks[3 - j])
    return total


def conv_rim(rim, taps, masks):
    lane = iota(rim.shape, 1)
    total = jnp.zeros(rim.shape, F32)
    for j in range(1, 4):
        before = jnp.where(lane < j, pltpu.roll(rim, j, 1), 0.0)
        total = total + before * (taps[:, 3 - j : 4 - j] * masks[3 - j][:, :128])
    return total


def conv_back(g, raw, rim, taps, masks):
    lane = iota((g.shape[0], 128), 1)
    grad = taps[:, 3:4] * g
    spill = jnp.zeros((g.shape[0], 128), F32)
    row = iota((8, 128), 0)

    def weight_row(k, product):
        return pick_nt((row == k).astype(BF16), product, 2)

    product = g * raw
    weights = weight_row(3, product[:, :128] + product[:, 128:])
    for j in range(1, 4):
        masked = g * masks[3 - j]
        rolled = pltpu.roll(masked, g.shape[1] - j, 1)
        wrapped = lane >= 128 - j
        first = rolled[:, :128]
        second = jnp.where(wrapped, 0.0, rolled[:, 128:])
        outer = jnp.where(wrapped, rolled[:, 128:], 0.0)
        tap = taps[:, 3 - j : 4 - j]
        grad = grad + tap * jnp.concatenate([first, second], axis=1)
        spill = spill + tap * outer
        weights = weights + weight_row(
            3 - j, first * raw[:, :128] + second * raw[:, 128:] + outer * rim
        )
    return grad, spill, weights


def wide_rim(rim):
    return jnp.concatenate([jnp.zeros((128 - RIM, rim.shape[1]), BF16), rim], axis=0)


def masks_of(rows_ref):
    return [rows_ref[MASK, k : k + 1, :] for k in range(4)]


def head_row(rows_ref, plane, head):
    return rows_ref[plane, pl.ds(head, 1), :]


def prep_kernel(
    x_ref, gy_ref, wx_ref, bc_ref, wbc_ref, dt_ref, hv_ref, seg_ref,
    xt_ref, dyt_ref, pre_ref, taps_ref, rows_ref, bct_ref, bcpre_ref, bctaps_ref,
):
    ident = eye(BLK, BF16)

    def taps_of(ref):
        taps = pick_nt(ident, ref[...], 3)
        return jnp.concatenate([taps, jnp.zeros((BLK, 124), F32)], axis=1)

    @pl.when(pl.program_id(0) == 0)
    def _():
        target = seg_ref[3:4, :]
        rows_ref[MASK] = jnp.concatenate(
            [(seg_ref[k : k + 1, :] == target).astype(F32) for k in range(4)]
            + [target, jnp.zeros((11, BLK), F32)],
            axis=0,
        )
        heads = dt_ref.shape[0]
        per_head = pick_nt(eye(heads, BF16), hv_ref[...], 3)
        rate = jnp.exp(per_head[:, 0:1])
        pre = dt_ref[...] + per_head[:, 1:2]
        dt = jnp.maximum(pre, 0.0) + jnp.log1p(jnp.exp(-jnp.abs(pre)))
        upto = (iota((BLK, BLK), 0) <= iota((BLK, BLK), 1)).astype(BF16)
        cumul = pick_right(-rate * dt, upto, 3)
        keep = (target == seg_ref[2:3, 0:1]).astype(F32)
        same_end = target == target[:, BLK - 1 :]
        rows_ref[DT] = dt
        rows_ref[CUMUL] = cumul
        rows_ref[CARRY] = keep * jnp.exp(cumul)
        rows_ref[END] = jnp.exp(jnp.where(same_end, cumul[:, BLK - 1 :] - cumul, -jnp.inf))
        rows_ref[SIG] = 1.0 / (1.0 + jnp.exp(-pre))
        rows_ref[SKIP] = jnp.broadcast_to(per_head[:, 2:3], (heads, BLK))
        rows_ref[RATE] = jnp.broadcast_to(rate, (heads, BLK))
        bct = mm_nt(ident, bc_ref[...])
        bct_ref[...] = bct.astype(BF16)
        bctaps = taps_of(wbc_ref)
        bctaps_ref[...] = bctaps
        bcpre_ref[...] = conv_own(bct, bctaps, masks_of(rows_ref))

    raw = mm_nt(ident, x_ref[...])
    xt_ref[...] = raw.astype(BF16)
    dyt_ref[...] = mm_nt(ident, gy_ref[...]).astype(BF16)
    taps = taps_of(wx_ref)
    taps_ref[...] = taps
    pre_ref[...] = conv_own(raw, taps, masks_of(rows_ref))


def state_kernel(
    pre_ref, rim_ref, taps_ref, dyt_ref, rows_ref, bcpre_ref, rimbc_ref, bctaps_ref,
    pay_ref, xa_ref, slope_ref, eu_ref, cdy_ref, rimt_ref,
    bctok_ref, bcact_ref, bcslope_ref, bcrimt_ref,
):
    step = pl.program_id(0)
    ident = eye(BLK, BF16)
    masks = masks_of(rows_ref)

    def activate(pre, rim_rows, taps):
        rim = mm_nt(ident, wide_rim(rim_rows))
        pre = jnp.concatenate([pre[:, :128] + conv_rim(rim, taps, masks), pre[:, 128:]], axis=1)
        act, slope = silu_and_slope(pre)
        return act.astype(BF16), slope, rim.astype(BF16)

    @pl.when(step == 0)
    def _():
        act, slope, rim = activate(bcpre_ref[...], rimbc_ref[...], bctaps_ref[...])
        bcact_ref[...] = act
        bcslope_ref[...] = slope
        bcrimt_ref[...] = rim
        bctok_ref[...] = mm_nt(ident, act).astype(BF16)

    act, slope, rim = activate(pre_ref[...], rim_ref[...], taps_ref[...])
    xa_ref[...] = act
    slope_ref[...] = slope
    rimt_ref[...] = rim
    for k in range(PER):
        head = step * PER + k
        lo, hi = k * HD, (k + 1) * HD
        u = head_row(rows_ref, DT, head) * act[lo:hi].astype(F32)
        eu_ref[lo:hi, :] = (head_row(rows_ref, END, head) * u).astype(BF16)
        carry = head_row(rows_ref, CARRY, head)
        cdy_ref[lo:hi, :] = (carry * dyt_ref[lo:hi, :].astype(F32)).astype(BF16)
        parts = split(carry[:, BLK - 1 :], 3)
        which = iota((16, NS), 0)
        through = jnp.where(
            which == 0, parts[0].astype(F32),
            jnp.where(which == 1, parts[1].astype(F32), parts[2].astype(F32)),
        ).astype(BF16)
        pay_ref[2 * k, 64:80, :] = through
        pay_ref[2 * k + 1, 64:80, :] = through
    state = mm(eu_ref[...], bctok_ref[:, :NS]).astype(BF16)
    back = mm(cdy_ref[...], bctok_ref[:, NS:]).astype(BF16)
    for j in range(2 * PER):
        pay_ref[j, 0:32, :] = state[j * 32 : j * 32 + 32]
        pay_ref[j, 32:64, :] = back[j * 32 : j * 32 + 32]


def block_kernel(
    xa_ref, gy_ref, dyt_ref, rows_ref, bctok_ref, bcact_ref,
    y_ref, du_ref, dbc_ref,
    scores_ref, link_ref, acol_ref, dg_ref,
):
    step = pl.program_id(0)

    @pl.when(step == 0)
    def _():
        ident = eye(BLK, BF16)
        scores_ref[...] = mm_nt(bctok_ref[:, NS:], bctok_ref[:, :NS])
        seg_row = rows_ref[MASK, 4:5, :]
        seg_col = mm_nt(ident, rows_ref[MASK].astype(BF16))[:, 4:5]
        later = iota((BLK, BLK), 0) >= iota((BLK, BLK), 1)
        linked = jnp.logical_and(later, seg_col == seg_row)
        link_ref[...] = jnp.where(linked, 0.0, -jnp.inf)
        dg_ref[...] = jnp.zeros_like(dg_ref)
        cumul = pick_nt(ident, rows_ref[CUMUL], 3)
        for at in range(acol_ref.shape[0]):
            acol_ref[at] = cumul[:, at * PER : (at + 1) * PER]

    acols = acol_ref[step]
    for k in range(PER):
        head = step * PER + k
        lo, hi = k * HD, (k + 1) * HD
        arow = head_row(rows_ref, CUMUL, head)
        u_low = (head_row(rows_ref, DT, head) * xa_ref[lo:hi, :].astype(F32)).astype(BF16)
        du_first = None
        for tb in range(2):
            t0, t1 = tb * 128, tb * 128 + 128
            decay = jnp.exp(acols[t0:t1, k : k + 1] - arow[:, :t1] + link_ref[t0:t1, :t1])
            mixed = (decay * scores_ref[t0:t1, :t1]).astype(BF16)
            y_ref[lo:hi, t0:t1] = mm_nt(u_low[:, :t1], mixed)
            du = mm(dyt_ref[lo:hi, t0:t1], mixed)
            if tb == 0:
                du_first = du
            else:
                du_ref[lo:hi, :128] = du_first + du[:, :128]
                du_ref[lo:hi, 128:] = du[:, 128:]
            dmix = mm(gy_ref[t0:t1, lo:hi], u_low[:, :t1])
            dg_ref[t0:t1, :t1] += decay * dmix

    @pl.when(step == pl.num_programs(0) - 1)
    def _():
        dg = dg_ref[...].astype(BF16)
        dbc_ref[:NS, :] = mm(bcact_ref[NS:, :], dg)
        dbc_ref[NS:, :] = mm_nt(bcact_ref[:NS, :], dg)


def scan_kernel(in_ref, out_ref):
    peers = in_ref.shape[0]
    ahead = jnp.zeros((32, NS), F32)
    behind = jnp.zeros((32, NS), F32)

    def through(at):
        parts = in_ref[at, 64:80, :].astype(F32)
        return parts[0:1] + parts[1:2] + parts[2:3]

    for i in range(peers):
        out_ref[i, 0:32, :] = ahead.astype(BF16)
        ahead = through(i) * ahead + in_ref[i, 0:32, :].astype(F32)
        at = peers - 1 - i
        out_ref[at, 32:64, :] = behind.astype(BF16)
        behind = through(at) * behind + in_ref[at, 32:64, :].astype(F32)


def bc_kernel(
    state_ref, eu_ref, cdy_ref, dbc_ref, bcslope_ref, bct_ref, bcrimt_ref, bctaps_ref, rows_ref,
    pay_ref,
    acc_ref,
):
    step = pl.program_id(0)

    @pl.when(step == 0)
    def _():
        acc_ref[...] = dbc_ref[...]

    small = eye(NS, BF16)
    state_in = state_ref[:, 0:32, :].reshape(BLK, NS)
    state_back = state_ref[:, 32:64, :].reshape(BLK, NS)
    acc_ref[:NS, :] += mm(mm_nt(small, state_back).astype(BF16), eu_ref[...])
    acc_ref[NS:, :] += mm(mm_nt(small, state_in).astype(BF16), cdy_ref[...])

    @pl.when(step == pl.num_programs(0) - 1)
    def _():
        grad, spill, weights = conv_back(
            acc_ref[...] * bcslope_ref[...], bct_ref[...].astype(F32),
            bcrimt_ref[...].astype(F32), bctaps_ref[...], masks_of(rows_ref),
        )
        token = mm_nt(eye(BLK, BF16), grad.astype(BF16)).astype(BF16)
        last8 = (iota((8, 128), 0) + 120 == iota((8, 128), 1)).astype(BF16)
        rest = jnp.concatenate([weights, mm_nt(last8, spill.astype(BF16))], axis=0).astype(BF16)
        shares = pay_ref.shape[0]
        share = BLK // shares
        for j in range(shares):
            pay_ref[j, 0:share, :] = token[j * share : (j + 1) * share]
            pay_ref[j, share : share + 16, :] = rest


def x_kernel(
    state_ref, xa_ref, slope_ref, y_ref, du_ref, xt_ref, dyt_ref, rimt_ref, taps_ref, rows_ref,
    bctok_ref,
    out_ref, gx_ref, last_ref, spill_ref, gw_ref, gdt_ref, gh_ref,
    red_ref,
):
    step = pl.program_id(0)
    ident = eye(BLK, BF16)
    masks = masks_of(rows_ref)
    state_in = state_ref[:, 0:32, :].reshape(BLK, NS)
    state_back = state_ref[:, 32:64, :].reshape(BLK, NS)
    carried = mm_nt(state_in, bctok_ref[:, NS:])
    from_end = mm_nt(state_back, bctok_ref[:, :NS])
    both = state_in.astype(F32) * state_back.astype(F32)
    last_lane = iota((1, BLK), 1) == BLK - 1
    y_parts, g_parts = [], []
    for k in range(PER):
        head = step * PER + k
        lo, hi = k * HD, (k + 1) * HD
        dt = head_row(rows_ref, DT, head)
        carry = head_row(rows_ref, CARRY, head)
        skip = head_row(rows_ref, SKIP, head)
        x_h = xa_ref[lo:hi, :].astype(F32)
        dy_h = dyt_ref[lo:hi, :].astype(F32)
        y_h = y_ref[lo:hi, :] + carry * carried[lo:hi]
        ext = head_row(rows_ref, END, head) * from_end[lo:hi]
        du = du_ref[lo:hi, :] + ext
        u_low = (dt * x_h).astype(BF16).astype(F32)
        at_end = jnp.sum(jnp.sum(u_low * ext, axis=0, keepdims=True), axis=1, keepdims=True)
        joint = jnp.sum(jnp.sum(both[lo:hi], axis=0, keepdims=True), axis=1, keepdims=True)
        at_end = at_end + carry[:, BLK - 1 :] * joint
        ga = jnp.sum(dy_h * y_h - u_low * du, axis=0, keepdims=True)
        red_ref[0, pl.ds(head, 1), :] = ga + jnp.where(last_lane, at_end, 0.0)
        red_ref[1, pl.ds(head, 1), :] = jnp.sum(x_h * du, axis=0, keepdims=True)
        red_ref[2, pl.ds(head, 1), :] = jnp.sum(x_h * dy_h, axis=0, keepdims=True)
        y_parts.append((y_h + skip * x_h).astype(BF16))
        g_parts.append((dt * du + skip * dy_h) * slope_ref[lo:hi, :])
    out_ref[...] = mm_nt(ident, jnp.concatenate(y_parts, axis=0)).astype(BF16)
    grad, spill, weights = conv_back(
        jnp.concatenate(g_parts, axis=0), xt_ref[...].astype(F32), rimt_ref[...].astype(F32),
        taps_ref[...], masks,
    )
    gx_ref[...] = mm_nt(ident, grad.astype(BF16)).astype(BF16)
    pick = (iota((RIM, 128), 0) + (128 - RIM) == iota((RIM, 128), 1)).astype(BF16)
    last_ref[...] = pick_nt(pick, grad[:, 128:], 2)
    spill_ref[...] = pick_nt(pick, spill, 2)
    gw_ref[...] = weights

    @pl.when(step == pl.num_programs(0) - 1)
    def _():
        later = (iota((BLK, BLK), 0) >= iota((BLK, BLK), 1)).astype(BF16)
        grad_log = pick_right(red_ref[0], later, 3)
        rate = rows_ref[RATE]
        grad_step = (red_ref[1] - rate * grad_log) * rows_ref[SIG]
        gdt_ref[...] = grad_step
        which = iota((8, BLK), 0)
        terms = (-rate * rows_ref[DT] * grad_log, grad_step, red_ref[2])
        gh_ref[...] = jnp.zeros_like(gh_ref)
        gh_ref[:, : rate.shape[0]] = sum(
            pick_nt((which == k).astype(BF16), term, 3) for k, term in enumerate(terms)
        )


def patch_kernel(gx_ref, last_ref, spill_ref, out_ref):
    del gx_ref
    out_ref[...] = (last_ref[...] + spill_ref[...]).astype(BF16)


def pack_kernel(got_ref, gw_ref, gh_ref, sums_ref, own_ref, spill_ref):
    share = own_ref.shape[0]
    total = jnp.sum(got_ref[...].astype(F32), axis=0)
    own_ref[...] = total[:share]
    spill_ref[...] = total[share + 8 :]
    width = gw_ref.shape[1]
    sums_ref[:, :width] = gw_ref[...]
    sums_ref[:, width : width + 256] = total[share : share + 8]
    sums_ref[:, width + 256 :] = gh_ref[...]


def finish_kernel(a_ref, b_ref, c_ref, d_ref, wx_ref, wbc_ref, heads_ref):
    total = (a_ref[...] + b_ref[...]) + (c_ref[...] + d_ref[...])
    width = wx_ref.shape[1]
    wx_ref[...] = total[:4, :width]
    wbc_ref[...] = total[:4, width : width + 256]
    heads_ref[...] = total[:3, width + 256 : width + 256 + heads_ref.shape[1]]


def whole(shape):
    zeros = (0,) * len(shape)
    return pl.BlockSpec(shape, lambda *_: zeros)


def columns(rows):
    return pl.BlockSpec((rows, BLK), lambda i: (0, i))


def channel_rows(width):
    return pl.BlockSpec((BLK, width), lambda i: (i, 0))


def shaped(shape, dtype):
    return jax.ShapeDtypeStruct(shape, dtype)


def stored(shape, dtype):
    return pltpu.HBM(shape, dtype)


def from_hbm(*values):
    return [pltpu.with_memory_space_constraint(value, pltpu.HBM) for value in values]


def passed_along(value, by):
    peers = lax.axis_size("ctx")
    pairs = [(i, i + by) for i in range(peers) if 0 <= i + by < peers]
    return lax.ppermute(value, "ctx", pairs)


def summed_over_ctx(value):
    peers = lax.axis_size("ctx")

    def turned(value, stride):
        def to(i, by):
            at = i // stride % 4
            return i + ((at + by) % 4 - at) * stride

        return [value] + [
            lax.ppermute(value, "ctx", [(i, to(i, by)) for i in range(peers)])
            for by in (1, 2, 3)
        ]

    value = value + lax.ppermute(value, "ctx", [(i, i ^ 1) for i in range(peers)])
    own, one, two, three = turned(value, 2)
    return turned((own + one) + (two + three), 8)


def cost(micros):
    return pl.CostEstimate(
        flops=int(micros * 1e8), bytes_accessed=int(micros * 3e6), transcendentals=0
    )


def local(x_raw, bc_raw, dt_raw, conv_x, conv_bc, a_log, dt_bias, skip_weight, segment, grad_y):
    rows, channels = x_raw.shape
    heads = dt_raw.shape[1]
    steps = channels // BLK
    peers = lax.axis_size("ctx")
    shares = lax.axis_size("head")
    share = rows // shares
    params = pltpu.CompilerParams(vmem_limit_bytes=VMEM)
    rim = passed_along(jnp.concatenate([x_raw[rows - RIM :], bc_raw[rows - RIM :]], axis=1), 1)
    padded = jnp.concatenate([jnp.full((3,), -1, jnp.int32), segment])
    seg_ext = lax.dynamic_slice_in_dim(padded, lax.axis_index("ctx") * rows, rows + 3)
    seg = jnp.stack([seg_ext[min(k, 3) : min(k, 3) + rows] for k in range(8)]).astype(F32)
    hv = jnp.stack([a_log, dt_bias, skip_weight, skip_weight])
    row_spec = whole((8, heads, rows))
    square = whole((256, rows))
    by_channel = channel_rows(rows)

    def chan(dtype):
        return stored((channels, rows), dtype)

    xt, dyt, pre, taps, head_rows, bct, bcpre, bctaps = pl.pallas_call(
        prep_kernel,
        grid=(steps,),
        in_specs=[
            columns(rows), columns(rows), columns(4), whole((rows, 256)), whole((4, 256)),
            whole((heads, rows)), whole((4, heads)), whole((8, rows)),
        ],
        out_specs=[
            by_channel, by_channel, by_channel, channel_rows(128), row_spec,
            square, square, whole((256, 128)),
        ],
        out_shape=[
            chan(BF16), chan(BF16), shaped((channels, rows), F32), stored((channels, 128), F32),
            stored((8, heads, rows), F32), stored((256, rows), BF16), shaped((256, rows), F32),
            stored((256, 128), F32),
        ],
        compiler_params=params,
        cost_estimate=cost(4),
        name="prep",
    )(*from_hbm(x_raw, grad_y, conv_x, bc_raw, conv_bc, dt_raw.T), hv, seg)

    pay, xa, slope, eu, cdy, rimt, bctok, bcact, bcslope, bcrimt = pl.pallas_call(
        state_kernel,
        grid=(steps,),
        in_specs=[
            by_channel, columns(RIM), channel_rows(128), by_channel, row_spec,
            square, pl.BlockSpec((RIM, 256), lambda i: (0, channels // 256)), whole((256, 128)),
        ],
        out_specs=[
            pl.BlockSpec((8, 80, NS), lambda i: (i, 0, 0)),
            by_channel, by_channel, by_channel, by_channel, channel_rows(128),
            whole((rows, 256)), square, square, whole((256, 128)),
        ],
        out_shape=[
            shaped((peers, 80, NS), BF16), chan(BF16), chan(F32), chan(BF16), chan(BF16),
            stored((channels, 128), BF16), stored((rows, 256), BF16), stored((256, rows), BF16),
            stored((256, rows), F32), stored((256, 128), BF16),
        ],
        compiler_params=params,
        cost_estimate=cost(4),
        name="states",
    )(pre, rim, *from_hbm(taps, dyt, head_rows), bcpre, rim, *from_hbm(bctaps))

    got = lax.all_to_all(pay, "ctx", 0, 0, tiled=True)

    y_loc, du_loc, dbc = pl.pallas_call(
        block_kernel,
        grid=(steps,),
        in_specs=[
            by_channel, columns(rows), by_channel, row_spec, whole((rows, 256)), square,
        ],
        out_specs=[by_channel, by_channel, square],
        out_shape=[chan(F32), chan(F32), stored((256, rows), F32)],
        scratch_shapes=[
            pltpu.VMEM((rows, rows), F32), pltpu.VMEM((rows, rows), F32),
            pltpu.VMEM((steps, rows, PER), F32), pltpu.VMEM((rows, rows), F32),
        ],
        compiler_params=params,
        cost_estimate=cost(8),
        name="in_block",
    )(*from_hbm(xa, grad_y, dyt, head_rows, bctok, bcact))

    carried = pl.pallas_call(
        scan_kernel,
        in_specs=[pl.BlockSpec(memory_space=pltpu.VMEM)],
        out_specs=pl.BlockSpec(memory_space=pltpu.VMEM),
        out_shape=stored((peers, 64, NS), BF16),
        compiler_params=params,
        cost_estimate=cost(1),
        name="state_scan",
    )(*from_hbm(got))
    states = lax.all_to_all(carried, "ctx", 0, 0, tiled=True)

    state_spec = pl.BlockSpec((8, 64, NS), lambda i: (i, 0, 0))
    pay_bc = pl.pallas_call(
        bc_kernel,
        grid=(steps,),
        in_specs=[
            state_spec, by_channel, by_channel, square, square, square, whole((256, 128)),
            whole((256, 128)), row_spec,
        ],
        out_specs=whole((shares, share + 16, 256)),
        out_shape=shaped((shares, share + 16, 256), BF16),
        scratch_shapes=[pltpu.VMEM((256, rows), F32)],
        compiler_params=params,
        cost_estimate=cost(4),
        name="bc_part",
    )(states, *from_hbm(eu, cdy, dbc, bcslope, bct, bcrimt, bctaps, head_rows))
    got_bc = lax.all_to_all(pay_bc, "head", 0, 0, tiled=True)

    ssd_out, gx, last, spill, gw, grad_dt, gh = pl.pallas_call(
        x_kernel,
        grid=(steps,),
        in_specs=[
            state_spec, by_channel, by_channel, by_channel, by_channel, by_channel, by_channel,
            channel_rows(128), channel_rows(128), row_spec, whole((rows, 256)),
        ],
        out_specs=[
            columns(rows), columns(rows), columns(RIM), columns(RIM), columns(8),
            whole((heads, rows)), whole((8, 128)),
        ],
        out_shape=[
            stored((rows, channels), BF16), stored((rows, channels), BF16),
            stored((RIM, channels), F32), stored((RIM, channels), F32), stored((8, channels), F32),
            stored((heads, rows), F32), stored((8, 128), F32),
        ],
        scratch_shapes=[pltpu.VMEM((3, heads, rows), F32)],
        compiler_params=params,
        cost_estimate=cost(10),
        name="x_part",
    )(states, *from_hbm(xa, slope, y_loc, du_loc, xt, dyt, rimt, taps, head_rows, bctok))

    spill_x = passed_along(spill, -1)
    grad_x = pl.pallas_call(
        patch_kernel,
        grid=(1,),
        in_specs=[
            pl.BlockSpec(memory_space=pl.ANY), whole((RIM, channels)), whole((RIM, channels)),
        ],
        out_specs=pl.BlockSpec((RIM, channels), lambda i: (rows // RIM - 1, 0)),
        out_shape=stored((rows, channels), BF16),
        input_output_aliases={0: 0},
        compiler_params=params,
        cost_estimate=cost(1),
        name="last_rows",
    )(*from_hbm(gx, last), spill_x)

    vmem = pl.BlockSpec(memory_space=pltpu.VMEM)
    width = channels + 256 + 128
    sums, own_bc, spill_bc = pl.pallas_call(
        pack_kernel,
        in_specs=[vmem] * 3,
        out_specs=[vmem] * 3,
        out_shape=[shaped((8, width), F32), shaped((share, 256), F32), shaped((8, 256), F32)],
        compiler_params=params,
        cost_estimate=cost(1),
        name="pack_sums",
    )(got_bc, *from_hbm(gw, gh))
    spill_bc = passed_along(spill_bc, -1)
    parts = summed_over_ctx(sums)
    grad_wx, grad_wbc, grad_heads = pl.pallas_call(
        finish_kernel,
        in_specs=[vmem] * 4,
        out_specs=[vmem] * 3,
        out_shape=[stored((4, channels), F32), stored((4, 256), F32), stored((3, heads), F32)],
        compiler_params=params,
        cost_estimate=cost(1),
        name="finish_sums",
    )(*parts)
    is_last = lax.axis_index("head") == shares - 1
    grad_bc = own_bc + jnp.pad(jnp.where(is_last, spill_bc, 0.0), ((share - 8, 0), (0, 0)))
    return ssd_out, grad_x, grad_bc, grad_dt.T, grad_wx, grad_wbc, grad_heads


def solution(mesh):
    in_specs = (
        P("ctx", "head"), P("ctx", None), P("ctx", "head"), P(None, "head"), P(),
        P("head"), P("head"), P("head"), P(), P("ctx", "head"),
    )
    out_specs = (
        P("ctx", "head"), P("ctx", "head"), P(("ctx", "head"), None), P("ctx", "head"),
        P(None, "head"), P(), P(None, "head"),
    )
    return jax.shard_map(local, mesh=mesh, in_specs=in_specs, out_specs=out_specs, check_vma=False)
```

time: 130 us -> 103 us (0.79)
  the two profiles are of different devices: /device:TPU:2 before, /device:TPU:32 now
where the time goes in v2:
time: 103 us; the launch traced here: 102 us
  Pallas kernels  34.5 us (33%)
  starting transfers between devices  26.5 us (26%)
  blocking collectives  21.5 us (21%)
  waiting for transfers between devices  16.1 us (16%)
  local copies, waits for them, and re-layouts  1.63 us (2%)
    all_to_all x1, blocking collectives, local(): got = lax.all_to_all(pay, 'ctx', 0, 0, tiled=True)  21.5 us
    ppermute x6, waiting for transfers between devices, turned(): lax.ppermute(value, 'ctx', [(i, to(i, by)) for i in range(peers)])  9.55 us
    ppermute x6, starting transfers between devices, turned(): lax.ppermute(value, 'ctx', [(i, to(i, by)) for i in range(peers)])  9.02 us
    all_to_all x1, starting transfers between devices, local(): got_bc = lax.all_to_all(pay_bc, 'head', 0, 0, tiled=True)  8.57 us
    pallas_call x1, Pallas kernels, local(): pl.pallas_call(x_kernel, grid=(steps,), in_specs=[state_spec, by_channel,...  7.47 us
    all_to_all x1, waiting for transfers between devices, local(): states = lax.all_to_all(carried, 'ctx', 0, 0, tiled=True)  6.04 us
    pallas_call x1, Pallas kernels, local(): pl.pallas_call(prep_kernel, grid=(steps,), in_specs=[columns(rows), colum...  5.96 us
    pallas_call x1, Pallas kernels, local(): pl.pallas_call(block_kernel, grid=(steps,), in_specs=[by_channel, columns...  5.72 us
  transfers between devices with their start and end apart: 12, of which 6 were waited for; matrix products, arithmetic and copies ran while one was open for 1% of the time, Pallas kernels for 21%

profile of v2, /device:TPU:32, one launch (start us, length us, event | category | flops | bytes accessed | tf_op | source)
XLA Modules:
  0.0 101.7 jit_solution(6781352827749356217)
XLA Ops:
  0.7 0.7 slice-done
  1.4 1.7 %collective-permute-start = (bf16[16,1280]{1,0:T(8,128)(2,1)S(1)}, bf16[16,1280]{1,0:T(8,128)(2,1)S(1)}, u32[]{:S(2)}, u32[]{:S(2)}) collective-permute-start(bf16[16,1280]{1,0:T(8,128)(2,1)S(1)} %pad_maximum_fusion), channel_id=1, source_target_pairs={{0,8},{8,16},{16,24},{24,32},{32,40},{40,48},{48,56},{56,64},{64,7... | collective-permute-start | bytes 122888 | tf_op jit(solution)/shard_map/ppermute | solution.py:430
  3.2 0.1 pad_dynamic-slice_fusion
  3.3 0.1 fusion
  3.3 0.7 copy-done.1
  4.1 6.0 %prep.1 = (bf16[1024,256]{1,0:T(8,128)(2,1)}, bf16[1024,256]{1,0:T(8,128)(2,1)}, f32[1024,256]{1,0:T(8,128)S(1)}, f32[1024,128]{1,0:T(8,128)}, f32[8,16,256]{2,1...) custom-call(bf16[256,1024]{1,0:T(8,128)(2,1)} %x_ref.1, ...), custom_call_target="tpu_custom_call" | custom-call | flops 400000000 | bytes 12000000 | tf_op jit(solution)/shard_map/prep/pallas_call | solution.py:477
  10.0 5.6 %states.1 = (bf16[32,80,128]{2,1,0:T(8,128)(2,1)S(1)}, bf16[1024,256]{1,0:T(8,128)(2,1)}, f32[1024,256]{1,0:T(8,128)}, bf16[1024,256]{1,0:T(8,128)(2,1)}, bf16[1...) custom-call(f32[1024,256]{1,0:T(8,128)S(1)} %get-tuple-element.41.pr, ...), custom_call_target="tpu_custom_call" | custom-call | flops 400000000 | bytes 12000000 | tf_op jit(solution)/shard_map/states/pallas_call | solution.py:498
  15.6 21.5 %all_to_all.15.in_ref = bf16[32,80,128]{2,1,0:T(8,128)(2,1)} all-to-all(bf16[32,80,128]{2,1,0:T(8,128)(2,1)S(1)} %get-tuple-element.47), channel_id=1, replica_groups=mesh['ctx'=32,'head'=8] {'ctx'}, dimensions={0} | all-to-all | bytes 1310720 | tf_op jit(solution)/shard_map/all_to_all | solution.py:520
  37.2 2.1 %state_scan.1 = bf16[32,64,128]{2,1,0:T(8,128)(2,1)} custom-call(bf16[32,80,128]{2,1,0:T(8,128)(2,1)} %all_to_all.15.in_ref), custom_call_target="tpu_custom_call" | custom-call | flops 100000000 | bytes 3000000 | tf_op jit(solution)/shard_map/state_scan/pallas_call | solution.py:539
  39.2 3.9 %all-to-all-start.1 = ((bf16[32,64,128]{2,1,0:T(8,128)(2,1)}), bf16[32,64,128]{2,1,0:T(8,128)(2,1)S(1)}, u32[]{:S(2)}, u32[]{:S(2)}) async-start(bf16[32,64,128]{2,1,0:T(8,128)(2,1)} %state_scan.1), calls=%async_computation.1 | async-start | bytes 1048576 | tf_op jit(solution)/shard_map/all_to_all | solution.py:548
  43.1 5.7 %in_block.1 = (f32[1024,256]{1,0:T(8,128)}, f32[1024,256]{1,0:T(8,128)}, f32[256,256]{1,0:T(8,128)}) custom-call(bf16[1024,256]{1,0:T(8,128)(2,1)} %get-tuple-element.48.xa_ref, bf16[256,1024]{1,0:T(8,128)(2,1)} %gy_ref.3, bf16[1024,256]{1,0:T(8,128)(2,1)} %get-tuple-element.43.dyt_ref, f32[8,16,256]{2,1,0:T(8,128)} %get-tuple-element.44.rows_ref, ...), custom_call_target="tpu_custom_call" | custom-call | flops 800000000 | bytes 24000000 | tf_op jit(solution)/shard_map/in_block/pallas_call | solution.py:522
  48.8 6.0 %all-to-all-done.1.state_ref = bf16[32,64,128]{2,1,0:T(8,128)(2,1)S(1)} async-done(((bf16[32,64,128]{2,1,0:T(8,128)(2,1)}), bf16[32,64,128]{2,1,0:T(8,128)(2,1)S(1)}, u32[]{:S(2)}, u32[]{:S(2)}) %all-to-all-start.1) | async-done | bytes 524320 | tf_op jit(solution)/shard_map/all_to_all | solution.py:548
  54.9 4.8 %bc_part.1 = bf16[8,48,256]{2,1,0:T(8,128)(2,1)} custom-call(bf16[32,64,128]{2,1,0:T(8,128)(2,1)S(1)} %all-to-all-done.1.state_ref, bf16[1024,256]{1,0:T(8,128)(2,1)} %get-tuple-element.60.eu_ref, bf16[1024,256]{1,0:T(8,128)(2,1)} %get-tuple-element.61.cdy_ref, f32[256,256]{1,0:T(8,128)} %get-tuple-element.62.dbc_ref, ...), custom_call_target="tpu_custom_call" | custom-call | flops 400000000 | bytes 12000000 | tf_op jit(solution)/shard_map/bc_part/pallas_call | solution.py:551
  59.7 8.6 %all-to-all-start.2 = ((bf16[8,48,256]{2,1,0:T(8,128)(2,1)}), bf16[8,48,256]{2,1,0:T(8,128)(2,1)S(1)}, u32[]{:S(2)}, u32[]{:S(2)}) async-start(bf16[8,48,256]{2,1,0:T(8,128)(2,1)} %bc_part.1), calls=%async_computation.2 | async-start | bytes 393216 | tf_op jit(solution)/shard_map/all_to_all | solution.py:565
  68.2 7.5 %x_part.1 = (bf16[256,1024]{1,0:T(8,128)(2,1)}, bf16[256,1024]{1,0:T(8,128)(2,1)}, f32[16,1024]{1,0:T(8,128)}, f32[16,1024]{1,0:T(8,128)}, f32[8,1024]{1,0:T(8,1...) custom-call(bf16[32,64,128]{2,1,0:T(8,128)(2,1)S(1)} %all-to-all-done.1.state_ref, bf16[1024,256]{1,0:T(8,128)(2,1)} %get-tuple-element.48.xa_ref, ...), custom_call_target="tpu_custom_call" | custom-call | flops 1000000000 | bytes 30000000 | tf_op jit(solution)/shard_map/x_part/pallas_call | solution.py:567
  75.7 1.3 %collective-permute-start.1 = (f32[16,1024]{1,0:T(8,128)}, f32[16,1024]{1,0:T(8,128)S(1)}, u32[]{:S(2)}, u32[]{:S(2)}) collective-permute-start(f32[16,1024]{1,0:T(8,128)} %get-tuple-element.59), channel_id=1, source_target_pairs={{8,0},{16,8},{24,16},{32,24},{40,32},{48,40},{56,48},{64,56},{72,6... | collective-permute-start | bytes 196616 | tf_op jit(solution)/shard_map/ppermute | solution.py:430
  77.0 0.5 all-to-all-done.2.got_ref
  77.5 0.8 pack_sums.1
  78.3 0.8 collective-permute-start.3
  79.0 1.3 %collective-permute-start.2 = (f32[8,256]{1,0:T(8,128)S(1)}, f32[8,256]{1,0:T(8,128)S(1)}, u32[]{:S(2)}, u32[]{:S(2)}) collective-permute-start(f32[8,256]{1,0:T(8,128)S(1)} %get-tuple-element.69), channel_id=1, source_target_pairs={{8,0},{16,8},{24,16},{32,24},{40,32},{48,40},{56,48},{64,56},{72,6... | collective-permute-start | bytes 24584 | tf_op jit(solution)/shard_map/ppermute | solution.py:430
  80.3 1.5 %last_rows.1 = bf16[256,1024]{1,0:T(8,128)(2,1)} custom-call(bf16[256,1024]{1,0:T(8,128)(2,1)} %get-tuple-element.57.gx_ref, f32[16,1024]{1,0:T(8,128)} %get-tuple-element.58.last_ref, f32[16,1024]{1,0:T(8,128)S(1)} %collective-permute-done.1.spill_ref), custom_call_target="tpu_custom_call", output_to_operand_aliasing={{}: (0, {})} | custom-call | flops 100000000 | bytes 3000000 | tf_op jit(solution)/shard_map/last_rows/pallas_call | solution.py:590
  81.8 2.9 %collective-permute-start.6 = (f32[8,1408]{1,0:T(8,128)S(1)}, f32[8,1408]{1,0:T(8,128)S(1)}, u32[]{:S(2)}, u32[]{:S(2)}) collective-permute-start(f32[8,1408]{1,0:T(8,128)S(1)} %add.24), channel_id=1, source_target_pairs={{0,48},{8,56},{16,0},{24,8},{32,16},{40,24},{48,32},{56,40},{64,11... | collective-permute-start | bytes 135176 | tf_op jit(solution)/shard_map/ppermute | solution.py:442
  84.7 1.6 %collective-permute-start.5 = (f32[8,1408]{1,0:T(8,128)S(1)}, f32[8,1408]{1,0:T(8,128)S(1)}, u32[]{:S(2)}, u32[]{:S(2)}) collective-permute-start(f32[8,1408]{1,0:T(8,128)S(1)} %add.24), channel_id=1, source_target_pairs={{0,32},{8,40},{16,48},{24,56},{32,0},{40,8},{48,16},{56,24},{64,96... | collective-permute-start | bytes 135176 | tf_op jit(solution)/shard_map/ppermute | solution.py:442
  86.2 0.5 collective-permute-start.4
  86.8 3.7 %collective-permute-done.5 = f32[8,1408]{1,0:T(8,128)S(1)} collective-permute-done((f32[8,1408]{1,0:T(8,128)S(1)}, f32[8,1408]{1,0:T(8,128)S(1)}, u32[]{:S(2)}, u32[]{:S(2)}) %collective-permute-start.5) | collective-permute-done | bytes 45088 | tf_op jit(solution)/shard_map/ppermute | solution.py:442
  90.4 1.2 %collective-permute-done.4 = f32[8,1408]{1,0:T(8,128)S(1)} collective-permute-done((f32[8,1408]{1,0:T(8,128)S(1)}, f32[8,1408]{1,0:T(8,128)S(1)}, u32[]{:S(2)}, u32[]{:S(2)}) %collective-permute-start.4) | collective-permute-done | bytes 45088 | tf_op jit(solution)/shard_map/ppermute | solution.py:442
  91.7 1.1 %collective-permute-start.9 = (f32[8,1408]{1,0:T(8,128)S(1)}, f32[8,1408]{1,0:T(8,128)S(1)}, u32[]{:S(2)}, u32[]{:S(2)}) collective-permute-start(f32[8,1408]{1,0:T(8,128)S(1)} %add_add_fusion.a_ref), channel_id=1, source_target_pairs={{0,192},{8,200},{16,208},{24,216},{32,224},{40,232},{48,240},{56,2... | collective-permute-start | bytes 135176 | tf_op jit(solution)/shard_map/ppermute | solution.py:442
  92.8 3.0 %collective-permute-start.8 = (f32[8,1408]{1,0:T(8,128)S(1)}, f32[8,1408]{1,0:T(8,128)S(1)}, u32[]{:S(2)}, u32[]{:S(2)}) collective-permute-start(f32[8,1408]{1,0:T(8,128)S(1)} %add_add_fusion.a_ref), channel_id=1, source_target_pairs={{0,128},{8,136},{16,144},{24,152},{32,160},{40,168},{48,176},{56,1... | collective-permute-start | bytes 135176 | tf_op jit(solution)/shard_map/ppermute | solution.py:442
  95.8 0.6 pad_add_fusion
  96.4 2.3 %collective-permute-done.8.c_ref = f32[8,1408]{1,0:T(8,128)S(1)} collective-permute-done((f32[8,1408]{1,0:T(8,128)S(1)}, f32[8,1408]{1,0:T(8,128)S(1)}, u32[]{:S(2)}, u32[]{:S(2)}) %collective-permute-start.8) | collective-permute-done | bytes 45088 | tf_op jit(solution)/shard_map/ppermute | solution.py:442
  98.7 2.3 %collective-permute-done.7.b_ref = f32[8,1408]{1,0:T(8,128)S(1)} collective-permute-done((f32[8,1408]{1,0:T(8,128)S(1)}, f32[8,1408]{1,0:T(8,128)S(1)}, u32[]{:S(2)}, u32[]{:S(2)}) %collective-permute-start.7) | collective-permute-done | bytes 45088 | tf_op jit(solution)/shard_map/ppermute | solution.py:442
  101.0 0.6 finish_sums.1
  (24 shorter events, 0.2 us)
Async XLA Ops:
  0.6 0.8 slice-start
  0.6 0.8 slice-start.1
  1.4 1.8 %copy-start = (s32[8192]{0:T(1024)S(1)}, s32[8192]{0:T(1024)}, u32[]{:S(2)}) copy-start(s32[8192]{0:T(1024)} %param.18) | copy-start | bytes 98308
  1.4 8.6 %collective-permute-start = (bf16[16,1280]{1,0:T(8,128)(2,1)S(1)}, bf16[16,1280]{1,0:T(8,128)(2,1)S(1)}, u32[]{:S(2)}, u32[]{:S(2)}) collective-permute-start(bf16[16,1280]{1,0:T(8,128)(2,1)S(1)} %pad_maximum_fusion), channel_id=1, source_target_pairs={{0,8},{8,16},{16,24},{24,32},{32,40},{40,48},{48,56},{56,64},{64,7... | collective-permute-start | bytes 122888 | tf_op jit(solution)/shard_map/ppermute | solution.py:430
  3.3 0.7 copy-start.1
  3.3 0.7 copy-start.2
  3.3 0.7 copy-start.3
  39.2 15.7 %all-to-all-start.1 = ((bf16[32,64,128]{2,1,0:T(8,128)(2,1)}), bf16[32,64,128]{2,1,0:T(8,128)(2,1)S(1)}, u32[]{:S(2)}, u32[]{:S(2)}) async-start(bf16[32,64,128]{2,1,0:T(8,128)(2,1)} %state_scan.1), calls=%async_computation.1 | async-start | bytes 1048576 | tf_op jit(solution)/shard_map/all_to_all | solution.py:548
  59.7 17.8 %all-to-all-start.2 = ((bf16[8,48,256]{2,1,0:T(8,128)(2,1)}), bf16[8,48,256]{2,1,0:T(8,128)(2,1)S(1)}, u32[]{:S(2)}, u32[]{:S(2)}) async-start(bf16[8,48,256]{2,1,0:T(8,128)(2,1)} %bc_part.1), calls=%async_computation.2 | async-start | bytes 393216 | tf_op jit(solution)/shard_map/all_to_all | solution.py:565
  75.7 4.6 %collective-permute-start.1 = (f32[16,1024]{1,0:T(8,128)}, f32[16,1024]{1,0:T(8,128)S(1)}, u32[]{:S(2)}, u32[]{:S(2)}) collective-permute-start(f32[16,1024]{1,0:T(8,128)} %get-tuple-element.59), channel_id=1, source_target_pairs={{8,0},{16,8},{24,16},{32,24},{40,32},{48,40},{56,48},{64,56},{72,6... | collective-permute-start | bytes 196616 | tf_op jit(solution)/shard_map/ppermute | solution.py:430
  78.3 3.5 %collective-permute-start.3 = (f32[8,1408]{1,0:T(8,128)S(1)}, f32[8,1408]{1,0:T(8,128)S(1)}, u32[]{:S(2)}, u32[]{:S(2)}) collective-permute-start(f32[8,1408]{1,0:T(8,128)S(1)} %get-tuple-element.71), channel_id=1, source_target_pairs={{0,8},{8,0},{16,24},{24,16},{32,40},{40,32},{48,56},{56,48},{64,72... | collective-permute-start | bytes 135176 | tf_op jit(solution)/shard_map/ppermute | solution.py:446
  79.0 7.7 %collective-permute-start.2 = (f32[8,256]{1,0:T(8,128)S(1)}, f32[8,256]{1,0:T(8,128)S(1)}, u32[]{:S(2)}, u32[]{:S(2)}) collective-permute-start(f32[8,256]{1,0:T(8,128)S(1)} %get-tuple-element.69), channel_id=1, source_target_pairs={{8,0},{16,8},{24,16},{32,24},{40,32},{48,40},{56,48},{64,56},{72,6... | collective-permute-start | bytes 24584 | tf_op jit(solution)/shard_map/ppermute | solution.py:430
  81.8 4.9 %collective-permute-start.6 = (f32[8,1408]{1,0:T(8,128)S(1)}, f32[8,1408]{1,0:T(8,128)S(1)}, u32[]{:S(2)}, u32[]{:S(2)}) collective-permute-start(f32[8,1408]{1,0:T(8,128)S(1)} %add.24), channel_id=1, source_target_pairs={{0,48},{8,56},{16,0},{24,8},{32,16},{40,24},{48,32},{56,40},{64,11... | collective-permute-start | bytes 135176 | tf_op jit(solution)/shard_map/ppermute | solution.py:442
  84.7 5.8 %collective-permute-start.5 = (f32[8,1408]{1,0:T(8,128)S(1)}, f32[8,1408]{1,0:T(8,128)S(1)}, u32[]{:S(2)}, u32[]{:S(2)}) collective-permute-start(f32[8,1408]{1,0:T(8,128)S(1)} %add.24), channel_id=1, source_target_pairs={{0,32},{8,40},{16,48},{24,56},{32,0},{40,8},{48,16},{56,24},{64,96... | collective-permute-start | bytes 135176 | tf_op jit(solution)/shard_map/ppermute | solution.py:442
  86.2 5.4 %collective-permute-start.4 = (f32[8,1408]{1,0:T(8,128)S(1)}, f32[8,1408]{1,0:T(8,128)S(1)}, u32[]{:S(2)}, u32[]{:S(2)}) collective-permute-start(f32[8,1408]{1,0:T(8,128)S(1)} %add.24), channel_id=1, source_target_pairs={{0,16},{8,24},{16,32},{24,40},{32,48},{40,56},{48,0},{56,8},{64,80... | collective-permute-start | bytes 135176 | tf_op jit(solution)/shard_map/ppermute | solution.py:442
  91.7 4.7 %collective-permute-start.9 = (f32[8,1408]{1,0:T(8,128)S(1)}, f32[8,1408]{1,0:T(8,128)S(1)}, u32[]{:S(2)}, u32[]{:S(2)}) collective-permute-start(f32[8,1408]{1,0:T(8,128)S(1)} %add_add_fusion.a_ref), channel_id=1, source_target_pairs={{0,192},{8,200},{16,208},{24,216},{32,224},{40,232},{48,240},{56,2... | collective-permute-start | bytes 135176 | tf_op jit(solution)/shard_map/ppermute | solution.py:442
  92.8 5.9 %collective-permute-start.8 = (f32[8,1408]{1,0:T(8,128)S(1)}, f32[8,1408]{1,0:T(8,128)S(1)}, u32[]{:S(2)}, u32[]{:S(2)}) collective-permute-start(f32[8,1408]{1,0:T(8,128)S(1)} %add_add_fusion.a_ref), channel_id=1, source_target_pairs={{0,128},{8,136},{16,144},{24,152},{32,160},{40,168},{48,176},{56,1... | collective-permute-start | bytes 135176 | tf_op jit(solution)/shard_map/ppermute | solution.py:442
  95.8 5.3 %collective-permute-start.7 = (f32[8,1408]{1,0:T(8,128)S(1)}, f32[8,1408]{1,0:T(8,128)S(1)}, u32[]{:S(2)}, u32[]{:S(2)}) collective-permute-start(f32[8,1408]{1,0:T(8,128)S(1)} %add_add_fusion.a_ref), channel_id=1, source_target_pairs={{0,64},{8,72},{16,80},{24,88},{32,96},{40,104},{48,112},{56,120},{... | collective-permute-start | bytes 135176 | tf_op jit(solution)/shard_map/ppermute | solution.py:442

commit v3 on v2

--- a/solution.py
+++ b/solution.py
@@ -49,11 +49,6 @@
 
 def eye(n, dtype):
     return (iota((n, n), 0) == iota((n, n), 1)).astype(dtype)
-
-
-def silu_and_slope(pre):
-    sig = 1.0 / (1.0 + jnp.exp(-pre))
-    return pre * sig, sig * (1.0 + pre * (1.0 - sig))
 
 
 def conv_own(raw, taps, masks):
@@ -116,17 +111,33 @@
     return rows_ref[plane, pl.ds(head, 1), :]
 
 
-def prep_kernel(
-    x_ref, gy_ref, wx_ref, bc_ref, wbc_ref, dt_ref, hv_ref, seg_ref,
-    xt_ref, dyt_ref, pre_ref, taps_ref, rows_ref, bct_ref, bcpre_ref, bctaps_ref,
+def taps_of(ref):
+    return pick_nt(eye(BLK, BF16), ref[...], 3)
+
+
+def conv_all(raw_ref, rim_ref, w_ref, masks):
+    ident = eye(BLK, BF16)
+    raw = mm_nt(ident, raw_ref[...])
+    rim = mm_nt(ident, wide_rim(rim_ref[...]))
+    taps = taps_of(w_ref)
+    pre = conv_own(raw, taps, masks)
+    return raw, jnp.concatenate(
+        [pre[:, :128] + conv_rim(rim, taps, masks), pre[:, 128:]], axis=1
+    )
+
+
+def sigmoid(value):
+    return 1.0 / (1.0 + jnp.exp(-value))
+
+
+def state_kernel(
+    x_ref, rim_ref, gy_ref, wx_ref, bc_ref, rimbc_ref, wbc_ref, dt_ref, hv_ref, seg_ref,
+    pay_ref, xa_ref, dyt_ref, rows_ref, bctok_ref, bcact_ref,
 ):
+    step = pl.program_id(0)
     ident = eye(BLK, BF16)
 
-    def taps_of(ref):
-        taps = pick_nt(ident, ref[...], 3)
-        return jnp.concatenate([taps, jnp.zeros((BLK, 124), F32)], axis=1)
-
-    @pl.when(pl.program_id(0) == 0)
+    @pl.when(step == 0)
     def _():
         target = seg_ref[3:4, :]
         rows_ref[MASK] = jnp.concatenate(
@@ -147,76 +158,76 @@
         rows_ref[CUMUL] = cumul
         rows_ref[CARRY] = keep * jnp.exp(cumul)
         rows_ref[END] = jnp.exp(jnp.where(same_end, cumul[:, BLK - 1 :] - cumul, -jnp.inf))
-        rows_ref[SIG] = 1.0 / (1.0 + jnp.exp(-pre))
+        rows_ref[SIG] = sigmoid(pre)
         rows_ref[SKIP] = jnp.broadcast_to(per_head[:, 2:3], (heads, BLK))
         rows_ref[RATE] = jnp.broadcast_to(rate, (heads, BLK))
-        bct = mm_nt(ident, bc_ref[...])
-        bct_ref[...] = bct.astype(BF16)
-        bctaps = taps_of(wbc_ref)
-        bctaps_ref[...] = bctaps
-        bcpre_ref[...] = conv_own(bct, bctaps, masks_of(rows_ref))
-
-    raw = mm_nt(ident, x_ref[...])
-    xt_ref[...] = raw.astype(BF16)
-    dyt_ref[...] = mm_nt(ident, gy_ref[...]).astype(BF16)
-    taps = taps_of(wx_ref)
-    taps_ref[...] = taps
-    pre_ref[...] = conv_own(raw, taps, masks_of(rows_ref))
-
-
-def state_kernel(
-    pre_ref, rim_ref, taps_ref, dyt_ref, rows_ref, bcpre_ref, rimbc_ref, bctaps_ref,
-    pay_ref, xa_ref, slope_ref, eu_ref, cdy_ref, rimt_ref,
-    bctok_ref, bcact_ref, bcslope_ref, bcrimt_ref,
-):
-    step = pl.program_id(0)
-    ident = eye(BLK, BF16)
-    masks = masks_of(rows_ref)
-
-    def activate(pre, rim_rows, taps):
-        rim = mm_nt(ident, wide_rim(rim_rows))
-        pre = jnp.concatenate([pre[:, :128] + conv_rim(rim, taps, masks), pre[:, 128:]], axis=1)
-        act, slope = silu_and_slope(pre)
-        return act.astype(BF16), slope, rim.astype(BF16)
-
-    @pl.when(step == 0)
-    def _():
-        act, slope, rim = activate(bcpre_ref[...], rimbc_ref[...], bctaps_ref[...])
+        _, bcpre = conv_all(bc_ref, rimbc_ref, wbc_ref, masks_of(rows_ref))
+        act = (bcpre * sigmoid(bcpre)).astype(BF16)
         bcact_ref[...] = act
-        bcslope_ref[...] = slope
-        bcrimt_ref[...] = rim
         bctok_ref[...] = mm_nt(ident, act).astype(BF16)
 
-    act, slope, rim = activate(pre_ref[...], rim_ref[...], taps_ref[...])
+    _, pre = conv_all(x_ref, rim_ref, wx_ref, masks_of(rows_ref))
+    act = (pre * sigmoid(pre)).astype(BF16)
     xa_ref[...] = act
-    slope_ref[...] = slope
-    rimt_ref[...] = rim
+    act = act.astype(F32)
+    dy = mm_nt(ident, gy_ref[...])
+    dyt_ref[...] = dy.astype(BF16)
+    ends, carries = [], []
     for k in range(PER):
         head = step * PER + k
         lo, hi = k * HD, (k + 1) * HD
-        u = head_row(rows_ref, DT, head) * act[lo:hi].astype(F32)
-        eu_ref[lo:hi, :] = (head_row(rows_ref, END, head) * u).astype(BF16)
         carry = head_row(rows_ref, CARRY, head)
-        cdy_ref[lo:hi, :] = (carry * dyt_ref[lo:hi, :].astype(F32)).astype(BF16)
+        weight = head_row(rows_ref, END, head) * head_row(rows_ref, DT, head)
+        ends.append((weight * act[lo:hi]).astype(BF16))
+        carries.append((carry * dy[lo:hi]).astype(BF16))
         parts = split(carry[:, BLK - 1 :], 3)
-        which = iota((16, NS), 0)
+        which = iota((8, NS), 0)
         through = jnp.where(
             which == 0, parts[0].astype(F32),
             jnp.where(which == 1, parts[1].astype(F32), parts[2].astype(F32)),
         ).astype(BF16)
-        pay_ref[2 * k, 64:80, :] = through
-        pay_ref[2 * k + 1, 64:80, :] = through
-    state = mm(eu_ref[...], bctok_ref[:, :NS]).astype(BF16)
-    back = mm(cdy_ref[...], bctok_ref[:, NS:]).astype(BF16)
+        pay_ref[2 * k, 64:72, :] = through
+        pay_ref[2 * k + 1, 64:72, :] = through
+    state = mm(jnp.concatenate(ends, axis=0), bctok_ref[:, :NS]).astype(BF16)
+    back = mm(jnp.concatenate(carries, axis=0), bctok_ref[:, NS:]).astype(BF16)
     for j in range(2 * PER):
         pay_ref[j, 0:32, :] = state[j * 32 : j * 32 + 32]
         pay_ref[j, 32:64, :] = back[j * 32 : j * 32 + 32]
 
 
+def slope_kernel(
+    x_ref, rim_ref, wx_ref, bc_ref, rimbc_ref, wbc_ref, xa_ref, dyt_ref, rows_ref,
+    xt_ref, slope_ref, eu_ref, cdy_ref, bct_ref, bcslope_ref,
+):
+    step = pl.program_id(0)
+    masks = masks_of(rows_ref)
+
+    def slope_of(pre):
+        sig = sigmoid(pre)
+        return sig * (1.0 + pre * (1.0 - sig))
+
+    @pl.when(step == 0)
+    def _():
+        raw, pre = conv_all(bc_ref, rimbc_ref, wbc_ref, masks)
+        bct_ref[...] = raw.astype(BF16)
+        bcslope_ref[...] = slope_of(pre)
+
+    raw, pre = conv_all(x_ref, rim_ref, wx_ref, masks)
+    xt_ref[...] = raw.astype(BF16)
+    slope_ref[...] = slope_of(pre)
+    for k in range(PER):
+        head = step * PER + k
+        lo, hi = k * HD, (k + 1) * HD
+        weight = head_row(rows_ref, END, head) * head_row(rows_ref, DT, head)
+        eu_ref[lo:hi, :] = (weight * xa_ref[lo:hi, :].astype(F32)).astype(BF16)
+        carry = head_row(rows_ref, CARRY, head)
+        cdy_ref[lo:hi, :] = (carry * dyt_ref[lo:hi, :].astype(F32)).astype(BF16)
+
+
 def block_kernel(
-    xa_ref, gy_ref, dyt_ref, rows_ref, bctok_ref, bcact_ref,
-    y_ref, du_ref, dbc_ref,
-    scores_ref, link_ref, acol_ref, dg_ref,
+    xa_ref, gy_ref, dyt_ref, rows_ref, bctok_ref, bcact_ref, slope_ref,
+    y_ref, g_ref, ends_ref, red_ref, dbc_ref,
+    scores_ref, link_ref, acol_ref, dg_ref, yt_ref, du_ref,
 ):
     step = pl.program_id(0)
 
@@ -239,21 +250,35 @@
         head = step * PER + k
         lo, hi = k * HD, (k + 1) * HD
         arow = head_row(rows_ref, CUMUL, head)
-        u_low = (head_row(rows_ref, DT, head) * xa_ref[lo:hi, :].astype(F32)).astype(BF16)
+        dt = head_row(rows_ref, DT, head)
+        skip = head_row(rows_ref, SKIP, head)
+        u_low = (dt * xa_ref[lo:hi, :].astype(F32)).astype(BF16)
         du_first = None
         for tb in range(2):
             t0, t1 = tb * 128, tb * 128 + 128
             decay = jnp.exp(acols[t0:t1, k : k + 1] - arow[:, :t1] + link_ref[t0:t1, :t1])
             mixed = (decay * scores_ref[t0:t1, :t1]).astype(BF16)
-            y_ref[lo:hi, t0:t1] = mm_nt(u_low[:, :t1], mixed)
+            yt_ref[:, t0:t1] = mm_nt(u_low[:, :t1], mixed)
             du = mm(dyt_ref[lo:hi, t0:t1], mixed)
             if tb == 0:
                 du_first = du
             else:
-                du_ref[lo:hi, :128] = du_first + du[:, :128]
-                du_ref[lo:hi, 128:] = du[:, 128:]
+                du_ref[:, :128] = du_first + du[:, :128]
+                du_ref[:, 128:] = du[:, 128:]
             dmix = mm(gy_ref[t0:t1, lo:hi], u_low[:, :t1])
             dg_ref[t0:t1, :t1] += decay * dmix
+        x_h = xa_ref[lo:hi, :].astype(F32)
+        dy_h = dyt_ref[lo:hi, :].astype(F32)
+        y_h = yt_ref[...]
+        du_h = du_ref[...]
+        slope = slope_ref[lo:hi, :]
+        y_ref[lo:hi, :] = y_h + skip * x_h
+        g_ref[lo:hi, :] = slope * (dt * du_h + skip * dy_h)
+        ends_ref[lo:hi, :] = slope * (dt * head_row(rows_ref, END, head))
+        ga = jnp.sum(dy_h * y_h - u_low.astype(F32) * du_h, axis=0, keepdims=True)
+        red_ref[0, pl.ds(head, 1), :] = ga
+        red_ref[1, pl.ds(head, 1), :] = jnp.sum(x_h * du_h, axis=0, keepdims=True)
+        red_ref[2, pl.ds(head, 1), :] = jnp.sum(x_h * dy_h, axis=0, keepdims=True)
 
     @pl.when(step == pl.num_programs(0) - 1)
     def _():
@@ -268,7 +293,7 @@
     behind = jnp.zeros((32, NS), F32)
 
     def through(at):
-        parts = in_ref[at, 64:80, :].astype(F32)
+        parts = in_ref[at, 64:72, :].astype(F32)
         return parts[0:1] + parts[1:2] + parts[2:3]
 
     for i in range(peers):
@@ -280,7 +305,7 @@
 
 
 def bc_kernel(
-    state_ref, eu_ref, cdy_ref, dbc_ref, bcslope_ref, bct_ref, bcrimt_ref, bctaps_ref, rows_ref,
+    state_ref, eu_ref, cdy_ref, dbc_ref, bcslope_ref, bct_ref, rimbc_ref, wbc_ref, rows_ref,
     pay_ref,
     acc_ref,
 ):
@@ -300,7 +325,7 @@
     def _():
         grad, spill, weights = conv_back(
             acc_ref[...] * bcslope_ref[...], bct_ref[...].astype(F32),
-            bcrimt_ref[...].astype(F32), bctaps_ref[...], masks_of(rows_ref),
+            mm_nt(eye(BLK, BF16), wide_rim(rimbc_ref[...])), taps_of(wbc_ref), masks_of(rows_ref),
         )
         token = mm_nt(eye(BLK, BF16), grad.astype(BF16)).astype(BF16)
         last8 = (iota((8, 128), 0) + 120 == iota((8, 128), 1)).astype(BF16)
@@ -313,8 +338,8 @@
 
 
 def x_kernel(
-    state_ref, xa_ref, slope_ref, y_ref, du_ref, xt_ref, dyt_ref, rimt_ref, taps_ref, rows_ref,
-    bctok_ref,
+    state_ref, xa_ref, y_ref, g_ref, ends_ref, xt_ref, dyt_ref, rim_ref, wx_ref, rows_ref,
+    bctok_ref, local_ref,
     out_ref, gx_ref, last_ref, spill_ref, gw_ref, gdt_ref, gh_ref,
     red_ref,
 ):
@@ -327,32 +352,30 @@
     from_end = mm_nt(state_back, bctok_ref[:, :NS])
     both = state_in.astype(F32) * state_back.astype(F32)
     last_lane = iota((1, BLK), 1) == BLK - 1
-    y_parts, g_parts = [], []
+    y_parts = []
     for k in range(PER):
         head = step * PER + k
         lo, hi = k * HD, (k + 1) * HD
         dt = head_row(rows_ref, DT, head)
         carry = head_row(rows_ref, CARRY, head)
-        skip = head_row(rows_ref, SKIP, head)
+        end = head_row(rows_ref, END, head)
         x_h = xa_ref[lo:hi, :].astype(F32)
-        dy_h = dyt_ref[lo:hi, :].astype(F32)
-        y_h = y_ref[lo:hi, :] + carry * carried[lo:hi]
-        ext = head_row(rows_ref, END, head) * from_end[lo:hi]
-        du = du_ref[lo:hi, :] + ext
+        add = carry * carried[lo:hi]
         u_low = (dt * x_h).astype(BF16).astype(F32)
-        at_end = jnp.sum(jnp.sum(u_low * ext, axis=0, keepdims=True), axis=1, keepdims=True)
+        fed = jnp.sum(u_low * from_end[lo:hi], axis=0, keepdims=True) * end
+        at_end = jnp.sum(fed, axis=1, keepdims=True)
         joint = jnp.sum(jnp.sum(both[lo:hi], axis=0, keepdims=True), axis=1, keepdims=True)
         at_end = at_end + carry[:, BLK - 1 :] * joint
-        ga = jnp.sum(dy_h * y_h - u_low * du, axis=0, keepdims=True)
+        ga = jnp.sum(dyt_ref[lo:hi, :].astype(F32) * add, axis=0, keepdims=True) - fed
         red_ref[0, pl.ds(head, 1), :] = ga + jnp.where(last_lane, at_end, 0.0)
-        red_ref[1, pl.ds(head, 1), :] = jnp.sum(x_h * du, axis=0, keepdims=True)
-        red_ref[2, pl.ds(head, 1), :] = jnp.sum(x_h * dy_h, axis=0, keepdims=True)
-        y_parts.append((y_h + skip * x_h).astype(BF16))
-        g_parts.append((dt * du + skip * dy_h) * slope_ref[lo:hi, :])
+        red_ref[1, pl.ds(head, 1), :] = end * jnp.sum(
+            x_h * from_end[lo:hi], axis=0, keepdims=True
+        )
+        y_parts.append((y_ref[lo:hi, :] + add).astype(BF16))
     out_ref[...] = mm_nt(ident, jnp.concatenate(y_parts, axis=0)).astype(BF16)
     grad, spill, weights = conv_back(
-        jnp.concatenate(g_parts, axis=0), xt_ref[...].astype(F32), rimt_ref[...].astype(F32),
-        taps_ref[...], masks,
+        g_ref[...] + ends_ref[...] * from_end, xt_ref[...].astype(F32),
+        mm_nt(ident, wide_rim(rim_ref[...])), taps_of(wx_ref), masks,
     )
     gx_ref[...] = mm_nt(ident, grad.astype(BF16)).astype(BF16)
     pick = (iota((RIM, 128), 0) + (128 - RIM) == iota((RIM, 128), 1)).astype(BF16)
@@ -363,29 +386,37 @@
     @pl.when(step == pl.num_programs(0) - 1)
     def _():
         later = (iota((BLK, BLK), 0) >= iota((BLK, BLK), 1)).astype(BF16)
-        grad_log = pick_right(red_ref[0], later, 3)
+        grad_log = pick_right(local_ref[0] + red_ref[0], later, 3)
         rate = rows_ref[RATE]
-        grad_step = (red_ref[1] - rate * grad_log) * rows_ref[SIG]
+        grad_step = (local_ref[1] + red_ref[1] - rate * grad_log) * rows_ref[SIG]
         gdt_ref[...] = grad_step
         which = iota((8, BLK), 0)
-        terms = (-rate * rows_ref[DT] * grad_log, grad_step, red_ref[2])
+        terms = (-rate * rows_ref[DT] * grad_log, grad_step, local_ref[2])
         gh_ref[...] = jnp.zeros_like(gh_ref)
         gh_ref[:, : rate.shape[0]] = sum(
             pick_nt((which == k).astype(BF16), term, 3) for k, term in enumerate(terms)
         )
 
 
-def patch_kernel(gx_ref, last_ref, spill_ref, out_ref):
+def patch_kernel(gx_ref, last_ref, own_ref, spill_ref, out_ref, bc_ref):
     del gx_ref
-    out_ref[...] = (last_ref[...] + spill_ref[...]).astype(BF16)
-
-
-def pack_kernel(got_ref, gw_ref, gh_ref, sums_ref, own_ref, spill_ref):
+    width = last_ref.shape[1]
+    out_ref[...] = (last_ref[...] + spill_ref[:, :width]).astype(BF16)
+    share = own_ref.shape[0]
+    bc_ref[: share - 8, :] = own_ref[: share - 8, :]
+    is_last = lax.axis_index("head") == lax.axis_size("head") - 1
+    came = spill_ref[RIM - 8 :, width:]
+    bc_ref[share - 8 :, :] = own_ref[share - 8 :, :] + jnp.where(is_last, came, 0.0)
+
+
+def pack_kernel(got_ref, gw_ref, gh_ref, spill_ref, sums_ref, own_ref, out_ref):
     share = own_ref.shape[0]
     total = jnp.sum(got_ref[...].astype(F32), axis=0)
     own_ref[...] = total[:share]
-    spill_ref[...] = total[share + 8 :]
     width = gw_ref.shape[1]
+    out_ref[:, :width] = spill_ref[...]
+    out_ref[: RIM - 8, width:] = jnp.zeros((RIM - 8, 256), F32)
+    out_ref[RIM - 8 :, width:] = total[share + 8 :]
     sums_ref[:, :width] = gw_ref[...]
     sums_ref[:, width : width + 256] = total[share : share + 8]
     sums_ref[:, width + 256 :] = gh_ref[...]
@@ -474,86 +505,93 @@
     def chan(dtype):
         return stored((channels, rows), dtype)
 
-    xt, dyt, pre, taps, head_rows, bct, bcpre, bctaps = pl.pallas_call(
-        prep_kernel,
-        grid=(steps,),
-        in_specs=[
-            columns(rows), columns(rows), columns(4), whole((rows, 256)), whole((4, 256)),
-            whole((heads, rows)), whole((4, heads)), whole((8, rows)),
-        ],
-        out_specs=[
-            by_channel, by_channel, by_channel, channel_rows(128), row_spec,
-            square, square, whole((256, 128)),
-        ],
-        out_shape=[
-            chan(BF16), chan(BF16), shaped((channels, rows), F32), stored((channels, 128), F32),
-            stored((8, heads, rows), F32), stored((256, rows), BF16), shaped((256, rows), F32),
-            stored((256, 128), F32),
-        ],
-        compiler_params=params,
-        cost_estimate=cost(4),
-        name="prep",
-    )(*from_hbm(x_raw, grad_y, conv_x, bc_raw, conv_bc, dt_raw.T), hv, seg)
-
-    pay, xa, slope, eu, cdy, rimt, bctok, bcact, bcslope, bcrimt = pl.pallas_call(
+    rim_bc_spec = pl.BlockSpec((RIM, 256), lambda i: (0, channels // 256))
+    local_spec = whole((3, heads, rows))
+
+    pay, xa, dyt, head_rows, bctok, bcact = pl.pallas_call(
         state_kernel,
         grid=(steps,),
         in_specs=[
-            by_channel, columns(RIM), channel_rows(128), by_channel, row_spec,
-            square, pl.BlockSpec((RIM, 256), lambda i: (0, channels // 256)), whole((256, 128)),
+            columns(rows), columns(RIM), columns(rows), columns(4),
+            whole((rows, 256)), rim_bc_spec, whole((4, 256)),
+            whole((heads, rows)), whole((4, heads)), whole((8, rows)),
         ],
         out_specs=[
-            pl.BlockSpec((8, 80, NS), lambda i: (i, 0, 0)),
-            by_channel, by_channel, by_channel, by_channel, channel_rows(128),
-            whole((rows, 256)), square, square, whole((256, 128)),
+            pl.BlockSpec((8, 72, NS), lambda i: (i, 0, 0)),
+            by_channel, by_channel, row_spec, whole((rows, 256)), square,
         ],
         out_shape=[
-            shaped((peers, 80, NS), BF16), chan(BF16), chan(F32), chan(BF16), chan(BF16),
-            stored((channels, 128), BF16), stored((rows, 256), BF16), stored((256, rows), BF16),
-            stored((256, rows), F32), stored((256, 128), BF16),
-        ],
-        compiler_params=params,
-        cost_estimate=cost(4),
+            shaped((peers, 72, NS), BF16), chan(BF16), chan(BF16),
+            stored((8, heads, rows), F32), stored((rows, 256), BF16), stored((256, rows), BF16),
+        ],
+        compiler_params=params,
+        cost_estimate=cost(7),
         name="states",
-    )(pre, rim, *from_hbm(taps, dyt, head_rows), bcpre, rim, *from_hbm(bctaps))
+    )(
+        *from_hbm(x_raw), rim, *from_hbm(grad_y, conv_x, bc_raw), rim,
+        *from_hbm(conv_bc, dt_raw.T), hv, seg,
+    )
 
     got = lax.all_to_all(pay, "ctx", 0, 0, tiled=True)
 
-    y_loc, du_loc, dbc = pl.pallas_call(
+    xt, slope, eu, cdy, bct, bcslope = pl.pallas_call(
+        slope_kernel,
+        grid=(steps,),
+        in_specs=[
+            columns(rows), columns(RIM), columns(4), whole((rows, 256)), rim_bc_spec,
+            whole((4, 256)), by_channel, by_channel, row_spec,
+        ],
+        out_specs=[by_channel, by_channel, by_channel, by_channel, square, square],
+        out_shape=[
+            chan(BF16), chan(F32), chan(BF16), chan(BF16),
+            stored((256, rows), BF16), stored((256, rows), F32),
+        ],
+        compiler_params=params,
+        cost_estimate=cost(6),
+        name="slopes",
+    )(*from_hbm(x_raw, rim, conv_x, bc_raw, rim, conv_bc, xa, dyt, head_rows))
+    got, xt = lax.optimization_barrier((got, xt))
+
+    carried = pl.pallas_call(
+        scan_kernel,
+        in_specs=[pl.BlockSpec(memory_space=pltpu.VMEM)],
+        out_specs=pl.BlockSpec(memory_space=pltpu.VMEM),
+        out_shape=shaped((peers, 64, NS), BF16),
+        compiler_params=params,
+        cost_estimate=cost(1),
+        name="state_scan",
+    )(got)
+    states = lax.all_to_all(carried, "ctx", 0, 0, tiled=True)
+
+    y_loc, g_loc, ends, red_loc, dbc = pl.pallas_call(
         block_kernel,
         grid=(steps,),
         in_specs=[
             by_channel, columns(rows), by_channel, row_spec, whole((rows, 256)), square,
-        ],
-        out_specs=[by_channel, by_channel, square],
-        out_shape=[chan(F32), chan(F32), stored((256, rows), F32)],
+            by_channel,
+        ],
+        out_specs=[by_channel, by_channel, by_channel, local_spec, square],
+        out_shape=[
+            chan(F32), chan(F32), chan(F32), stored((3, heads, rows), F32),
+            stored((256, rows), F32),
+        ],
         scratch_shapes=[
             pltpu.VMEM((rows, rows), F32), pltpu.VMEM((rows, rows), F32),
             pltpu.VMEM((steps, rows, PER), F32), pltpu.VMEM((rows, rows), F32),
+            pltpu.VMEM((HD, rows), F32), pltpu.VMEM((HD, rows), F32),
         ],
         compiler_params=params,
         cost_estimate=cost(8),
         name="in_block",
-    )(*from_hbm(xa, grad_y, dyt, head_rows, bctok, bcact))
-
-    carried = pl.pallas_call(
-        scan_kernel,
-        in_specs=[pl.BlockSpec(memory_space=pltpu.VMEM)],
-        out_specs=pl.BlockSpec(memory_space=pltpu.VMEM),
-        out_shape=stored((peers, 64, NS), BF16),
-        compiler_params=params,
-        cost_estimate=cost(1),
-        name="state_scan",
-    )(*from_hbm(got))
-    states = lax.all_to_all(carried, "ctx", 0, 0, tiled=True)
+    )(*from_hbm(xa, grad_y, dyt, head_rows, bctok, bcact, slope))
 
     state_spec = pl.BlockSpec((8, 64, NS), lambda i: (i, 0, 0))
     pay_bc = pl.pallas_call(
         bc_kernel,
         grid=(steps,),
         in_specs=[
-            state_spec, by_channel, by_channel, square, square, square, whole((256, 128)),
-            whole((256, 128)), row_spec,
+            state_spec, by_channel, by_channel, square, square, square, rim_bc_spec,
+            whole((4, 256)), row_spec,
         ],
         out_specs=whole((shares, share + 16, 256)),
         out_shape=shaped((shares, share + 16, 256), BF16),
@@ -561,7 +599,7 @@
         compiler_params=params,
         cost_estimate=cost(4),
         name="bc_part",
-    )(states, *from_hbm(eu, cdy, dbc, bcslope, bct, bcrimt, bctaps, head_rows))
+    )(states, *from_hbm(eu, cdy, dbc, bcslope, bct, rim, conv_bc, head_rows))
     got_bc = lax.all_to_all(pay_bc, "head", 0, 0, tiled=True)
 
     ssd_out, gx, last, spill, gw, grad_dt, gh = pl.pallas_call(
@@ -569,7 +607,7 @@
         grid=(steps,),
         in_specs=[
             state_spec, by_channel, by_channel, by_channel, by_channel, by_channel, by_channel,
-            channel_rows(128), channel_rows(128), row_spec, whole((rows, 256)),
+            columns(RIM), columns(4), row_spec, whole((rows, 256)), local_spec,
         ],
         out_specs=[
             columns(rows), columns(rows), columns(RIM), columns(RIM), columns(8),
@@ -580,40 +618,47 @@
             stored((RIM, channels), F32), stored((RIM, channels), F32), stored((8, channels), F32),
             stored((heads, rows), F32), stored((8, 128), F32),
         ],
-        scratch_shapes=[pltpu.VMEM((3, heads, rows), F32)],
+        scratch_shapes=[pltpu.VMEM((2, heads, rows), F32)],
         compiler_params=params,
         cost_estimate=cost(10),
         name="x_part",
-    )(states, *from_hbm(xa, slope, y_loc, du_loc, xt, dyt, rimt, taps, head_rows, bctok))
-
-    spill_x = passed_along(spill, -1)
-    grad_x = pl.pallas_call(
+    )(
+        states,
+        *from_hbm(xa, y_loc, g_loc, ends, xt, dyt, rim, conv_x, head_rows, bctok, red_loc),
+    )
+
+    vmem = pl.BlockSpec(memory_space=pltpu.VMEM)
+    width = channels + 256 + 128
+    sums, own_bc, spills = pl.pallas_call(
+        pack_kernel,
+        in_specs=[vmem] * 4,
+        out_specs=[vmem] * 3,
+        out_shape=[
+            shaped((8, width), F32), shaped((share, 256), F32),
+            shaped((RIM, channels + 256), F32),
+        ],
+        compiler_params=params,
+        cost_estimate=cost(1),
+        name="pack_sums",
+    )(got_bc, *from_hbm(gw, gh, spill))
+    parts = summed_over_ctx(sums)
+    spills = passed_along(spills, -1)
+    grad_x, grad_bc = pl.pallas_call(
         patch_kernel,
         grid=(1,),
         in_specs=[
-            pl.BlockSpec(memory_space=pl.ANY), whole((RIM, channels)), whole((RIM, channels)),
-        ],
-        out_specs=pl.BlockSpec((RIM, channels), lambda i: (rows // RIM - 1, 0)),
-        out_shape=stored((rows, channels), BF16),
+            pl.BlockSpec(memory_space=pl.ANY), whole((RIM, channels)), whole((share, 256)),
+            whole((RIM, channels + 256)),
+        ],
+        out_specs=[
+            pl.BlockSpec((RIM, channels), lambda i: (rows // RIM - 1, 0)), whole((share, 256)),
+        ],
+        out_shape=[stored((rows, channels), BF16), stored((share, 256), F32)],
         input_output_aliases={0: 0},
         compiler_params=params,
         cost_estimate=cost(1),
         name="last_rows",
-    )(*from_hbm(gx, last), spill_x)
-
-    vmem = pl.BlockSpec(memory_space=pltpu.VMEM)
-    width = channels + 256 + 128
-    sums, own_bc, spill_bc = pl.pallas_call(
-        pack_kernel,
-        in_specs=[vmem] * 3,
-        out_specs=[vmem] * 3,
-        out_shape=[shaped((8, width), F32), shaped((share, 256), F32), shaped((8, 256), F32)],
-        compiler_params=params,
-        cost_estimate=cost(1),
-        name="pack_sums",
-    )(got_bc, *from_hbm(gw, gh))
-    spill_bc = passed_along(spill_bc, -1)
-    parts = summed_over_ctx(sums)
+    )(*from_hbm(gx, last), own_bc, spills)
     grad_wx, grad_wbc, grad_heads = pl.pallas_call(
         finish_kernel,
         in_specs=[vmem] * 4,
@@ -623,8 +668,6 @@
         cost_estimate=cost(1),
         name="finish_sums",
     )(*parts)
-    is_last = lax.axis_index("head") == shares - 1
-    grad_bc = own_bc + jnp.pad(jnp.where(is_last, spill_bc, 0.0), ((share - 8, 0), (0, 0)))
     return ssd_out, grad_x, grad_bc, grad_dt.T, grad_wx, grad_wbc, grad_heads
 
 

time: 103 us -> 93.1 us (0.904)
  the two profiles are of different devices: /device:TPU:32 before, /device:TPU:1 now
where the time goes in v3:
time: 93.1 us; the launch traced here: 91.5 us
  Pallas kernels  36.4 us (39%)
  starting transfers between devices  34.7 us (37%)
  waiting for transfers between devices  17.9 us (19%)
  local copies, waits for them, and re-layouts  1.63 us (2%)
    all_to_all x1, starting transfers between devices, local(): got = lax.all_to_all(pay, 'ctx', 0, 0, tiled=True)  8.32 us
    all_to_all x1, starting transfers between devices, local(): got_bc = lax.all_to_all(pay_bc, 'head', 0, 0, tiled=True)  8.18 us
    pallas_call x1, Pallas kernels, local(): pl.pallas_call(x_kernel, grid=(steps,), in_specs=[state_spec, by_channel,...  7.55 us
    ppermute x2, starting transfers between devices, passed_along(): return lax.ppermute(value, 'ctx', pairs)  7.39 us
    pallas_call x1, Pallas kernels, local(): pl.pallas_call(state_kernel, grid=(steps,), in_specs=[columns(rows), colu...  7.16 us
    pallas_call x1, Pallas kernels, local(): pl.pallas_call(slope_kernel, grid=(steps,), in_specs=[columns(rows), colu...  6.68 us
    pallas_call x1, Pallas kernels, local(): pl.pallas_call(block_kernel, grid=(steps,), in_specs=[by_channel, columns...  6.26 us
    all_to_all x1, waiting for transfers between devices, local(): got = lax.all_to_all(pay, 'ctx', 0, 0, tiled=True)  5.57 us
  transfers between devices with their start and end apart: 12, of which 10 were waited for; matrix products, arithmetic and copies ran while one was open for 0% of the time, Pallas kernels for 24%

profile of v3, /device:TPU:1, one launch (start us, length us, event | category | flops | bytes accessed | tf_op | source)
XLA Modules:
  0.0 91.5 jit_solution(1312886695006832396)
XLA Ops:
  0.7 0.7 slice-done
  1.4 4.5 %collective-permute-start = (bf16[16,1280]{1,0:T(8,128)(2,1)S(1)}, bf16[16,1280]{1,0:T(8,128)(2,1)S(1)}, u32[]{:S(2)}, u32[]{:S(2)}) collective-permute-start(bf16[16,1280]{1,0:T(8,128)(2,1)S(1)} %pad_maximum_fusion), channel_id=1, source_target_pairs={{0,8},{8,16},{16,24},{24,32},{32,40},{40,48},{48,56},{56,64},{64,7... | collective-permute-start | bytes 122888 | tf_op jit(solution)/shard_map/ppermute | solution.py:461
  5.9 0.1 pad_dynamic-slice_fusion
  6.1 0.7 copy-done.2
  6.8 0.2 collective-permute-done.rim_ref.rimbc_ref
  7.0 7.2 %states.1 = (bf16[32,72,128]{2,1,0:T(8,128)(2,1)}, bf16[1024,256]{1,0:T(8,128)(2,1)}, bf16[1024,256]{1,0:T(8,128)(2,1)}, f32[8,16,256]{2,1,0:T(8,128)}, bf16[256...) custom-call(bf16[256,1024]{1,0:T(8,128)(2,1)} %x_ref.3, bf16[16,1280]{1,0:T(8,128)(2,1)S(1)} %collective-permute-done.rim_ref.rimbc_ref, ...), custom_call_target="tpu_custom_call" | custom-call | flops 700000000 | bytes 21000000 | tf_op jit(solution)/shard_map/states/pallas_call | solution.py:511
  14.2 8.3 %all-to-all-start = ((bf16[32,72,128]{2,1,0:T(8,128)(2,1)}), bf16[32,72,128]{2,1,0:T(8,128)(2,1)S(1)}, u32[]{:S(2)}, u32[]{:S(2)}) async-start(bf16[32,72,128]{2,1,0:T(8,128)(2,1)} %get-tuple-element.41), calls=%async_computation | async-start | bytes 1179648 | tf_op jit(solution)/shard_map/all_to_all | solution.py:535
  22.5 6.7 %slopes.1 = (bf16[1024,256]{1,0:T(8,128)(2,1)}, f32[1024,256]{1,0:T(8,128)}, bf16[1024,256]{1,0:T(8,128)(2,1)}, bf16[1024,256]{1,0:T(8,128)(2,1)}, bf16[256,256]{1,0:T(8,128)(2,1)}, /*index=5*/f32[256,256]{1,0:T(8,128)}) custom-call(bf16[256,1024]{1,0:T(8,128)(2,1)} %x_ref.3, bf16[16,1280]{1,0:T(8,128)(2,1)} %copy-done, f32[4,1024]{1,0:T(4,128)} %wx_ref.5, ...), custom_call_target="tpu_custom_call" | custom-call | flops 600000000 | bytes 18000000 | tf_op jit(solution)/shard_map/slopes/pallas_call | solution.py:537
  29.2 5.6 %all-to-all-done.in_ref = bf16[32,72,128]{2,1,0:T(8,128)(2,1)S(1)} async-done(((bf16[32,72,128]{2,1,0:T(8,128)(2,1)}), bf16[32,72,128]{2,1,0:T(8,128)(2,1)S(1)}, u32[]{:S(2)}, u32[]{:S(2)}) %all-to-all-start) | async-done | bytes 589856 | tf_op jit(solution)/shard_map/all_to_all | solution.py:535
  34.7 1.0 %state_scan.1 = bf16[32,64,128]{2,1,0:T(8,128)(2,1)} custom-call(bf16[32,72,128]{2,1,0:T(8,128)(2,1)S(1)} %all-to-all-done.in_ref), custom_call_target="tpu_custom_call" | custom-call | flops 100000000 | bytes 3000000 | tf_op jit(solution)/shard_map/state_scan/pallas_call | solution.py:555
  35.7 4.1 %all-to-all-start.1 = ((bf16[32,64,128]{2,1,0:T(8,128)(2,1)}), bf16[32,64,128]{2,1,0:T(8,128)(2,1)S(1)}, u32[]{:S(2)}, u32[]{:S(2)}) async-start(bf16[32,64,128]{2,1,0:T(8,128)(2,1)} %state_scan.1), calls=%async_computation.1 | async-start | bytes 1048576 | tf_op jit(solution)/shard_map/all_to_all | solution.py:564
  39.8 6.3 %in_block.1 = (f32[1024,256]{1,0:T(8,128)}, f32[1024,256]{1,0:T(8,128)}, f32[1024,256]{1,0:T(8,128)}, f32[3,16,256]{2,1,0:T(8,128)}, f32[256,256]{1,0:T(8,128)}) custom-call(bf16[1024,256]{1,0:T(8,128)(2,1)} %get-tuple-element.42.xa_ref, bf16[256,1024]{1,0:T(8,128)(2,1)} %gy_ref.3, bf16[1024,256]{1,0:T(8,128)(2,1)} %get-tuple-element.43.dyt_ref, ...), custom_call_target="tpu_custom_call" | custom-call | flops 800000000 | bytes 24000000 | tf_op jit(solution)/shard_map/in_block/pallas_call | solution.py:566
  46.0 5.4 %all-to-all-done.1.state_ref = bf16[32,64,128]{2,1,0:T(8,128)(2,1)S(1)} async-done(((bf16[32,64,128]{2,1,0:T(8,128)(2,1)}), bf16[32,64,128]{2,1,0:T(8,128)(2,1)S(1)}, u32[]{:S(2)}, u32[]{:S(2)}) %all-to-all-start.1) | async-done | bytes 524320 | tf_op jit(solution)/shard_map/all_to_all | solution.py:564
  51.4 4.8 %bc_part.1 = bf16[8,48,256]{2,1,0:T(8,128)(2,1)} custom-call(bf16[32,64,128]{2,1,0:T(8,128)(2,1)S(1)} %all-to-all-done.1.state_ref, bf16[1024,256]{1,0:T(8,128)(2,1)} %get-tuple-element.58.eu_ref, bf16[1024,256]{1,0:T(8,128)(2,1)} %get-tuple-element.59.cdy_ref, f32[256,256]{1,0:T(8,128)} %get-tuple-element.60.dbc_ref, ...), custom_call_target="tpu_custom_call" | custom-call | flops 400000000 | bytes 12000000 | tf_op jit(solution)/shard_map/bc_part/pallas_call | solution.py:589
  56.3 8.2 %all-to-all-start.2 = ((bf16[8,48,256]{2,1,0:T(8,128)(2,1)}), bf16[8,48,256]{2,1,0:T(8,128)(2,1)S(1)}, u32[]{:S(2)}, u32[]{:S(2)}) async-start(bf16[8,48,256]{2,1,0:T(8,128)(2,1)} %bc_part.1), calls=%async_computation.2 | async-start | bytes 393216 | tf_op jit(solution)/shard_map/all_to_all | solution.py:603
  64.4 7.6 %x_part.1 = (bf16[256,1024]{1,0:T(8,128)(2,1)}, bf16[256,1024]{1,0:T(8,128)(2,1)}, f32[16,1024]{1,0:T(8,128)}, f32[16,1024]{1,0:T(8,128)}, f32[8,1024]{1,0:T(8,1...) custom-call(bf16[32,64,128]{2,1,0:T(8,128)(2,1)S(1)} %all-to-all-done.1.state_ref, bf16[1024,256]{1,0:T(8,128)(2,1)} %get-tuple-element.42.xa_ref, ...), custom_call_target="tpu_custom_call" | custom-call | flops 1000000000 | bytes 30000000 | tf_op jit(solution)/shard_map/x_part/pallas_call | solution.py:605
  72.0 1.8 %all-to-all-done.2.got_ref = bf16[8,48,256]{2,1,0:T(8,128)(2,1)S(1)} async-done(((bf16[8,48,256]{2,1,0:T(8,128)(2,1)}), bf16[8,48,256]{2,1,0:T(8,128)(2,1)S(1)}, u32[]{:S(2)}, u32[]{:S(2)}) %all-to-all-start.2) | async-done | bytes 196640 | tf_op jit(solution)/shard_map/all_to_all | solution.py:603
  73.8 0.9 pack_sums.1
  74.7 2.2 %collective-permute-start.2 = (f32[8,1408]{1,0:T(8,128)S(1)}, f32[8,1408]{1,0:T(8,128)S(1)}, u32[]{:S(2)}, u32[]{:S(2)}) collective-permute-start(f32[8,1408]{1,0:T(8,128)S(1)} %get-tuple-element.71), channel_id=1, source_target_pairs={{0,8},{8,0},{16,24},{24,16},{32,40},{40,32},{48,56},{56,48},{64,72... | collective-permute-start | bytes 135176 | tf_op jit(solution)/shard_map/ppermute | solution.py:477
  76.9 0.9 collective-permute-done.2
  77.8 1.3 %collective-permute-start.5 = (f32[8,1408]{1,0:T(8,128)S(1)}, f32[8,1408]{1,0:T(8,128)S(1)}, u32[]{:S(2)}, u32[]{:S(2)}) collective-permute-start(f32[8,1408]{1,0:T(8,128)S(1)} %add.18), channel_id=1, source_target_pairs={{0,48},{8,56},{16,0},{24,8},{32,16},{40,24},{48,32},{56,40},{64,11... | collective-permute-start | bytes 135176 | tf_op jit(solution)/shard_map/ppermute | solution.py:473
  79.1 1.0 %collective-permute-start.4 = (f32[8,1408]{1,0:T(8,128)S(1)}, f32[8,1408]{1,0:T(8,128)S(1)}, u32[]{:S(2)}, u32[]{:S(2)}) collective-permute-start(f32[8,1408]{1,0:T(8,128)S(1)} %add.18), channel_id=1, source_target_pairs={{0,32},{8,40},{16,48},{24,56},{32,0},{40,8},{48,16},{56,24},{64,96... | collective-permute-start | bytes 135176 | tf_op jit(solution)/shard_map/ppermute | solution.py:473
  80.1 2.9 %collective-permute-start.1 = (f32[16,1280]{1,0:T(8,128)S(1)}, f32[16,1280]{1,0:T(8,128)S(1)}, u32[]{:S(2)}, u32[]{:S(2)}) collective-permute-start(f32[16,1280]{1,0:T(8,128)S(1)} %get-tuple-element.67), channel_id=1, source_target_pairs={{8,0},{16,8},{24,16},{32,24},{40,32},{48,40},{56,48},{64,56},{72,6... | collective-permute-start | bytes 245768 | tf_op jit(solution)/shard_map/ppermute | solution.py:461
  83.0 0.5 collective-permute-done.4
  83.5 1.0 %collective-permute-done.3 = f32[8,1408]{1,0:T(8,128)S(1)} collective-permute-done((f32[8,1408]{1,0:T(8,128)S(1)}, f32[8,1408]{1,0:T(8,128)S(1)}, u32[]{:S(2)}, u32[]{:S(2)}) %collective-permute-start.3) | collective-permute-done | bytes 45088 | tf_op jit(solution)/shard_map/ppermute | solution.py:473
  84.5 0.9 %collective-permute-start.8 = (f32[8,1408]{1,0:T(8,128)S(1)}, f32[8,1408]{1,0:T(8,128)S(1)}, u32[]{:S(2)}, u32[]{:S(2)}) collective-permute-start(f32[8,1408]{1,0:T(8,128)S(1)} %add_add_fusion.a_ref), channel_id=1, source_target_pairs={{0,192},{8,200},{16,208},{24,216},{32,224},{40,232},{48,240},{56,2... | collective-permute-start | bytes 135176 | tf_op jit(solution)/shard_map/ppermute | solution.py:473
  85.4 1.3 %collective-permute-start.7 = (f32[8,1408]{1,0:T(8,128)S(1)}, f32[8,1408]{1,0:T(8,128)S(1)}, u32[]{:S(2)}, u32[]{:S(2)}) collective-permute-start(f32[8,1408]{1,0:T(8,128)S(1)} %add_add_fusion.a_ref), channel_id=1, source_target_pairs={{0,128},{8,136},{16,144},{24,152},{32,160},{40,168},{48,176},{56,1... | collective-permute-start | bytes 135176 | tf_op jit(solution)/shard_map/ppermute | solution.py:473
  86.7 0.1 collective-permute-done.1.spill_ref
  86.9 1.5 %last_rows.1 = (bf16[256,1024]{1,0:T(8,128)(2,1)}, f32[32,256]{1,0:T(8,128)}) custom-call(bf16[256,1024]{1,0:T(8,128)(2,1)} %get-tuple-element.56.gx_ref, f32[16,1024]{1,0:T(8,128)} %get-tuple-element.57.last_ref, f32[32,256]{1,0:T(8,128)S(1)} %get-tuple-element.66.own_ref, ...), custom_call_target="tpu_custom_call", output_to_operand_aliasing={{0}: (0, {})} | custom-call | flops 100000000 | bytes 3000000 | tf_op jit(solution)/shard_map/last_rows/pallas_call | solution.py:646
  88.3 1.5 %collective-permute-done.7.c_ref = f32[8,1408]{1,0:T(8,128)S(1)} collective-permute-done((f32[8,1408]{1,0:T(8,128)S(1)}, f32[8,1408]{1,0:T(8,128)S(1)}, u32[]{:S(2)}, u32[]{:S(2)}) %collective-permute-start.7) | collective-permute-done | bytes 45088 | tf_op jit(solution)/shard_map/ppermute | solution.py:473
  89.8 1.0 %collective-permute-done.6.b_ref = f32[8,1408]{1,0:T(8,128)S(1)} collective-permute-done((f32[8,1408]{1,0:T(8,128)S(1)}, f32[8,1408]{1,0:T(8,128)S(1)}, u32[]{:S(2)}, u32[]{:S(2)}) %collective-permute-start.6) | collective-permute-done | bytes 45088 | tf_op jit(solution)/shard_map/ppermute | solution.py:473
  90.9 0.6 finish_sums.1
  (23 shorter events, 0.2 us)
Async XLA Ops:
  0.6 0.8 slice-start
  0.6 0.8 slice-start.1
  1.4 4.5 %copy-start.1 = (s32[8192]{0:T(1024)S(1)}, s32[8192]{0:T(1024)}, u32[]{:S(2)}) copy-start(s32[8192]{0:T(1024)} %param.18) | copy-start | bytes 98308
  1.4 5.6 %collective-permute-start = (bf16[16,1280]{1,0:T(8,128)(2,1)S(1)}, bf16[16,1280]{1,0:T(8,128)(2,1)S(1)}, u32[]{:S(2)}, u32[]{:S(2)}) collective-permute-start(bf16[16,1280]{1,0:T(8,128)(2,1)S(1)} %pad_maximum_fusion), channel_id=1, source_target_pairs={{0,8},{8,16},{16,24},{24,32},{32,40},{40,48},{48,56},{56,64},{64,7... | collective-permute-start | bytes 122888 | tf_op jit(solution)/shard_map/ppermute | solution.py:461
  6.1 0.7 copy-start.2
  6.1 0.7 copy-start.3
  6.1 0.7 copy-start.4
  7.0 7.2 %copy-start = (bf16[16,1280]{1,0:T(8,128)(2,1)}, bf16[16,1280]{1,0:T(8,128)(2,1)S(1)}, u32[]{:S(2)}) copy-start(bf16[16,1280]{1,0:T(8,128)(2,1)S(1)} %collective-permute-done.rim_ref.rimbc_ref) | copy-start | bytes 122884
  14.2 20.6 %all-to-all-start = ((bf16[32,72,128]{2,1,0:T(8,128)(2,1)}), bf16[32,72,128]{2,1,0:T(8,128)(2,1)S(1)}, u32[]{:S(2)}, u32[]{:S(2)}) async-start(bf16[32,72,128]{2,1,0:T(8,128)(2,1)} %get-tuple-element.41), calls=%async_computation | async-start | bytes 1179648 | tf_op jit(solution)/shard_map/all_to_all | solution.py:535
  35.7 15.7 %all-to-all-start.1 = ((bf16[32,64,128]{2,1,0:T(8,128)(2,1)}), bf16[32,64,128]{2,1,0:T(8,128)(2,1)S(1)}, u32[]{:S(2)}, u32[]{:S(2)}) async-start(bf16[32,64,128]{2,1,0:T(8,128)(2,1)} %state_scan.1), calls=%async_computation.1 | async-start | bytes 1048576 | tf_op jit(solution)/shard_map/all_to_all | solution.py:564
  56.3 17.5 %all-to-all-start.2 = ((bf16[8,48,256]{2,1,0:T(8,128)(2,1)}), bf16[8,48,256]{2,1,0:T(8,128)(2,1)S(1)}, u32[]{:S(2)}, u32[]{:S(2)}) async-start(bf16[8,48,256]{2,1,0:T(8,128)(2,1)} %bc_part.1), calls=%async_computation.2 | async-start | bytes 393216 | tf_op jit(solution)/shard_map/all_to_all | solution.py:603
  74.7 3.1 %collective-permute-start.2 = (f32[8,1408]{1,0:T(8,128)S(1)}, f32[8,1408]{1,0:T(8,128)S(1)}, u32[]{:S(2)}, u32[]{:S(2)}) collective-permute-start(f32[8,1408]{1,0:T(8,128)S(1)} %get-tuple-element.71), channel_id=1, source_target_pairs={{0,8},{8,0},{16,24},{24,16},{32,40},{40,32},{48,56},{56,48},{64,72... | collective-permute-start | bytes 135176 | tf_op jit(solution)/shard_map/ppermute | solution.py:477
  77.8 5.2 %collective-permute-start.5 = (f32[8,1408]{1,0:T(8,128)S(1)}, f32[8,1408]{1,0:T(8,128)S(1)}, u32[]{:S(2)}, u32[]{:S(2)}) collective-permute-start(f32[8,1408]{1,0:T(8,128)S(1)} %add.18), channel_id=1, source_target_pairs={{0,48},{8,56},{16,0},{24,8},{32,16},{40,24},{48,32},{56,40},{64,11... | collective-permute-start | bytes 135176 | tf_op jit(solution)/shard_map/ppermute | solution.py:473
  79.1 4.4 %collective-permute-start.4 = (f32[8,1408]{1,0:T(8,128)S(1)}, f32[8,1408]{1,0:T(8,128)S(1)}, u32[]{:S(2)}, u32[]{:S(2)}) collective-permute-start(f32[8,1408]{1,0:T(8,128)S(1)} %add.18), channel_id=1, source_target_pairs={{0,32},{8,40},{16,48},{24,56},{32,0},{40,8},{48,16},{56,24},{64,96... | collective-permute-start | bytes 135176 | tf_op jit(solution)/shard_map/ppermute | solution.py:473
  80.1 4.4 %collective-permute-start.3 = (f32[8,1408]{1,0:T(8,128)S(1)}, f32[8,1408]{1,0:T(8,128)S(1)}, u32[]{:S(2)}, u32[]{:S(2)}) collective-permute-start(f32[8,1408]{1,0:T(8,128)S(1)} %add.18), channel_id=1, source_target_pairs={{0,16},{8,24},{16,32},{24,40},{32,48},{40,56},{48,0},{56,8},{64,80... | collective-permute-start | bytes 135176 | tf_op jit(solution)/shard_map/ppermute | solution.py:473
  80.1 6.8 %collective-permute-start.1 = (f32[16,1280]{1,0:T(8,128)S(1)}, f32[16,1280]{1,0:T(8,128)S(1)}, u32[]{:S(2)}, u32[]{:S(2)}) collective-permute-start(f32[16,1280]{1,0:T(8,128)S(1)} %get-tuple-element.67), channel_id=1, source_target_pairs={{8,0},{16,8},{24,16},{32,24},{40,32},{48,40},{56,48},{64,56},{72,6... | collective-permute-start | bytes 245768 | tf_op jit(solution)/shard_map/ppermute | solution.py:461
  84.5 3.8 %collective-permute-start.8 = (f32[8,1408]{1,0:T(8,128)S(1)}, f32[8,1408]{1,0:T(8,128)S(1)}, u32[]{:S(2)}, u32[]{:S(2)}) collective-permute-start(f32[8,1408]{1,0:T(8,128)S(1)} %add_add_fusion.a_ref), channel_id=1, source_target_pairs={{0,192},{8,200},{16,208},{24,216},{32,224},{40,232},{48,240},{56,2... | collective-permute-start | bytes 135176 | tf_op jit(solution)/shard_map/ppermute | solution.py:473
  85.4 4.4 %collective-permute-start.7 = (f32[8,1408]{1,0:T(8,128)S(1)}, f32[8,1408]{1,0:T(8,128)S(1)}, u32[]{:S(2)}, u32[]{:S(2)}) collective-permute-start(f32[8,1408]{1,0:T(8,128)S(1)} %add_add_fusion.a_ref), channel_id=1, source_target_pairs={{0,128},{8,136},{16,144},{24,152},{32,160},{40,168},{48,176},{56,1... | collective-permute-start | bytes 135176 | tf_op jit(solution)/shard_map/ppermute | solution.py:473
  86.7 4.1 %collective-permute-start.6 = (f32[8,1408]{1,0:T(8,128)S(1)}, f32[8,1408]{1,0:T(8,128)S(1)}, u32[]{:S(2)}, u32[]{:S(2)}) collective-permute-start(f32[8,1408]{1,0:T(8,128)S(1)} %add_add_fusion.a_ref), channel_id=1, source_target_pairs={{0,64},{8,72},{16,80},{24,88},{32,96},{40,104},{48,112},{56,120},{... | collective-permute-start | bytes 135176 | tf_op jit(solution)/shard_map/ppermute | solution.py:473

commit v4 on v3

v4 whole, which is shorter than its diff:
```python
import jax
import jax.numpy as jnp
from jax import lax
from jax.experimental import pallas as pl
from jax.experimental.pallas import tpu as pltpu
from jax.sharding import PartitionSpec as P

F32 = jnp.float32
BF16 = jnp.bfloat16

BLK = 256
HD = 64
NS = 128
RIM = 16
PER = BLK // HD
VMEM = 24 * 1024 * 1024

DT, CUMUL, CARRY, END, SIG, SKIP, RATE, MASK = range(8)


def mm(a, b):
    return lax.dot_general(a, b, (((1,), (0,)), ((), ())), preferred_element_type=F32)


def mm_nt(a, b):
    return lax.dot_general(a, b, (((1,), (1,)), ((), ())), preferred_element_type=F32)


def split(value, count):
    parts = []
    for _ in range(count):
        part = value.astype(BF16)
        parts.append(part)
        value = value - part.astype(F32)
    return parts


def pick_nt(pick, value, count):
    return sum(mm_nt(pick, part) for part in split(value, count))


def pick_right(value, pick, count):
    return sum(mm(part, pick) for part in split(value, count))


def iota(shape, dim):
    return lax.broadcasted_iota(jnp.int32, shape, dim)


def eye(n, dtype):
    return (iota((n, n), 0) == iota((n, n), 1)).astype(dtype)


def conv_own(raw, taps, masks):
    lane = iota((raw.shape[0], 128), 1)
    total = taps[:, 3:4] * raw
    for j in range(1, 4):
        rolled = pltpu.roll(raw, j, 1)
        shifted = jnp.concatenate(
            [jnp.where(lane < j, 0.0, rolled[:, :128]), rolled[:, 128:]], axis=1
        )
        total = total + shifted * (taps[:, 3 - j : 4 - j] * masks[3 - j])
    return total


def conv_rim(rim, taps, masks):
    lane = iota(rim.shape, 1)
    total = jnp.zeros(rim.shape, F32)
    for j in range(1, 4):
        before = jnp.where(lane < j, pltpu.roll(rim, j, 1), 0.0)
        total = total + before * (taps[:, 3 - j : 4 - j] * masks[3 - j][:, :128])
    return total


def conv_back(g, raw, rim, taps, masks):
    lane = iota((g.shape[0], 128), 1)
    grad = taps[:, 3:4] * g
    spill = jnp.zeros((g.shape[0], 128), F32)
    product = g * raw
    products = [None, None, None, product[:, :128] + product[:, 128:]]
    for j in range(1, 4):
        masked = g * masks[3 - j]
        rolled = pltpu.roll(masked, g.shape[1] - j, 1)
        wrapped = lane >= 128 - j
        first = rolled[:, :128]
        second = jnp.where(wrapped, 0.0, rolled[:, 128:])
        outer = jnp.where(wrapped, rolled[:, 128:], 0.0)
        tap = taps[:, 3 - j : 4 - j]
        grad = grad + tap * jnp.concatenate([first, second], axis=1)
        spill = spill + tap * outer
        products[3 - j] = first * raw[:, :128] + second * raw[:, 128:] + outer * rim
    chosen = (iota((512, 128), 0) // 128 == iota((512, 128), 1)).astype(BF16)
    sums = pick_right(jnp.concatenate(products, axis=1), chosen, 2)
    moved = pltpu.roll(spill, 128 - RIM, 1)
    sides = jnp.where(lane >= 128 - RIM, grad[:, 128:], jnp.where(lane >= 96, moved, sums))
    return grad, sides


def wide_rim(rim):
    return jnp.concatenate([jnp.zeros((128 - RIM, rim.shape[1]), BF16), rim], axis=0)


def masks_of(rows_ref):
    return [rows_ref[MASK, k : k + 1, :] for k in range(4)]


def head_row(rows_ref, plane, head):
    return rows_ref[plane, pl.ds(head, 1), :]


def taps_of(w):
    padded = jnp.concatenate([w, jnp.zeros((124, BLK), F32)], axis=0)
    return jnp.transpose(padded)


def conv_all(raw_ref, rim_ref, taps, masks):
    ident = eye(BLK, BF16)
    raw = mm_nt(ident, raw_ref[...])
    rim = mm_nt(ident, wide_rim(rim_ref[...]))
    pre = conv_own(raw, taps, masks)
    pre = jnp.concatenate([pre[:, :128] + conv_rim(rim, taps, masks), pre[:, 128:]], axis=1)
    return raw, rim, pre


def with_taps(rim, taps):
    return jnp.where(iota(rim.shape, 1) < 4, taps, rim)


def sigmoid(value):
    return 1.0 / (1.0 + jnp.exp(-value))


def rim_kernel(x_ref, bc_ref, out_ref, sems):
    rows, width = x_ref.shape
    copies = [
        pltpu.make_async_copy(
            x_ref.at[pl.ds(rows - RIM, RIM), :], out_ref.at[:, pl.ds(0, width)], sems.at[0]
        ),
        pltpu.make_async_copy(
            bc_ref.at[pl.ds(rows - RIM, RIM), :],
            out_ref.at[:, pl.ds(width, bc_ref.shape[1])],
            sems.at[1],
        ),
    ]
    for copy in copies:
        copy.start()
    for copy in copies:
        copy.wait()


def head_rows_of(rows_ref, seg_ref, rate_ref, bias_ref, skip_ref, dt_ref):
    here = lax.axis_index("ctx")
    own = [seg_ref[pl.ds(2 * here + half, 1), :] for half in range(2)]
    target = jnp.concatenate(own, axis=1).astype(F32)
    before = seg_ref[pl.ds(jnp.maximum(2 * here - 1, 0), 1), :].astype(F32)
    before = jnp.where(here == 0, -1.0, before)
    lane = iota((1, 128), 1)
    masks = []
    for j in (3, 2, 1):
        rolled = pltpu.roll(target, j, 1)
        first = jnp.where(lane < j, pltpu.roll(before, j, 1), rolled[:, :128])
        shifted = jnp.concatenate([first, rolled[:, 128:]], axis=1)
        masks.append((shifted == target).astype(F32))
    rows_ref[MASK] = jnp.concatenate(
        masks + [jnp.ones((1, BLK), F32), target, jnp.zeros((11, BLK), F32)], axis=0
    )
    heads = dt_ref.shape[0]
    values = jnp.concatenate(
        [rate_ref[...], bias_ref[...], skip_ref[...], jnp.zeros((5, heads), F32)], axis=0
    )
    per_head = pick_nt(eye(heads, BF16), values, 3)
    rate = jnp.exp(per_head[:, 0:1])
    pre = dt_ref[...] + per_head[:, 1:2]
    dt = jnp.maximum(pre, 0.0) + jnp.log1p(jnp.exp(-jnp.abs(pre)))
    upto = (iota((BLK, BLK), 0) <= iota((BLK, BLK), 1)).astype(BF16)
    cumul = pick_right(-rate * dt, upto, 3)
    keep = (target == before[:, 127:]).astype(F32)
    same_end = target == target[:, BLK - 1 :]
    rows_ref[DT] = dt
    rows_ref[CUMUL] = cumul
    rows_ref[CARRY] = keep * jnp.exp(cumul)
    rows_ref[END] = jnp.exp(jnp.where(same_end, cumul[:, BLK - 1 :] - cumul, -jnp.inf))
    rows_ref[SIG] = sigmoid(pre)
    rows_ref[SKIP] = jnp.broadcast_to(per_head[:, 2:3], (heads, BLK))
    rows_ref[RATE] = jnp.broadcast_to(rate, (heads, BLK))


def state_kernel(
    x_ref, rim_ref, gy_ref, wx_ref, bc_ref, rimbc_ref, wbc_ref, seg_ref, rate_ref, bias_ref,
    skip_ref, dt_ref,
    pay_ref, rows_ref, bctok_ref,
):
    step = pl.program_id(0)
    ident = eye(BLK, BF16)

    @pl.when(step == 0)
    def _():
        head_rows_of(rows_ref, seg_ref, rate_ref, bias_ref, skip_ref, dt_ref)
        _, _, pre = conv_all(bc_ref, rimbc_ref, taps_of(wbc_ref[...]), masks_of(rows_ref))
        bctok_ref[...] = mm_nt(ident, (pre * sigmoid(pre)).astype(BF16)).astype(BF16)

    _, _, pre = conv_all(x_ref, rim_ref, taps_of(wx_ref[...]), masks_of(rows_ref))
    act = (pre * sigmoid(pre)).astype(BF16).astype(F32)
    dy = mm_nt(ident, gy_ref[...])
    ends, carries = [], []
    for k in range(PER):
        head = step * PER + k
        lo, hi = k * HD, (k + 1) * HD
        carry = head_row(rows_ref, CARRY, head)
        weight = head_row(rows_ref, END, head) * head_row(rows_ref, DT, head)
        ends.append((weight * act[lo:hi]).astype(BF16))
        carries.append((carry * dy[lo:hi]).astype(BF16))
        parts = split(carry[:, BLK - 1 :], 3)
        which = iota((8, NS), 0)
        through = jnp.where(
            which == 0, parts[0].astype(F32),
            jnp.where(which == 1, parts[1].astype(F32), parts[2].astype(F32)),
        ).astype(BF16)
        pay_ref[2 * k, 64:72, :] = through
        pay_ref[2 * k + 1, 64:72, :] = through
    state = mm(jnp.concatenate(ends, axis=0), bctok_ref[:, :NS]).astype(BF16)
    back = mm(jnp.concatenate(carries, axis=0), bctok_ref[:, NS:]).astype(BF16)
    for j in range(2 * PER):
        pay_ref[j, 0:32, :] = state[j * 32 : j * 32 + 32]
        pay_ref[j, 32:64, :] = back[j * 32 : j * 32 + 32]


def slope_kernel(
    x_ref, rim_ref, gy_ref, wx_ref, bc_ref, rimbc_ref, wbc_ref, rows_ref,
    low_ref, slope_ref, scaled_ref, sides_ref, bclow_ref, bcslope_ref, bcsides_ref,
):
    step = pl.program_id(0)
    masks = masks_of(rows_ref)

    @pl.when(step == 0)
    def _():
        taps = taps_of(wbc_ref[...])
        raw, rim, pre = conv_all(bc_ref, rimbc_ref, taps, masks)
        bcsides_ref[...] = with_taps(rim, taps)
        sig = sigmoid(pre)
        bclow_ref[0] = raw.astype(BF16)
        bclow_ref[1] = (pre * sig).astype(BF16)
        bcslope_ref[...] = sig * (1.0 + pre * (1.0 - sig))

    taps = taps_of(wx_ref[...])
    raw, rim, pre = conv_all(x_ref, rim_ref, taps, masks)
    sides_ref[...] = with_taps(rim, taps)
    sig = sigmoid(pre)
    slope_ref[...] = sig * (1.0 + pre * (1.0 - sig))
    low = (pre * sig).astype(BF16)
    dy = mm_nt(eye(BLK, BF16), gy_ref[...])
    low_ref[0] = low
    low_ref[1] = dy.astype(BF16)
    low_ref[2] = raw.astype(BF16)
    act = low.astype(F32)
    for k in range(PER):
        head = step * PER + k
        lo, hi = k * HD, (k + 1) * HD
        weight = head_row(rows_ref, END, head) * head_row(rows_ref, DT, head)
        scaled_ref[0, lo:hi, :] = (weight * act[lo:hi]).astype(BF16)
        scaled_ref[1, lo:hi, :] = (head_row(rows_ref, CARRY, head) * dy[lo:hi]).astype(BF16)


def block_kernel(
    low_ref, gy_ref, rows_ref, bctok_ref, bclow_ref, slope_ref,
    high_ref, red_ref, dbc_ref,
    scores_ref, link_ref, acol_ref, dg_ref, yt_ref, du_ref,
):
    step = pl.program_id(0)

    @pl.when(step == 0)
    def _():
        ident = eye(BLK, BF16)
        scores_ref[...] = mm_nt(bctok_ref[:, NS:], bctok_ref[:, :NS])
        seg_row = rows_ref[MASK, 4:5, :]
        seg_col = mm_nt(ident, rows_ref[MASK].astype(BF16))[:, 4:5]
        later = iota((BLK, BLK), 0) >= iota((BLK, BLK), 1)
        linked = jnp.logical_and(later, seg_col == seg_row)
        link_ref[...] = jnp.where(linked, 0.0, -jnp.inf)
        dg_ref[...] = jnp.zeros_like(dg_ref)
        cumul = pick_nt(ident, rows_ref[CUMUL], 3)
        for at in range(acol_ref.shape[0]):
            acol_ref[at] = cumul[:, at * PER : (at + 1) * PER]

    acols = acol_ref[step]
    for k in range(PER):
        head = step * PER + k
        lo, hi = k * HD, (k + 1) * HD
        arow = head_row(rows_ref, CUMUL, head)
        dt = head_row(rows_ref, DT, head)
        skip = head_row(rows_ref, SKIP, head)
        u_low = (dt * low_ref[0, lo:hi, :].astype(F32)).astype(BF16)
        du_first = None
        for tb in range(2):
            t0, t1 = tb * 128, tb * 128 + 128
            decay = jnp.exp(acols[t0:t1, k : k + 1] - arow[:, :t1] + link_ref[t0:t1, :t1])
            mixed = (decay * scores_ref[t0:t1, :t1]).astype(BF16)
            yt_ref[:, t0:t1] = mm_nt(u_low[:, :t1], mixed)
            du = mm(low_ref[1, lo:hi, t0:t1], mixed)
            if tb == 0:
                du_first = du
            else:
                du_ref[:, :128] = du_first + du[:, :128]
                du_ref[:, 128:] = du[:, 128:]
            dmix = mm(gy_ref[t0:t1, lo:hi], u_low[:, :t1])
            dg_ref[t0:t1, :t1] += decay * dmix
        x_h = low_ref[0, lo:hi, :].astype(F32)
        dy_h = low_ref[1, lo:hi, :].astype(F32)
        y_h = yt_ref[...]
        du_h = du_ref[...]
        slope = slope_ref[lo:hi, :]
        high_ref[0, lo:hi, :] = y_h + skip * x_h
        high_ref[1, lo:hi, :] = slope * (dt * du_h + skip * dy_h)
        high_ref[2, lo:hi, :] = slope * (dt * head_row(rows_ref, END, head))
        ga = jnp.sum(dy_h * y_h - u_low.astype(F32) * du_h, axis=0, keepdims=True)
        red_ref[0, pl.ds(head, 1), :] = ga
        red_ref[1, pl.ds(head, 1), :] = jnp.sum(x_h * du_h, axis=0, keepdims=True)
        red_ref[2, pl.ds(head, 1), :] = jnp.sum(x_h * dy_h, axis=0, keepdims=True)

    @pl.when(step == pl.num_programs(0) - 1)
    def _():
        dg = dg_ref[...].astype(BF16)
        dbc_ref[:NS, :] = mm(bclow_ref[1, NS:, :], dg)
        dbc_ref[NS:, :] = mm_nt(bclow_ref[1, :NS, :], dg)


def scan_kernel(in_ref, out_ref):
    peers = in_ref.shape[0]
    ahead = jnp.zeros((32, NS), F32)
    behind = jnp.zeros((32, NS), F32)

    def through(at):
        parts = in_ref[at, 64:72, :].astype(F32)
        return parts[0:1] + parts[1:2] + parts[2:3]

    for i in range(peers):
        out_ref[i, 0:32, :] = ahead.astype(BF16)
        ahead = through(i) * ahead + in_ref[i, 0:32, :].astype(F32)
        at = peers - 1 - i
        out_ref[at, 32:64, :] = behind.astype(BF16)
        behind = through(at) * behind + in_ref[at, 32:64, :].astype(F32)


def bc_kernel(
    state_ref, scaled_ref, dbc_ref, bcslope_ref, bclow_ref, bcsides_ref, rows_ref, pay_ref
):
    small = eye(NS, BF16)
    channels = scaled_ref.shape[1]
    state_in = state_ref[:, 0:32, :].reshape(channels, NS)
    state_back = state_ref[:, 32:64, :].reshape(channels, NS)
    grad_b = mm(mm_nt(small, state_back).astype(BF16), scaled_ref[0])
    grad_c = mm(mm_nt(small, state_in).astype(BF16), scaled_ref[1])
    grad_act = dbc_ref[...] + jnp.concatenate([grad_b, grad_c], axis=0)
    grad, sides = conv_back(
        grad_act * bcslope_ref[...], bclow_ref[0].astype(F32), bcsides_ref[...],
        bcsides_ref[...], masks_of(rows_ref),
    )
    token = mm_nt(eye(BLK, BF16), grad.astype(BF16)).astype(BF16)
    row = iota((16, 128), 0)
    pick = (jnp.where(row < 8, row, row + 96) == iota((16, 128), 1)).astype(BF16)
    rest = mm_nt(pick, sides.astype(BF16)).astype(BF16)
    shares = pay_ref.shape[0]
    share = BLK // shares
    for j in range(shares):
        pay_ref[j, 0:share, :] = token[j * share : (j + 1) * share]
        pay_ref[j, share : share + 16, :] = rest


def x_kernel(
    state_ref, low_ref, high_ref, taps_ref, rows_ref, bctok_ref, local_ref,
    out_ref, gx_ref, sides_ref, gdt_ref, gh_ref,
    red_ref,
):
    step = pl.program_id(0)
    ident = eye(BLK, BF16)
    masks = masks_of(rows_ref)
    state_in = state_ref[:, 0:32, :].reshape(BLK, NS)
    state_back = state_ref[:, 32:64, :].reshape(BLK, NS)
    carried = mm_nt(state_in, bctok_ref[:, NS:])
    from_end = mm_nt(state_back, bctok_ref[:, :NS])
    both = state_in.astype(F32) * state_back.astype(F32)
    last_lane = iota((1, BLK), 1) == BLK - 1
    y_parts = []
    for k in range(PER):
        head = step * PER + k
        lo, hi = k * HD, (k + 1) * HD
        dt = head_row(rows_ref, DT, head)
        carry = head_row(rows_ref, CARRY, head)
        end = head_row(rows_ref, END, head)
        x_h = low_ref[0, lo:hi, :].astype(F32)
        add = carry * carried[lo:hi]
        fed = end * jnp.sum(x_h * from_end[lo:hi], axis=0, keepdims=True)
        from_step = dt * fed
        at_end = jnp.sum(from_step, axis=1, keepdims=True)
        joint = jnp.sum(jnp.sum(both[lo:hi], axis=0, keepdims=True), axis=1, keepdims=True)
        at_end = at_end + carry[:, BLK - 1 :] * joint
        ga = jnp.sum(low_ref[1, lo:hi, :].astype(F32) * add, axis=0, keepdims=True) - from_step
        red_ref[0, pl.ds(head, 1), :] = ga + jnp.where(last_lane, at_end, 0.0)
        red_ref[1, pl.ds(head, 1), :] = fed
        y_parts.append((high_ref[0, lo:hi, :] + add).astype(BF16))
    out_ref[...] = mm_nt(ident, jnp.concatenate(y_parts, axis=0)).astype(BF16)
    grad, sides = conv_back(
        high_ref[1] + high_ref[2] * from_end, low_ref[2].astype(F32),
        taps_ref[...], taps_ref[...], masks,
    )
    gx_ref[...] = mm_nt(ident, grad.astype(BF16)).astype(BF16)
    row = iota((8 + 2 * RIM, 128), 0)
    pick = (jnp.where(row < 8, row, row + 88) == iota((8 + 2 * RIM, 128), 1)).astype(BF16)
    sides_ref[...] = pick_nt(pick, sides, 2)

    @pl.when(step == pl.num_programs(0) - 1)
    def _():
        later = (iota((BLK, BLK), 0) >= iota((BLK, BLK), 1)).astype(BF16)
        grad_log = pick_right(local_ref[0] + red_ref[0], later, 3)
        rate = rows_ref[RATE]
        grad_step = (local_ref[1] + red_ref[1] - rate * grad_log) * rows_ref[SIG]
        gdt_ref[...] = grad_step
        which = iota((8, BLK), 0)
        terms = (-rate * rows_ref[DT] * grad_log, grad_step, local_ref[2])
        gh_ref[...] = jnp.zeros_like(gh_ref)
        gh_ref[:, : rate.shape[0]] = sum(
            pick_nt((which == k).astype(BF16), term, 3) for k, term in enumerate(terms)
        )


def patch_kernel(gx_ref, sides_ref, own_ref, spill_ref, out_ref, bc_ref):
    del gx_ref
    width = sides_ref.shape[1]
    out_ref[...] = (sides_ref[8 + RIM :, :] + spill_ref[:, :width]).astype(BF16)
    share = own_ref.shape[0]
    bc_ref[: share - 8, :] = own_ref[: share - 8, :]
    is_last = lax.axis_index("head") == lax.axis_size("head") - 1
    came = spill_ref[RIM - 8 :, width:]
    bc_ref[share - 8 :, :] = own_ref[share - 8 :, :] + jnp.where(is_last, came, 0.0)


def pack_kernel(got_ref, sides_ref, gh_ref, sums_ref, own_ref, out_ref):
    share = own_ref.shape[0]
    total = jnp.sum(got_ref[...].astype(F32), axis=0)
    own_ref[...] = total[:share]
    width = sides_ref.shape[1]
    out_ref[:, :width] = sides_ref[8 : 8 + RIM, :]
    out_ref[: RIM - 8, width:] = jnp.zeros((RIM - 8, 256), F32)
    out_ref[RIM - 8 :, width:] = total[share + 8 :]
    sums_ref[:, :width] = sides_ref[:8, :]
    sums_ref[:, width : width + 256] = total[share : share + 8]
    sums_ref[:, width + 256 :] = gh_ref[...]


def finish_kernel(a_ref, b_ref, c_ref, d_ref, wx_ref, wbc_ref, heads_ref):
    total = (a_ref[...] + b_ref[...]) + (c_ref[...] + d_ref[...])
    width = wx_ref.shape[1]
    wx_ref[...] = total[:4, :width]
    wbc_ref[...] = total[:4, width : width + 256]
    heads_ref[...] = total[:3, width + 256 : width + 256 + heads_ref.shape[1]]


def whole(shape):
    zeros = (0,) * len(shape)
    return pl.BlockSpec(shape, lambda *_: zeros)


def columns(rows):
    return pl.BlockSpec((rows, BLK), lambda i: (0, i))


def channel_rows(width):
    return pl.BlockSpec((BLK, width), lambda i: (i, 0))


def shaped(shape, dtype):
    return jax.ShapeDtypeStruct(shape, dtype)


def stored(shape, dtype):
    return pltpu.HBM(shape, dtype)


def from_hbm(*values):
    return [pltpu.with_memory_space_constraint(value, pltpu.HBM) for value in values]


def passed_along(value, by):
    peers = lax.axis_size("ctx")
    pairs = [(i, i + by) for i in range(peers) if 0 <= i + by < peers]
    return lax.ppermute(value, "ctx", pairs)


def summed_over_ctx(value):
    peers = lax.axis_size("ctx")

    def turned(value, stride):
        def to(i, by):
            at = i // stride % 4
            return i + ((at + by) % 4 - at) * stride

        return [value] + [
            lax.ppermute(value, "ctx", [(i, to(i, by)) for i in range(peers)])
            for by in (1, 2, 3)
        ]

    value = value + lax.ppermute(value, "ctx", [(i, i ^ 1) for i in range(peers)])
    own, one, two, three = turned(value, 2)
    return turned((own + one) + (two + three), 8)


def cost(micros):
    return pl.CostEstimate(
        flops=int(micros * 1e8), bytes_accessed=int(micros * 3e6), transcendentals=0
    )


def local(x_raw, bc_raw, dt_raw, conv_x, conv_bc, a_log, dt_bias, skip_weight, segment, grad_y):
    rows, channels = x_raw.shape
    heads = dt_raw.shape[1]
    steps = channels // BLK
    peers = lax.axis_size("ctx")
    shares = lax.axis_size("head")
    share = rows // shares
    params = pltpu.CompilerParams(vmem_limit_bytes=VMEM)
    last_inputs = pl.pallas_call(
        rim_kernel,
        in_specs=[pl.BlockSpec(memory_space=pl.ANY)] * 2,
        out_specs=pl.BlockSpec(memory_space=pltpu.VMEM),
        out_shape=shaped((RIM, channels + 256), BF16),
        scratch_shapes=[pltpu.SemaphoreType.DMA((2,))],
        compiler_params=params,
        name="rim_rows",
    )(*from_hbm(x_raw, bc_raw))
    rim = passed_along(last_inputs, 1)
    row_spec = whole((8, heads, rows))
    square = whole((256, rows))
    by_channel = channel_rows(rows)

    def chan(dtype):
        return stored((channels, rows), dtype)

    rim_bc_spec = pl.BlockSpec((RIM, 256), lambda i: (0, channels // 256))
    local_spec = whole((3, heads, rows))

    def stack(count):
        return pl.BlockSpec((count, BLK, rows), lambda i: (0, i, 0))

    wide_spec = channel_rows(128)

    def one(shape):
        return pl.BlockSpec(shape, lambda i: (0,) * len(shape))

    pay, head_rows, bctok = pl.pallas_call(
        state_kernel,
        grid=(steps,),
        in_specs=[
            columns(rows), columns(RIM), columns(rows), columns(4),
            one((rows, 256)), rim_bc_spec, one((4, 256)),
            one(segment_rows := (segment.shape[0] // 128, 128)), one((1, heads)), one((1, heads)),
            one((1, heads)), one((heads, rows)),
        ],
        out_specs=[
            pl.BlockSpec((8, 72, NS), lambda i: (i, 0, 0)), row_spec, whole((rows, 256)),
        ],
        out_shape=[
            shaped((peers, 72, NS), BF16),
            stored((8, heads, rows), F32), stored((rows, 256), BF16),
        ],
        compiler_params=params,
        cost_estimate=cost(7),
        name="states",
    )(
        *from_hbm(x_raw), rim, *from_hbm(grad_y, conv_x, bc_raw), rim,
        *from_hbm(
            conv_bc, segment.reshape(segment_rows), a_log[None], dt_bias[None],
            skip_weight[None], dt_raw.T,
        ),
    )

    got = lax.all_to_all(pay, "ctx", 0, 0, tiled=True)

    low, slope, scaled, sides_in, bclow, bcslope, bcsides = pl.pallas_call(
        slope_kernel,
        grid=(steps,),
        in_specs=[
            columns(rows), columns(RIM), columns(rows), columns(4), whole((rows, 256)),
            rim_bc_spec, whole((4, 256)), row_spec,
        ],
        out_specs=[
            stack(3), by_channel, stack(2), wide_spec, whole((2, 256, rows)), square,
            whole((256, 128)),
        ],
        out_shape=[
            stored((3, channels, rows), BF16), chan(F32), stored((2, channels, rows), BF16),
            stored((channels, 128), F32), stored((2, 256, rows), BF16), stored((256, rows), F32),
            stored((256, 128), F32),
        ],
        compiler_params=params,
        cost_estimate=cost(6),
        name="slopes",
    )(*from_hbm(x_raw, rim, grad_y, conv_x, bc_raw, rim, conv_bc, head_rows))
    got, low = lax.optimization_barrier((got, low))

    carried = pl.pallas_call(
        scan_kernel,
        in_specs=[pl.BlockSpec(memory_space=pltpu.VMEM)],
        out_specs=pl.BlockSpec(memory_space=pltpu.VMEM),
        out_shape=shaped((peers, 64, NS), BF16),
        compiler_params=params,
        cost_estimate=cost(1),
        name="state_scan",
    )(got)
    states = lax.all_to_all(carried, "ctx", 0, 0, tiled=True)

    high, red_loc, dbc = pl.pallas_call(
        block_kernel,
        grid=(steps,),
        in_specs=[
            stack(2), columns(rows), row_spec, whole((rows, 256)), whole((2, 256, rows)),
            by_channel,
        ],
        out_specs=[stack(3), local_spec, square],
        out_shape=[
            stored((3, channels, rows), F32), stored((3, heads, rows), F32),
            stored((256, rows), F32),
        ],
        scratch_shapes=[
            pltpu.VMEM((rows, rows), F32), pltpu.VMEM((rows, rows), F32),
            pltpu.VMEM((steps, rows, PER), F32), pltpu.VMEM((rows, rows), F32),
            pltpu.VMEM((HD, rows), F32), pltpu.VMEM((HD, rows), F32),
        ],
        compiler_params=params,
        cost_estimate=cost(8),
        name="in_block",
    )(*from_hbm(low, grad_y, head_rows, bctok, bclow, slope))

    state_spec = pl.BlockSpec((8, 64, NS), lambda i: (i, 0, 0))
    pay_bc = pl.pallas_call(
        bc_kernel,
        grid=(1,),
        in_specs=[
            one((peers, 64, NS)), one((2, channels, rows)), square, square,
            whole((2, 256, rows)), whole((256, 128)), row_spec,
        ],
        out_specs=whole((shares, share + 16, 256)),
        out_shape=shaped((shares, share + 16, 256), BF16),
        compiler_params=params,
        cost_estimate=cost(4),
        name="bc_part",
    )(states, *from_hbm(scaled, dbc, bcslope, bclow, bcsides, head_rows))
    got_bc = lax.all_to_all(pay_bc, "head", 0, 0, tiled=True)

    side_rows = 8 + 2 * RIM
    ssd_out, gx, sides, grad_dt, gh = pl.pallas_call(
        x_kernel,
        grid=(steps,),
        in_specs=[
            state_spec, stack(3), stack(3), wide_spec, row_spec, whole((rows, 256)), local_spec,
        ],
        out_specs=[
            columns(rows), columns(rows), columns(side_rows), whole((heads, rows)),
            whole((8, 128)),
        ],
        out_shape=[
            stored((rows, channels), BF16), stored((rows, channels), BF16),
            stored((side_rows, channels), F32), stored((heads, rows), F32),
            stored((8, 128), F32),
        ],
        scratch_shapes=[pltpu.VMEM((2, heads, rows), F32)],
        compiler_params=params,
        cost_estimate=cost(10),
        name="x_part",
    )(states, *from_hbm(low, high, sides_in, head_rows, bctok, red_loc))

    vmem = pl.BlockSpec(memory_space=pltpu.VMEM)
    width = channels + 256 + 128
    sums, own_bc, spills = pl.pallas_call(
        pack_kernel,
        in_specs=[vmem] * 3,
        out_specs=[vmem] * 3,
        out_shape=[
            shaped((8, width), F32), shaped((share, 256), F32),
            shaped((RIM, channels + 256), F32),
        ],
        compiler_params=params,
        cost_estimate=cost(1),
        name="pack_sums",
    )(got_bc, *from_hbm(sides, gh))
    parts = summed_over_ctx(sums)
    spills = passed_along(spills, -1)
    grad_x, grad_bc = pl.pallas_call(
        patch_kernel,
        grid=(1,),
        in_specs=[
            pl.BlockSpec(memory_space=pl.ANY), whole((side_rows, channels)), whole((share, 256)),
            whole((RIM, channels + 256)),
        ],
        out_specs=[
            pl.BlockSpec((RIM, channels), lambda i: (rows // RIM - 1, 0)), whole((share, 256)),
        ],
        out_shape=[stored((rows, channels), BF16), stored((share, 256), F32)],
        input_output_aliases={0: 0},
        compiler_params=params,
        cost_estimate=cost(1),
        name="last_rows",
    )(*from_hbm(gx, sides), own_bc, spills)
    grad_wx, grad_wbc, grad_heads = pl.pallas_call(
        finish_kernel,
        in_specs=[vmem] * 4,
        out_specs=[vmem] * 3,
        out_shape=[stored((4, channels), F32), stored((4, 256), F32), stored((3, heads), F32)],
        compiler_params=params,
        cost_estimate=cost(1),
        name="finish_sums",
    )(*parts)
    return ssd_out, grad_x, grad_bc, grad_dt.T, grad_wx, grad_wbc, grad_heads


def solution(mesh):
    in_specs = (
        P("ctx", "head"), P("ctx", None), P("ctx", "head"), P(None, "head"), P(),
        P("head"), P("head"), P("head"), P(), P("ctx", "head"),
    )
    out_specs = (
        P("ctx", "head"), P("ctx", "head"), P(("ctx", "head"), None), P("ctx", "head"),
        P(None, "head"), P(), P(None, "head"),
    )
    return jax.shard_map(local, mesh=mesh, in_specs=in_specs, out_specs=out_specs, check_vma=False)
```

time: 93.1 us -> 90.9 us (0.976)
  local copies, waits for them, and re-layouts: 1.63 us -> 0.01 us
  Pallas kernels: 36.4 us -> 34.8 us
  waiting for transfers between devices: 17.9 us -> 19.2 us
    pallas_call x4 -> x5, Pallas kernels: 19.5 us -> 18.1 us  [the longest x1 6.89 us: local(): pl.pallas_call(x_kernel, grid=(steps,), in_specs=[state_spec, stack(3), s...]
where the time goes in v4:
time: 90.9 us; the launch traced here: 89.4 us
  Pallas kernels  34.8 us (38%)
  starting transfers between devices  34.7 us (38%)
  waiting for transfers between devices  19.2 us (21%)
    all_to_all x1, starting transfers between devices, local(): got = lax.all_to_all(pay, 'ctx', 0, 0, tiled=True)  8.32 us
    all_to_all x1, starting transfers between devices, local(): got_bc = lax.all_to_all(pay_bc, 'head', 0, 0, tiled=True)  8.18 us
    ppermute x2, starting transfers between devices, passed_along(): return lax.ppermute(value, 'ctx', pairs)  7.39 us
    pallas_call x1, Pallas kernels, local(): pl.pallas_call(slope_kernel, grid=(steps,), in_specs=[columns(rows), colu...  7.04 us
    pallas_call x1, Pallas kernels, local(): pl.pallas_call(x_kernel, grid=(steps,), in_specs=[state_spec, stack(3), s...  6.89 us
    pallas_call x1, Pallas kernels, local(): pl.pallas_call(state_kernel, grid=(steps,), in_specs=[columns(rows), colu...  6.58 us
    pallas_call x1, Pallas kernels, local(): pl.pallas_call(block_kernel, grid=(steps,), in_specs=[stack(2), columns(r...  6.12 us
    all_to_all x1, waiting for transfers between devices, local(): states = lax.all_to_all(carried, 'ctx', 0, 0, tiled=True)  5.54 us
  transfers between devices with their start and end apart: 12, of which 10 were waited for; matrix products, arithmetic and copies ran while one was open for 0% of the time, Pallas kernels for 24%

profile of v4, /device:TPU:1, one launch (start us, length us, event | category | flops | bytes accessed | tf_op | source)
XLA Modules:
  0.0 89.4 jit_solution(13735844789924991136)
XLA Ops:
  0.6 0.8 rim_rows.1
  1.4 4.5 %collective-permute-start = (bf16[16,1280]{1,0:T(8,128)(2,1)S(1)}, bf16[16,1280]{1,0:T(8,128)(2,1)S(1)}, u32[]{:S(2)}, u32[]{:S(2)}) collective-permute-start(bf16[16,1280]{1,0:T(8,128)(2,1)S(1)} %rim_rows.1), channel_id=1, source_target_pairs={{0,8},{8,16},{16,24},{24,32},{32,40},{40,48},{48,56},{56,64},{64,7... | collective-permute-start | bytes 122888 | tf_op jit(solution)/shard_map/ppermute | solution.py:486
  5.9 1.1 %collective-permute-done.rim_ref.rimbc_ref = bf16[16,1280]{1,0:T(8,128)(2,1)S(1)} collective-permute-done((bf16[16,1280]{1,0:T(8,128)(2,1)S(1)}, bf16[16,1280]{1,0:T(8,128)(2,1)S(1)}, u32[]{:S(2)}, u32[]{:S(2)}) %collective-permute-start) | collective-permute-done | bytes 40992 | tf_op jit(solution)/shard_map/ppermute | solution.py:486
  7.0 6.6 %states.1 = (bf16[32,72,128]{2,1,0:T(8,128)(2,1)}, f32[8,16,256]{2,1,0:T(8,128)}, bf16[256,256]{1,0:T(8,128)(2,1)}) custom-call(bf16[256,1024]{1,0:T(8,128)(2,1)} %x_ref.5, bf16[16,1280]{1,0:T(8,128)(2,1)S(1)} %collective-permute-done.rim_ref.rimbc_ref, bf16[256,1024]{1,0:T(8,128)(2,1)} %gy_ref.5, f32[4,1024]{1,0:T(4,128)} %wx_ref.3, ...), custom_call_target="tpu_custom_call" | custom-call | flops 700000000 | bytes 21000000 | tf_op jit(solution)/shard_map/states/pallas_call | solution.py:549
  13.6 8.3 %all-to-all-start = ((bf16[32,72,128]{2,1,0:T(8,128)(2,1)}), bf16[32,72,128]{2,1,0:T(8,128)(2,1)S(1)}, u32[]{:S(2)}, u32[]{:S(2)}) async-start(bf16[32,72,128]{2,1,0:T(8,128)(2,1)} %get-tuple-element.35), calls=%async_computation | async-start | bytes 1179648 | tf_op jit(solution)/shard_map/all_to_all | solution.py:576
  21.9 7.0 %slopes.1 = (bf16[3,1024,256]{2,1,0:T(8,128)(2,1)}, f32[1024,256]{1,0:T(8,128)}, bf16[2,1024,256]{2,1,0:T(8,128)(2,1)}, f32[1024,128]{1,0:T(8,128)}, bf16[2,256,...) custom-call(bf16[256,1024]{1,0:T(8,128)(2,1)} %x_ref.5, bf16[16,1280]{1,0:T(8,128)(2,1)} %copy-done, ...), custom_call_target="tpu_custom_call" | custom-call | flops 600000000 | bytes 18000000 | tf_op jit(solution)/shard_map/slopes/pallas_call | solution.py:578
  29.0 5.2 %all-to-all-done.in_ref = bf16[32,72,128]{2,1,0:T(8,128)(2,1)S(1)} async-done(((bf16[32,72,128]{2,1,0:T(8,128)(2,1)}), bf16[32,72,128]{2,1,0:T(8,128)(2,1)S(1)}, u32[]{:S(2)}, u32[]{:S(2)}) %all-to-all-start) | async-done | bytes 589856 | tf_op jit(solution)/shard_map/all_to_all | solution.py:576
  34.2 1.0 %state_scan.1 = bf16[32,64,128]{2,1,0:T(8,128)(2,1)} custom-call(bf16[32,72,128]{2,1,0:T(8,128)(2,1)S(1)} %all-to-all-done.in_ref), custom_call_target="tpu_custom_call" | custom-call | flops 100000000 | bytes 3000000 | tf_op jit(solution)/shard_map/state_scan/pallas_call | solution.py:600
  35.1 4.1 %all-to-all-start.1 = ((bf16[32,64,128]{2,1,0:T(8,128)(2,1)}), bf16[32,64,128]{2,1,0:T(8,128)(2,1)S(1)}, u32[]{:S(2)}, u32[]{:S(2)}) async-start(bf16[32,64,128]{2,1,0:T(8,128)(2,1)} %state_scan.1), calls=%async_computation.1 | async-start | bytes 1048576 | tf_op jit(solution)/shard_map/all_to_all | solution.py:609
  39.2 6.1 %in_block.1 = (f32[3,1024,256]{2,1,0:T(8,128)}, f32[3,16,256]{2,1,0:T(8,128)}, f32[256,256]{1,0:T(8,128)}) custom-call(bf16[3,1024,256]{2,1,0:T(8,128)(2,1)} %get-tuple-element.39.low_ref, bf16[256,1024]{1,0:T(8,128)(2,1)} %gy_ref.5, f32[8,16,256]{2,1,0:T(8,128)} %get-tuple-element.36.rows_ref, bf16[256,256]{1,0:T(8,128)(2,1)} %get-tuple-element.40.bctok_ref, ...), custom_call_target="tpu_custom_call" | custom-call | flops 800000000 | bytes 24000000 | tf_op jit(solution)/shard_map/in_block/pallas_call | solution.py:611
  45.3 5.5 %all-to-all-done.1.state_ref = bf16[32,64,128]{2,1,0:T(8,128)(2,1)S(1)} async-done(((bf16[32,64,128]{2,1,0:T(8,128)(2,1)}), bf16[32,64,128]{2,1,0:T(8,128)(2,1)S(1)}, u32[]{:S(2)}, u32[]{:S(2)}) %all-to-all-start.1) | async-done | bytes 524320 | tf_op jit(solution)/shard_map/all_to_all | solution.py:609
  50.9 3.3 %bc_part.1 = bf16[8,48,256]{2,1,0:T(8,128)(2,1)} custom-call(bf16[32,64,128]{2,1,0:T(8,128)(2,1)S(1)} %all-to-all-done.1.state_ref, bf16[2,1024,256]{2,1,0:T(8,128)(2,1)} %get-tuple-element.49.scaled_ref, f32[256,256]{1,0:T(8,128)} %get-tuple-element.50.dbc_ref, f32[256,256]{1,0:T(8,128)} %get-tuple-element.51.bcslope_ref, ...), custom_call_target="tpu_custom_call" | custom-call | flops 400000000 | bytes 12000000 | tf_op jit(solution)/shard_map/bc_part/pallas_call | solution.py:634
  54.2 8.2 %all-to-all-start.2 = ((bf16[8,48,256]{2,1,0:T(8,128)(2,1)}), bf16[8,48,256]{2,1,0:T(8,128)(2,1)S(1)}, u32[]{:S(2)}, u32[]{:S(2)}) async-start(bf16[8,48,256]{2,1,0:T(8,128)(2,1)} %bc_part.1), calls=%async_computation.2 | async-start | bytes 393216 | tf_op jit(solution)/shard_map/all_to_all | solution.py:647
  62.4 6.9 %x_part.1 = (bf16[256,1024]{1,0:T(8,128)(2,1)}, bf16[256,1024]{1,0:T(8,128)(2,1)}, f32[40,1024]{1,0:T(8,128)}, f32[16,256]{1,0:T(8,128)}, f32[8,128]{1,0:T(8,128)}) custom-call(bf16[32,64,128]{2,1,0:T(8,128)(2,1)S(1)} %all-to-all-done.1.state_ref, bf16[3,1024,256]{2,1,0:T(8,128)(2,1)} %get-tuple-element.39.low_ref, ...), custom_call_target="tpu_custom_call" | custom-call | flops 1000000000 | bytes 30000000 | tf_op jit(solution)/shard_map/x_part/pallas_call | solution.py:650
  69.3 2.4 %all-to-all-done.2.got_ref = bf16[8,48,256]{2,1,0:T(8,128)(2,1)S(1)} async-done(((bf16[8,48,256]{2,1,0:T(8,128)(2,1)}), bf16[8,48,256]{2,1,0:T(8,128)(2,1)S(1)}, u32[]{:S(2)}, u32[]{:S(2)}) %all-to-all-start.2) | async-done | bytes 196640 | tf_op jit(solution)/shard_map/all_to_all | solution.py:647
  71.7 0.9 %pack_sums.1 = (f32[8,1408]{1,0:T(8,128)S(1)}, f32[32,256]{1,0:T(8,128)S(1)}, f32[16,1280]{1,0:T(8,128)S(1)}) custom-call(bf16[8,48,256]{2,1,0:T(8,128)(2,1)S(1)} %all-to-all-done.2.got_ref, f32[40,1024]{1,0:T(8,128)} %get-tuple-element.48.sides_ref, f32[8,128]{1,0:T(8,128)} %get-tuple-element.53.gh_ref), custom_call_target="tpu_custom_call" | custom-call | flops 100000000 | bytes 3000000 | tf_op jit(solution)/shard_map/pack_sums/pallas_call | solution.py:673
  72.7 2.2 %collective-permute-start.2 = (f32[8,1408]{1,0:T(8,128)S(1)}, f32[8,1408]{1,0:T(8,128)S(1)}, u32[]{:S(2)}, u32[]{:S(2)}) collective-permute-start(f32[8,1408]{1,0:T(8,128)S(1)} %get-tuple-element.59), channel_id=1, source_target_pairs={{0,8},{8,0},{16,24},{24,16},{32,40},{40,32},{48,56},{56,48},{64,72... | collective-permute-start | bytes 135176 | tf_op jit(solution)/shard_map/ppermute | solution.py:502
  74.8 0.9 collective-permute-done.2
  75.7 1.3 %collective-permute-start.5 = (f32[8,1408]{1,0:T(8,128)S(1)}, f32[8,1408]{1,0:T(8,128)S(1)}, u32[]{:S(2)}, u32[]{:S(2)}) collective-permute-start(f32[8,1408]{1,0:T(8,128)S(1)} %add.12), channel_id=1, source_target_pairs={{0,48},{8,56},{16,0},{24,8},{32,16},{40,24},{48,32},{56,40},{64,11... | collective-permute-start | bytes 135176 | tf_op jit(solution)/shard_map/ppermute | solution.py:498
  77.0 1.0 %collective-permute-start.4 = (f32[8,1408]{1,0:T(8,128)S(1)}, f32[8,1408]{1,0:T(8,128)S(1)}, u32[]{:S(2)}, u32[]{:S(2)}) collective-permute-start(f32[8,1408]{1,0:T(8,128)S(1)} %add.12), channel_id=1, source_target_pairs={{0,32},{8,40},{16,48},{24,56},{32,0},{40,8},{48,16},{56,24},{64,96... | collective-permute-start | bytes 135176 | tf_op jit(solution)/shard_map/ppermute | solution.py:498
  78.0 2.9 %collective-permute-start.1 = (f32[16,1280]{1,0:T(8,128)S(1)}, f32[16,1280]{1,0:T(8,128)S(1)}, u32[]{:S(2)}, u32[]{:S(2)}) collective-permute-start(f32[16,1280]{1,0:T(8,128)S(1)} %get-tuple-element.55), channel_id=1, source_target_pairs={{8,0},{16,8},{24,16},{32,24},{40,32},{48,40},{56,48},{64,56},{72,6... | collective-permute-start | bytes 245768 | tf_op jit(solution)/shard_map/ppermute | solution.py:486
  80.9 0.0 collective-permute-done.5
  80.9 0.5 collective-permute-done.4
  81.5 1.0 %collective-permute-done.3 = f32[8,1408]{1,0:T(8,128)S(1)} collective-permute-done((f32[8,1408]{1,0:T(8,128)S(1)}, f32[8,1408]{1,0:T(8,128)S(1)}, u32[]{:S(2)}, u32[]{:S(2)}) %collective-permute-start.3) | collective-permute-done | bytes 45088 | tf_op jit(solution)/shard_map/ppermute | solution.py:498
  82.5 0.9 %collective-permute-start.8 = (f32[8,1408]{1,0:T(8,128)S(1)}, f32[8,1408]{1,0:T(8,128)S(1)}, u32[]{:S(2)}, u32[]{:S(2)}) collective-permute-start(f32[8,1408]{1,0:T(8,128)S(1)} %add_add_fusion.a_ref), channel_id=1, source_target_pairs={{0,192},{8,200},{16,208},{24,216},{32,224},{40,232},{48,240},{56,2... | collective-permute-start | bytes 135176 | tf_op jit(solution)/shard_map/ppermute | solution.py:498
  83.4 1.3 %collective-permute-start.7 = (f32[8,1408]{1,0:T(8,128)S(1)}, f32[8,1408]{1,0:T(8,128)S(1)}, u32[]{:S(2)}, u32[]{:S(2)}) collective-permute-start(f32[8,1408]{1,0:T(8,128)S(1)} %add_add_fusion.a_ref), channel_id=1, source_target_pairs={{0,128},{8,136},{16,144},{24,152},{32,160},{40,168},{48,176},{56,1... | collective-permute-start | bytes 135176 | tf_op jit(solution)/shard_map/ppermute | solution.py:498
  84.7 0.1 collective-permute-done.1.spill_ref
  84.8 1.6 %last_rows.1 = (bf16[256,1024]{1,0:T(8,128)(2,1)}, f32[32,256]{1,0:T(8,128)}) custom-call(bf16[256,1024]{1,0:T(8,128)(2,1)} %get-tuple-element.47.gx_ref, f32[40,1024]{1,0:T(8,128)} %get-tuple-element.48.sides_ref, f32[32,256]{1,0:T(8,128)S(1)} %get-tuple-element.54.own_ref, ...), custom_call_target="tpu_custom_call", output_to_operand_aliasing={{0}: (0, {})} | custom-call | flops 100000000 | bytes 3000000 | tf_op jit(solution)/shard_map/last_rows/pallas_call | solution.py:687
  86.4 0.0 collective-permute-done.8.d_ref
  86.4 1.4 %collective-permute-done.7.c_ref = f32[8,1408]{1,0:T(8,128)S(1)} collective-permute-done((f32[8,1408]{1,0:T(8,128)S(1)}, f32[8,1408]{1,0:T(8,128)S(1)}, u32[]{:S(2)}, u32[]{:S(2)}) %collective-permute-start.7) | collective-permute-done | bytes 45088 | tf_op jit(solution)/shard_map/ppermute | solution.py:498
  87.8 1.0 %collective-permute-done.6.b_ref = f32[8,1408]{1,0:T(8,128)S(1)} collective-permute-done((f32[8,1408]{1,0:T(8,128)S(1)}, f32[8,1408]{1,0:T(8,128)S(1)}, u32[]{:S(2)}, u32[]{:S(2)}) %collective-permute-start.6) | collective-permute-done | bytes 45088 | tf_op jit(solution)/shard_map/ppermute | solution.py:498
  88.8 0.6 finish_sums.1
  (6 shorter events, 0.0 us)
Async XLA Ops:
  1.4 5.6 %collective-permute-start = (bf16[16,1280]{1,0:T(8,128)(2,1)S(1)}, bf16[16,1280]{1,0:T(8,128)(2,1)S(1)}, u32[]{:S(2)}, u32[]{:S(2)}) collective-permute-start(bf16[16,1280]{1,0:T(8,128)(2,1)S(1)} %rim_rows.1), channel_id=1, source_target_pairs={{0,8},{8,16},{16,24},{24,32},{32,40},{40,48},{48,56},{56,64},{64,7... | collective-permute-start | bytes 122888 | tf_op jit(solution)/shard_map/ppermute | solution.py:486
  7.0 14.9 %copy-start = (bf16[16,1280]{1,0:T(8,128)(2,1)}, bf16[16,1280]{1,0:T(8,128)(2,1)S(1)}, u32[]{:S(2)}) copy-start(bf16[16,1280]{1,0:T(8,128)(2,1)S(1)} %collective-permute-done.rim_ref.rimbc_ref) | copy-start | bytes 122884
  13.6 20.6 %all-to-all-start = ((bf16[32,72,128]{2,1,0:T(8,128)(2,1)}), bf16[32,72,128]{2,1,0:T(8,128)(2,1)S(1)}, u32[]{:S(2)}, u32[]{:S(2)}) async-start(bf16[32,72,128]{2,1,0:T(8,128)(2,1)} %get-tuple-element.35), calls=%async_computation | async-start | bytes 1179648 | tf_op jit(solution)/shard_map/all_to_all | solution.py:576
  35.1 15.7 %all-to-all-start.1 = ((bf16[32,64,128]{2,1,0:T(8,128)(2,1)}), bf16[32,64,128]{2,1,0:T(8,128)(2,1)S(1)}, u32[]{:S(2)}, u32[]{:S(2)}) async-start(bf16[32,64,128]{2,1,0:T(8,128)(2,1)} %state_scan.1), calls=%async_computation.1 | async-start | bytes 1048576 | tf_op jit(solution)/shard_map/all_to_all | solution.py:609
  54.2 17.5 %all-to-all-start.2 = ((bf16[8,48,256]{2,1,0:T(8,128)(2,1)}), bf16[8,48,256]{2,1,0:T(8,128)(2,1)S(1)}, u32[]{:S(2)}, u32[]{:S(2)}) async-start(bf16[8,48,256]{2,1,0:T(8,128)(2,1)} %bc_part.1), calls=%async_computation.2 | async-start | bytes 393216 | tf_op jit(solution)/shard_map/all_to_all | solution.py:647
  72.7 3.1 %collective-permute-start.2 = (f32[8,1408]{1,0:T(8,128)S(1)}, f32[8,1408]{1,0:T(8,128)S(1)}, u32[]{:S(2)}, u32[]{:S(2)}) collective-permute-start(f32[8,1408]{1,0:T(8,128)S(1)} %get-tuple-element.59), channel_id=1, source_target_pairs={{0,8},{8,0},{16,24},{24,16},{32,40},{40,32},{48,56},{56,48},{64,72... | collective-permute-start | bytes 135176 | tf_op jit(solution)/shard_map/ppermute | solution.py:502
  75.7 5.2 %collective-permute-start.5 = (f32[8,1408]{1,0:T(8,128)S(1)}, f32[8,1408]{1,0:T(8,128)S(1)}, u32[]{:S(2)}, u32[]{:S(2)}) collective-permute-start(f32[8,1408]{1,0:T(8,128)S(1)} %add.12), channel_id=1, source_target_pairs={{0,48},{8,56},{16,0},{24,8},{32,16},{40,24},{48,32},{56,40},{64,11... | collective-permute-start | bytes 135176 | tf_op jit(solution)/shard_map/ppermute | solution.py:498
  77.0 4.4 %collective-permute-start.4 = (f32[8,1408]{1,0:T(8,128)S(1)}, f32[8,1408]{1,0:T(8,128)S(1)}, u32[]{:S(2)}, u32[]{:S(2)}) collective-permute-start(f32[8,1408]{1,0:T(8,128)S(1)} %add.12), channel_id=1, source_target_pairs={{0,32},{8,40},{16,48},{24,56},{32,0},{40,8},{48,16},{56,24},{64,96... | collective-permute-start | bytes 135176 | tf_op jit(solution)/shard_map/ppermute | solution.py:498
  78.0 4.4 %collective-permute-start.3 = (f32[8,1408]{1,0:T(8,128)S(1)}, f32[8,1408]{1,0:T(8,128)S(1)}, u32[]{:S(2)}, u32[]{:S(2)}) collective-permute-start(f32[8,1408]{1,0:T(8,128)S(1)} %add.12), channel_id=1, source_target_pairs={{0,16},{8,24},{16,32},{24,40},{32,48},{40,56},{48,0},{56,8},{64,80... | collective-permute-start | bytes 135176 | tf_op jit(solution)/shard_map/ppermute | solution.py:498
  78.0 6.8 %collective-permute-start.1 = (f32[16,1280]{1,0:T(8,128)S(1)}, f32[16,1280]{1,0:T(8,128)S(1)}, u32[]{:S(2)}, u32[]{:S(2)}) collective-permute-start(f32[16,1280]{1,0:T(8,128)S(1)} %get-tuple-element.55), channel_id=1, source_target_pairs={{8,0},{16,8},{24,16},{32,24},{40,32},{48,40},{56,48},{64,56},{72,6... | collective-permute-start | bytes 245768 | tf_op jit(solution)/shard_map/ppermute | solution.py:486
  82.5 3.9 %collective-permute-start.8 = (f32[8,1408]{1,0:T(8,128)S(1)}, f32[8,1408]{1,0:T(8,128)S(1)}, u32[]{:S(2)}, u32[]{:S(2)}) collective-permute-start(f32[8,1408]{1,0:T(8,128)S(1)} %add_add_fusion.a_ref), channel_id=1, source_target_pairs={{0,192},{8,200},{16,208},{24,216},{32,224},{40,232},{48,240},{56,2... | collective-permute-start | bytes 135176 | tf_op jit(solution)/shard_map/ppermute | solution.py:498
  83.4 4.4 %collective-permute-start.7 = (f32[8,1408]{1,0:T(8,128)S(1)}, f32[8,1408]{1,0:T(8,128)S(1)}, u32[]{:S(2)}, u32[]{:S(2)}) collective-permute-start(f32[8,1408]{1,0:T(8,128)S(1)} %add_add_fusion.a_ref), channel_id=1, source_target_pairs={{0,128},{8,136},{16,144},{24,152},{32,160},{40,168},{48,176},{56,1... | collective-permute-start | bytes 135176 | tf_op jit(solution)/shard_map/ppermute | solution.py:498
  84.7 4.1 %collective-permute-start.6 = (f32[8,1408]{1,0:T(8,128)S(1)}, f32[8,1408]{1,0:T(8,128)S(1)}, u32[]{:S(2)}, u32[]{:S(2)}) collective-permute-start(f32[8,1408]{1,0:T(8,128)S(1)} %add_add_fusion.a_ref), channel_id=1, source_target_pairs={{0,64},{8,72},{16,80},{24,88},{32,96},{40,104},{48,112},{56,120},{... | collective-permute-start | bytes 135176 | tf_op jit(solution)/shard_map/ppermute | solution.py:498

commit v5 on v4

--- a/solution.py
+++ b/solution.py
@@ -356,14 +356,14 @@
         bcsides_ref[...], masks_of(rows_ref),
     )
     token = mm_nt(eye(BLK, BF16), grad.astype(BF16)).astype(BF16)
-    row = iota((16, 128), 0)
-    pick = (jnp.where(row < 8, row, row + 96) == iota((16, 128), 1)).astype(BF16)
+    row = iota((8, 128), 0)
+    pick = (jnp.where(row < 4, row, row + 104) == iota((8, 128), 1)).astype(BF16)
     rest = mm_nt(pick, sides.astype(BF16)).astype(BF16)
     shares = pay_ref.shape[0]
     share = BLK // shares
     for j in range(shares):
         pay_ref[j, 0:share, :] = token[j * share : (j + 1) * share]
-        pay_ref[j, share : share + 16, :] = rest
+        pay_ref[j, share : share + 8, :] = rest
 
 
 def x_kernel(
@@ -426,11 +426,12 @@
 def patch_kernel(gx_ref, sides_ref, own_ref, spill_ref, out_ref, bc_ref):
     del gx_ref
     width = sides_ref.shape[1]
-    out_ref[...] = (sides_ref[8 + RIM :, :] + spill_ref[:, :width]).astype(BF16)
+    spill = jnp.concatenate([jnp.zeros((RIM - 8, width), F32), spill_ref[:, :width]], axis=0)
+    out_ref[...] = (sides_ref[8 + RIM :, :] + spill).astype(BF16)
     share = own_ref.shape[0]
     bc_ref[: share - 8, :] = own_ref[: share - 8, :]
     is_last = lax.axis_index("head") == lax.axis_size("head") - 1
-    came = spill_ref[RIM - 8 :, width:]
+    came = spill_ref[:, width:]
     bc_ref[share - 8 :, :] = own_ref[share - 8 :, :] + jnp.where(is_last, came, 0.0)
 
 
@@ -439,12 +440,12 @@
     total = jnp.sum(got_ref[...].astype(F32), axis=0)
     own_ref[...] = total[:share]
     width = sides_ref.shape[1]
-    out_ref[:, :width] = sides_ref[8 : 8 + RIM, :]
-    out_ref[: RIM - 8, width:] = jnp.zeros((RIM - 8, 256), F32)
-    out_ref[RIM - 8 :, width:] = total[share + 8 :]
-    sums_ref[:, :width] = sides_ref[:8, :]
-    sums_ref[:, width : width + 256] = total[share : share + 8]
-    sums_ref[:, width + 256 :] = gh_ref[...]
+    rest = total[share:]
+    out_ref[:, :width] = sides_ref[RIM : 8 + RIM, :]
+    out_ref[:, width:] = jnp.where(iota(rest.shape, 0) < 4, 0.0, rest)
+    sums_ref[:, :width] = sides_ref[:4, :]
+    sums_ref[:, width : width + 256] = rest[:4]
+    sums_ref[:, width + 256 :] = gh_ref[:4, :]
 
 
 def finish_kernel(a_ref, b_ref, c_ref, d_ref, wx_ref, wbc_ref, heads_ref):
@@ -482,26 +483,28 @@
 
 def passed_along(value, by):
     peers = lax.axis_size("ctx")
-    pairs = [(i, i + by) for i in range(peers) if 0 <= i + by < peers]
-    return lax.ppermute(value, "ctx", pairs)
+    return lax.ppermute(value, "ctx", [(i, (i + by) % peers) for i in range(peers)])
 
 
 def summed_over_ctx(value):
     peers = lax.axis_size("ctx")
 
-    def turned(value, stride):
-        def to(i, by):
-            at = i // stride % 4
-            return i + ((at + by) % 4 - at) * stride
-
-        return [value] + [
-            lax.ppermute(value, "ctx", [(i, to(i, by)) for i in range(peers)])
-            for by in (1, 2, 3)
-        ]
-
-    value = value + lax.ppermute(value, "ctx", [(i, i ^ 1) for i in range(peers)])
-    own, one, two, three = turned(value, 2)
-    return turned((own + one) + (two + three), 8)
+    def moved(value, to):
+        return lax.ppermute(value, "ctx", [(i, to(i)) for i in range(peers)])
+
+    def turned(i, stride, by):
+        at = i // stride % 4
+        return i + ((at + by) % 4 - at) * stride
+
+    def swap(i):
+        return i ^ 1
+
+    value = value + moved(value, swap)
+    one, two, three = [moved(value, lambda i, by=by: turned(i, 2, by)) for by in (1, 2, 3)]
+    value = (value + one) + (two + three)
+    near = moved(value, lambda i: turned(i, 8, 1 if i % 2 else 3))
+    far = moved(value, lambda i: turned(i, 8, 2))
+    return value, far, near, moved(near, swap)
 
 
 def cost(micros):
@@ -638,8 +641,8 @@
             one((peers, 64, NS)), one((2, channels, rows)), square, square,
             whole((2, 256, rows)), whole((256, 128)), row_spec,
         ],
-        out_specs=whole((shares, share + 16, 256)),
-        out_shape=shaped((shares, share + 16, 256), BF16),
+        out_specs=whole((shares, share + 8, 256)),
+        out_shape=shaped((shares, share + 8, 256), BF16),
         compiler_params=params,
         cost_estimate=cost(4),
         name="bc_part",
@@ -675,8 +678,8 @@
         in_specs=[vmem] * 3,
         out_specs=[vmem] * 3,
         out_shape=[
-            shaped((8, width), F32), shaped((share, 256), F32),
-            shaped((RIM, channels + 256), F32),
+            shaped((4, width), F32), shaped((share, 256), F32),
+            shaped((8, channels + 256), F32),
         ],
         compiler_params=params,
         cost_estimate=cost(1),
@@ -689,7 +692,7 @@
         grid=(1,),
         in_specs=[
             pl.BlockSpec(memory_space=pl.ANY), whole((side_rows, channels)), whole((share, 256)),
-            whole((RIM, channels + 256)),
+            whole((8, channels + 256)),
         ],
         out_specs=[
             pl.BlockSpec((RIM, channels), lambda i: (rows // RIM - 1, 0)), whole((share, 256)),

time: 90.9 us -> 88.4 us (0.972)
  starting transfers between devices: 34.7 us -> 32.4 us
    ppermute x9, starting transfers between devices: 14.1 us -> 12.2 us  [the longest x7 8.54 us: moved(): return lax.ppermute(value, 'ctx', [(i, to(i)) for i in range(peers)])]
    all_to_all x1, starting transfers between devices: 8.18 us -> 6.56 us  [local(): got_bc = lax.all_to_all(pay_bc, 'head', 0, 0, tiled=True)]
    all_to_all x1, starting transfers between devices: 8.32 us -> 9.58 us  [local(): got = lax.all_to_all(pay, 'ctx', 0, 0, tiled=True)]
    ppermute x9, waiting for transfers between devices: 6.02 us -> 7.24 us  [the longest x7 5.88 us: moved(): return lax.ppermute(value, 'ctx', [(i, to(i)) for i in range(peers)])]
  transfers between devices with their start and end apart: 12 -> 12, of which waited for: 10 -> 8; matrix products, arithmetic and copies ran while one was open for 0% -> 0% of each run, Pallas kernels for 24% -> 25%
where the time goes in v5:
time: 88.4 us; the launch traced here: 87.6 us
  Pallas kernels  34.8 us (39%)
  starting transfers between devices  32.4 us (37%)
  waiting for transfers between devices  19.6 us (22%)
    all_to_all x1, starting transfers between devices, local(): got = lax.all_to_all(pay, 'ctx', 0, 0, tiled=True)  9.58 us
    ppermute x7, starting transfers between devices, moved(): return lax.ppermute(value, 'ctx', [(i, to(i)) for i in range(peers)])  8.54 us
    pallas_call x1, Pallas kernels, local(): pl.pallas_call(slope_kernel, grid=(steps,), in_specs=[columns(rows), colu...  7.04 us
    pallas_call x1, Pallas kernels, local(): pl.pallas_call(x_kernel, grid=(steps,), in_specs=[state_spec, stack(3), s...  6.9 us
    pallas_call x1, Pallas kernels, local(): pl.pallas_call(state_kernel, grid=(steps,), in_specs=[columns(rows), colu...  6.58 us
    all_to_all x1, starting transfers between devices, local(): got_bc = lax.all_to_all(pay_bc, 'head', 0, 0, tiled=True)  6.56 us
    pallas_call x1, Pallas kernels, local(): pl.pallas_call(block_kernel, grid=(steps,), in_specs=[stack(2), columns(r...  6.13 us
    ppermute x7, waiting for transfers between devices, moved(): return lax.ppermute(value, 'ctx', [(i, to(i)) for i in range(peers)])  5.88 us
  transfers between devices with their start and end apart: 12, of which 8 were waited for; matrix products, arithmetic and copies ran while one was open for 0% of the time, Pallas kernels for 25%

profile of v5, /device:TPU:1, one launch (start us, length us, event | category | flops | bytes accessed | tf_op | source)
XLA Modules:
  0.0 87.6 jit_solution(14531076966131965952)
XLA Ops:
  0.6 0.8 rim_rows.1
  1.4 2.7 %collective-permute-start = (bf16[16,1280]{1,0:T(8,128)(2,1)S(1)}, bf16[16,1280]{1,0:T(8,128)(2,1)S(1)}, u32[]{:S(2)}, u32[]{:S(2)}) collective-permute-start(bf16[16,1280]{1,0:T(8,128)(2,1)S(1)} %rim_rows.1), channel_id=1, source_target_pairs={{0,8},{8,16},{16,24},{24,32},{32,40},{40,48},{48,56},{56,64},{64,7... | collective-permute-start | bytes 122888 | tf_op jit(solution)/shard_map/ppermute | solution.py:486
  4.1 1.4 %collective-permute-done.rim_ref.rimbc_ref = bf16[16,1280]{1,0:T(8,128)(2,1)S(1)} collective-permute-done((bf16[16,1280]{1,0:T(8,128)(2,1)S(1)}, bf16[16,1280]{1,0:T(8,128)(2,1)S(1)}, u32[]{:S(2)}, u32[]{:S(2)}) %collective-permute-start) | collective-permute-done | bytes 40992 | tf_op jit(solution)/shard_map/ppermute | solution.py:486
  5.5 6.6 %states.1 = (bf16[32,72,128]{2,1,0:T(8,128)(2,1)}, f32[8,16,256]{2,1,0:T(8,128)}, bf16[256,256]{1,0:T(8,128)(2,1)}) custom-call(bf16[256,1024]{1,0:T(8,128)(2,1)} %x_ref.5, bf16[16,1280]{1,0:T(8,128)(2,1)S(1)} %collective-permute-done.rim_ref.rimbc_ref, bf16[256,1024]{1,0:T(8,128)(2,1)} %gy_ref.5, f32[4,1024]{1,0:T(4,128)} %wx_ref.3, ...), custom_call_target="tpu_custom_call" | custom-call | flops 700000000 | bytes 21000000 | tf_op jit(solution)/shard_map/states/pallas_call | solution.py:552
  12.0 9.6 %all-to-all-start = ((bf16[32,72,128]{2,1,0:T(8,128)(2,1)}), bf16[32,72,128]{2,1,0:T(8,128)(2,1)S(1)}, u32[]{:S(2)}, u32[]{:S(2)}) async-start(bf16[32,72,128]{2,1,0:T(8,128)(2,1)} %get-tuple-element.35), calls=%async_computation | async-start | bytes 1179648 | tf_op jit(solution)/shard_map/all_to_all | solution.py:579
  21.6 7.0 %slopes.1 = (bf16[3,1024,256]{2,1,0:T(8,128)(2,1)}, f32[1024,256]{1,0:T(8,128)}, bf16[2,1024,256]{2,1,0:T(8,128)(2,1)}, f32[1024,128]{1,0:T(8,128)}, bf16[2,256,...) custom-call(bf16[256,1024]{1,0:T(8,128)(2,1)} %x_ref.5, bf16[16,1280]{1,0:T(8,128)(2,1)} %copy-done, ...), custom_call_target="tpu_custom_call" | custom-call | flops 600000000 | bytes 18000000 | tf_op jit(solution)/shard_map/slopes/pallas_call | solution.py:581
  28.7 5.3 %all-to-all-done.in_ref = bf16[32,72,128]{2,1,0:T(8,128)(2,1)S(1)} async-done(((bf16[32,72,128]{2,1,0:T(8,128)(2,1)}), bf16[32,72,128]{2,1,0:T(8,128)(2,1)S(1)}, u32[]{:S(2)}, u32[]{:S(2)}) %all-to-all-start) | async-done | bytes 589856 | tf_op jit(solution)/shard_map/all_to_all | solution.py:579
  34.0 1.0 %state_scan.1 = bf16[32,64,128]{2,1,0:T(8,128)(2,1)} custom-call(bf16[32,72,128]{2,1,0:T(8,128)(2,1)S(1)} %all-to-all-done.in_ref), custom_call_target="tpu_custom_call" | custom-call | flops 100000000 | bytes 3000000 | tf_op jit(solution)/shard_map/state_scan/pallas_call | solution.py:603
  34.9 4.1 %all-to-all-start.1 = ((bf16[32,64,128]{2,1,0:T(8,128)(2,1)}), bf16[32,64,128]{2,1,0:T(8,128)(2,1)S(1)}, u32[]{:S(2)}, u32[]{:S(2)}) async-start(bf16[32,64,128]{2,1,0:T(8,128)(2,1)} %state_scan.1), calls=%async_computation.1 | async-start | bytes 1048576 | tf_op jit(solution)/shard_map/all_to_all | solution.py:612
  39.0 6.1 %in_block.1 = (f32[3,1024,256]{2,1,0:T(8,128)}, f32[3,16,256]{2,1,0:T(8,128)}, f32[256,256]{1,0:T(8,128)}) custom-call(bf16[3,1024,256]{2,1,0:T(8,128)(2,1)} %get-tuple-element.39.low_ref, bf16[256,1024]{1,0:T(8,128)(2,1)} %gy_ref.5, f32[8,16,256]{2,1,0:T(8,128)} %get-tuple-element.36.rows_ref, bf16[256,256]{1,0:T(8,128)(2,1)} %get-tuple-element.40.bctok_ref, ...), custom_call_target="tpu_custom_call" | custom-call | flops 800000000 | bytes 24000000 | tf_op jit(solution)/shard_map/in_block/pallas_call | solution.py:614
  45.1 5.5 %all-to-all-done.1.state_ref = bf16[32,64,128]{2,1,0:T(8,128)(2,1)S(1)} async-done(((bf16[32,64,128]{2,1,0:T(8,128)(2,1)}), bf16[32,64,128]{2,1,0:T(8,128)(2,1)S(1)}, u32[]{:S(2)}, u32[]{:S(2)}) %all-to-all-start.1) | async-done | bytes 524320 | tf_op jit(solution)/shard_map/all_to_all | solution.py:612
  50.7 3.3 %bc_part.1 = bf16[8,40,256]{2,1,0:T(8,128)(2,1)} custom-call(bf16[32,64,128]{2,1,0:T(8,128)(2,1)S(1)} %all-to-all-done.1.state_ref, bf16[2,1024,256]{2,1,0:T(8,128)(2,1)} %get-tuple-element.49.scaled_ref, f32[256,256]{1,0:T(8,128)} %get-tuple-element.50.dbc_ref, f32[256,256]{1,0:T(8,128)} %get-tuple-element.51.bcslope_ref, ...), custom_call_target="tpu_custom_call" | custom-call | flops 400000000 | bytes 12000000 | tf_op jit(solution)/shard_map/bc_part/pallas_call | solution.py:637
  54.0 6.6 %all-to-all-start.2 = ((bf16[8,40,256]{2,1,0:T(8,128)(2,1)}), bf16[8,40,256]{2,1,0:T(8,128)(2,1)S(1)}, u32[]{:S(2)}, u32[]{:S(2)}) async-start(bf16[8,40,256]{2,1,0:T(8,128)(2,1)} %bc_part.1), calls=%async_computation.2 | async-start | bytes 327680 | tf_op jit(solution)/shard_map/all_to_all | solution.py:650
  60.5 6.9 %x_part.1 = (bf16[256,1024]{1,0:T(8,128)(2,1)}, bf16[256,1024]{1,0:T(8,128)(2,1)}, f32[40,1024]{1,0:T(8,128)}, f32[16,256]{1,0:T(8,128)}, f32[8,128]{1,0:T(8,128)}) custom-call(bf16[32,64,128]{2,1,0:T(8,128)(2,1)S(1)} %all-to-all-done.1.state_ref, bf16[3,1024,256]{2,1,0:T(8,128)(2,1)} %get-tuple-element.39.low_ref, ...), custom_call_target="tpu_custom_call" | custom-call | flops 1000000000 | bytes 30000000 | tf_op jit(solution)/shard_map/x_part/pallas_call | solution.py:653
  67.4 1.6 %all-to-all-done.2.got_ref = bf16[8,40,256]{2,1,0:T(8,128)(2,1)S(1)} async-done(((bf16[8,40,256]{2,1,0:T(8,128)(2,1)}), bf16[8,40,256]{2,1,0:T(8,128)(2,1)S(1)}, u32[]{:S(2)}, u32[]{:S(2)}) %all-to-all-start.2) | async-done | bytes 163872 | tf_op jit(solution)/shard_map/all_to_all | solution.py:650
  69.0 0.9 %pack_sums.1 = (f32[4,1408]{1,0:T(4,128)S(1)}, f32[32,256]{1,0:T(8,128)S(1)}, f32[8,1280]{1,0:T(8,128)S(1)}) custom-call(bf16[8,40,256]{2,1,0:T(8,128)(2,1)S(1)} %all-to-all-done.2.got_ref, f32[40,1024]{1,0:T(8,128)} %get-tuple-element.48.sides_ref, f32[8,128]{1,0:T(8,128)} %get-tuple-element.53.gh_ref), custom_call_target="tpu_custom_call" | custom-call | flops 100000000 | bytes 3000000 | tf_op jit(solution)/shard_map/pack_sums/pallas_call | solution.py:676
  69.9 2.3 %collective-permute-start.2 = (f32[4,1408]{1,0:T(4,128)S(1)}, f32[4,1408]{1,0:T(4,128)S(1)}, u32[]{:S(2)}, u32[]{:S(2)}) collective-permute-start(f32[4,1408]{1,0:T(4,128)S(1)} %get-tuple-element.59), channel_id=1, source_target_pairs={{0,8},{8,0},{16,24},{24,16},{32,40},{40,32},{48,56},{56,48},{64,72... | collective-permute-start | bytes 67592 | tf_op jit(solution)/shard_map/ppermute | solution.py:493
  72.3 0.8 collective-permute-done.2
  73.2 1.3 %collective-permute-start.5 = (f32[4,1408]{1,0:T(4,128)S(1)}, f32[4,1408]{1,0:T(4,128)S(1)}, u32[]{:S(2)}, u32[]{:S(2)}) collective-permute-start(f32[4,1408]{1,0:T(4,128)S(1)} %add.12), channel_id=1, source_target_pairs={{0,48},{8,56},{16,0},{24,8},{32,16},{40,24},{48,32},{56,40},{64,11... | collective-permute-start | bytes 67592 | tf_op jit(solution)/shard_map/ppermute | solution.py:493
  74.5 1.0 %collective-permute-start.4 = (f32[4,1408]{1,0:T(4,128)S(1)}, f32[4,1408]{1,0:T(4,128)S(1)}, u32[]{:S(2)}, u32[]{:S(2)}) collective-permute-start(f32[4,1408]{1,0:T(4,128)S(1)} %add.12), channel_id=1, source_target_pairs={{0,32},{8,40},{16,48},{24,56},{32,0},{40,8},{48,16},{56,24},{64,96... | collective-permute-start | bytes 67592 | tf_op jit(solution)/shard_map/ppermute | solution.py:493
  75.5 0.0 collective-permute-start.3
  75.5 1.0 %collective-permute-start.1 = (f32[8,1280]{1,0:T(8,128)S(1)}, f32[8,1280]{1,0:T(8,128)S(1)}, u32[]{:S(2)}, u32[]{:S(2)}) collective-permute-start(f32[8,1280]{1,0:T(8,128)S(1)} %get-tuple-element.55), channel_id=1, source_target_pairs={{0,248},{8,0},{16,8},{24,16},{32,24},{40,32},{48,40},{56,48},{64,5... | collective-permute-start | bytes 122888 | tf_op jit(solution)/shard_map/ppermute | solution.py:486
  76.5 0.0 collective-permute-done.5
  76.5 2.2 %collective-permute-done.4 = f32[4,1408]{1,0:T(4,128)S(1)} collective-permute-done((f32[4,1408]{1,0:T(4,128)S(1)}, f32[4,1408]{1,0:T(4,128)S(1)}, u32[]{:S(2)}, u32[]{:S(2)}) %collective-permute-start.4) | collective-permute-done | bytes 22560 | tf_op jit(solution)/shard_map/ppermute | solution.py:493
  78.6 1.0 %collective-permute-done.3 = f32[4,1408]{1,0:T(4,128)S(1)} collective-permute-done((f32[4,1408]{1,0:T(4,128)S(1)}, f32[4,1408]{1,0:T(4,128)S(1)}, u32[]{:S(2)}, u32[]{:S(2)}) %collective-permute-start.3) | collective-permute-done | bytes 22560 | tf_op jit(solution)/shard_map/ppermute | solution.py:493
  79.7 0.4 collective-permute-start.7
  80.1 1.7 %collective-permute-start.6 = (f32[4,1408]{1,0:T(4,128)S(1)}, f32[4,1408]{1,0:T(4,128)S(1)}, u32[]{:S(2)}, u32[]{:S(2)}) collective-permute-start(f32[4,1408]{1,0:T(4,128)S(1)} %add_add_fusion.a_ref), channel_id=1, source_target_pairs={{0,128},{8,136},{16,144},{24,152},{32,160},{40,168},{48,176},{56,1... | collective-permute-start | bytes 67592 | tf_op jit(solution)/shard_map/ppermute | solution.py:493
  81.8 1.8 %collective-permute-done.7.c_ref = f32[4,1408]{1,0:T(4,128)S(1)} collective-permute-done((f32[4,1408]{1,0:T(4,128)S(1)}, f32[4,1408]{1,0:T(4,128)S(1)}, u32[]{:S(2)}, u32[]{:S(2)}) %collective-permute-start.7) | collective-permute-done | bytes 22560 | tf_op jit(solution)/shard_map/ppermute | solution.py:493
  83.6 1.8 %collective-permute-start.8 = (f32[4,1408]{1,0:T(4,128)S(1)}, f32[4,1408]{1,0:T(4,128)S(1)}, u32[]{:S(2)}, u32[]{:S(2)}) collective-permute-start(f32[4,1408]{1,0:T(4,128)S(1)} %collective-permute-done.7.c_ref), channel_id=1, source_target_pairs={{0,8},{8,0},{16,24},{24,16},{32,40},{40,32},{48,56},{56,48},{64,72... | collective-permute-start | bytes 67592 | tf_op jit(solution)/shard_map/ppermute | solution.py:493
  85.4 0.0 collective-permute-done.1.spill_ref
  85.4 1.6 %last_rows.1 = (bf16[256,1024]{1,0:T(8,128)(2,1)}, f32[32,256]{1,0:T(8,128)}) custom-call(bf16[256,1024]{1,0:T(8,128)(2,1)} %get-tuple-element.47.gx_ref, f32[40,1024]{1,0:T(8,128)} %get-tuple-element.48.sides_ref, f32[32,256]{1,0:T(8,128)S(1)} %get-tuple-element.54.own_ref, ...), custom_call_target="tpu_custom_call", output_to_operand_aliasing={{0}: (0, {})} | custom-call | flops 100000000 | bytes 3000000 | tf_op jit(solution)/shard_map/last_rows/pallas_call | solution.py:690
  86.9 0.6 finish_sums.1
  (6 shorter events, 0.0 us)
Async XLA Ops:
  1.4 4.0 %collective-permute-start = (bf16[16,1280]{1,0:T(8,128)(2,1)S(1)}, bf16[16,1280]{1,0:T(8,128)(2,1)S(1)}, u32[]{:S(2)}, u32[]{:S(2)}) collective-permute-start(bf16[16,1280]{1,0:T(8,128)(2,1)S(1)} %rim_rows.1), channel_id=1, source_target_pairs={{0,8},{8,16},{16,24},{24,32},{32,40},{40,48},{48,56},{56,64},{64,7... | collective-permute-start | bytes 122888 | tf_op jit(solution)/shard_map/ppermute | solution.py:486
  5.5 16.2 %copy-start = (bf16[16,1280]{1,0:T(8,128)(2,1)}, bf16[16,1280]{1,0:T(8,128)(2,1)S(1)}, u32[]{:S(2)}) copy-start(bf16[16,1280]{1,0:T(8,128)(2,1)S(1)} %collective-permute-done.rim_ref.rimbc_ref) | copy-start | bytes 122884
  12.0 21.9 %all-to-all-start = ((bf16[32,72,128]{2,1,0:T(8,128)(2,1)}), bf16[32,72,128]{2,1,0:T(8,128)(2,1)S(1)}, u32[]{:S(2)}, u32[]{:S(2)}) async-start(bf16[32,72,128]{2,1,0:T(8,128)(2,1)} %get-tuple-element.35), calls=%async_computation | async-start | bytes 1179648 | tf_op jit(solution)/shard_map/all_to_all | solution.py:579
  34.9 15.7 %all-to-all-start.1 = ((bf16[32,64,128]{2,1,0:T(8,128)(2,1)}), bf16[32,64,128]{2,1,0:T(8,128)(2,1)S(1)}, u32[]{:S(2)}, u32[]{:S(2)}) async-start(bf16[32,64,128]{2,1,0:T(8,128)(2,1)} %state_scan.1), calls=%async_computation.1 | async-start | bytes 1048576 | tf_op jit(solution)/shard_map/all_to_all | solution.py:612
  54.0 15.0 %all-to-all-start.2 = ((bf16[8,40,256]{2,1,0:T(8,128)(2,1)}), bf16[8,40,256]{2,1,0:T(8,128)(2,1)S(1)}, u32[]{:S(2)}, u32[]{:S(2)}) async-start(bf16[8,40,256]{2,1,0:T(8,128)(2,1)} %bc_part.1), calls=%async_computation.2 | async-start | bytes 327680 | tf_op jit(solution)/shard_map/all_to_all | solution.py:650
  69.9 3.2 %collective-permute-start.2 = (f32[4,1408]{1,0:T(4,128)S(1)}, f32[4,1408]{1,0:T(4,128)S(1)}, u32[]{:S(2)}, u32[]{:S(2)}) collective-permute-start(f32[4,1408]{1,0:T(4,128)S(1)} %get-tuple-element.59), channel_id=1, source_target_pairs={{0,8},{8,0},{16,24},{24,16},{32,40},{40,32},{48,56},{56,48},{64,72... | collective-permute-start | bytes 67592 | tf_op jit(solution)/shard_map/ppermute | solution.py:493
  73.2 3.3 %collective-permute-start.5 = (f32[4,1408]{1,0:T(4,128)S(1)}, f32[4,1408]{1,0:T(4,128)S(1)}, u32[]{:S(2)}, u32[]{:S(2)}) collective-permute-start(f32[4,1408]{1,0:T(4,128)S(1)} %add.12), channel_id=1, source_target_pairs={{0,48},{8,56},{16,0},{24,8},{32,16},{40,24},{48,32},{56,40},{64,11... | collective-permute-start | bytes 67592 | tf_op jit(solution)/shard_map/ppermute | solution.py:493
  74.5 4.2 %collective-permute-start.4 = (f32[4,1408]{1,0:T(4,128)S(1)}, f32[4,1408]{1,0:T(4,128)S(1)}, u32[]{:S(2)}, u32[]{:S(2)}) collective-permute-start(f32[4,1408]{1,0:T(4,128)S(1)} %add.12), channel_id=1, source_target_pairs={{0,32},{8,40},{16,48},{24,56},{32,0},{40,8},{48,16},{56,24},{64,96... | collective-permute-start | bytes 67592 | tf_op jit(solution)/shard_map/ppermute | solution.py:493
  75.5 4.2 %collective-permute-start.3 = (f32[4,1408]{1,0:T(4,128)S(1)}, f32[4,1408]{1,0:T(4,128)S(1)}, u32[]{:S(2)}, u32[]{:S(2)}) collective-permute-start(f32[4,1408]{1,0:T(4,128)S(1)} %add.12), channel_id=1, source_target_pairs={{0,16},{8,24},{16,32},{24,40},{32,48},{40,56},{48,0},{56,8},{64,80... | collective-permute-start | bytes 67592 | tf_op jit(solution)/shard_map/ppermute | solution.py:493
  75.5 9.9 %collective-permute-start.1 = (f32[8,1280]{1,0:T(8,128)S(1)}, f32[8,1280]{1,0:T(8,128)S(1)}, u32[]{:S(2)}, u32[]{:S(2)}) collective-permute-start(f32[8,1280]{1,0:T(8,128)S(1)} %get-tuple-element.55), channel_id=1, source_target_pairs={{0,248},{8,0},{16,8},{24,16},{32,24},{40,32},{48,40},{56,48},{64,5... | collective-permute-start | bytes 122888 | tf_op jit(solution)/shard_map/ppermute | solution.py:486
  79.7 3.9 %collective-permute-start.7 = (f32[4,1408]{1,0:T(4,128)S(1)}, f32[4,1408]{1,0:T(4,128)S(1)}, u32[]{:S(2)}, u32[]{:S(2)}) collective-permute-start(f32[4,1408]{1,0:T(4,128)S(1)} %add_add_fusion.a_ref), channel_id=1, source_target_pairs={{0,192},{8,72},{16,208},{24,88},{32,224},{40,104},{48,240},{56,120... | collective-permute-start | bytes 67592 | tf_op jit(solution)/shard_map/ppermute | solution.py:493
  80.1 6.8 %collective-permute-start.6 = (f32[4,1408]{1,0:T(4,128)S(1)}, f32[4,1408]{1,0:T(4,128)S(1)}, u32[]{:S(2)}, u32[]{:S(2)}) collective-permute-start(f32[4,1408]{1,0:T(4,128)S(1)} %add_add_fusion.a_ref), channel_id=1, source_target_pairs={{0,128},{8,136},{16,144},{24,152},{32,160},{40,168},{48,176},{56,1... | collective-permute-start | bytes 67592 | tf_op jit(solution)/shard_map/ppermute | solution.py:493
  83.6 3.3 %collective-permute-start.8 = (f32[4,1408]{1,0:T(4,128)S(1)}, f32[4,1408]{1,0:T(4,128)S(1)}, u32[]{:S(2)}, u32[]{:S(2)}) collective-permute-start(f32[4,1408]{1,0:T(4,128)S(1)} %collective-permute-done.7.c_ref), channel_id=1, source_target_pairs={{0,8},{8,0},{16,24},{24,16},{32,40},{40,32},{48,56},{56,48},{64,72... | collective-permute-start | bytes 67592 | tf_op jit(solution)/shard_map/ppermute | solution.py:493

commit v6 on v5

--- a/solution.py
+++ b/solution.py
@@ -499,12 +499,14 @@
     def swap(i):
         return i ^ 1
 
+    def terms(value, stride):
+        near = moved(value, lambda i: turned(i, stride, 1 if i % 2 else 3))
+        far = moved(value, lambda i: turned(i, stride, 2))
+        return value, far, near, moved(near, swap)
+
     value = value + moved(value, swap)
-    one, two, three = [moved(value, lambda i, by=by: turned(i, 2, by)) for by in (1, 2, 3)]
-    value = (value + one) + (two + three)
-    near = moved(value, lambda i: turned(i, 8, 1 if i % 2 else 3))
-    far = moved(value, lambda i: turned(i, 8, 2))
-    return value, far, near, moved(near, swap)
+    own, far, near, other = terms(value, 2)
+    return terms((own + far) + (near + other), 8)
 
 
 def cost(micros):

time: 88.4 us -> 87.7 us (level)
  waiting for transfers between devices: 19.6 us -> 18.7 us
    ppermute x7, starting transfers between devices: 8.54 us -> 9.7 us  [moved(): return lax.ppermute(value, 'ctx', [(i, to(i)) for i in range(peers)])]
    ppermute x7, waiting for transfers between devices: 5.88 us -> 4.9 us  [moved(): return lax.ppermute(value, 'ctx', [(i, to(i)) for i in range(peers)])]
  transfers between devices with their start and end apart: 12 -> 12, of which waited for: 8 -> 9; matrix products, arithmetic and copies ran while one was open for 0% -> 0% of each run, Pallas kernels for 25% -> 25%
where the time goes in v6:
time: 87.7 us; the launch traced here: 86.9 us
  Pallas kernels  34.8 us (40%)
  starting transfers between devices  32.7 us (37%)
  waiting for transfers between devices  18.7 us (21%)
    ppermute x7, starting transfers between devices, moved(): return lax.ppermute(value, 'ctx', [(i, to(i)) for i in range(peers)])  9.7 us
    all_to_all x1, starting transfers between devices, local(): got = lax.all_to_all(pay, 'ctx', 0, 0, tiled=True)  9.58 us
    pallas_call x1, Pallas kernels, local(): pl.pallas_call(slope_kernel, grid=(steps,), in_specs=[columns(rows), colu...  7.04 us
    pallas_call x1, Pallas kernels, local(): pl.pallas_call(x_kernel, grid=(steps,), in_specs=[state_spec, stack(3), s...  6.9 us
    pallas_call x1, Pallas kernels, local(): pl.pallas_call(state_kernel, grid=(steps,), in_specs=[columns(rows), colu...  6.58 us
    all_to_all x1, starting transfers between devices, local(): got_bc = lax.all_to_all(pay_bc, 'head', 0, 0, tiled=True)  6.56 us
    pallas_call x1, Pallas kernels, local(): pl.pallas_call(block_kernel, grid=(steps,), in_specs=[stack(2), columns(r...  6.13 us
    all_to_all x1, waiting for transfers between devices, local(): states = lax.all_to_all(carried, 'ctx', 0, 0, tiled=True)  5.54 us
  transfers between devices with their start and end apart: 12, of which 9 were waited for; matrix products, arithmetic and copies ran while one was open for 0% of the time, Pallas kernels for 25%

profile of v6, /device:TPU:1, one launch (start us, length us, event | category | flops | bytes accessed | tf_op | source)
XLA Modules:
  0.0 86.9 jit_solution(11366555605472762258)
XLA Ops:
  0.6 0.8 rim_rows.1
  1.4 2.7 %collective-permute-start = (bf16[16,1280]{1,0:T(8,128)(2,1)S(1)}, bf16[16,1280]{1,0:T(8,128)(2,1)S(1)}, u32[]{:S(2)}, u32[]{:S(2)}) collective-permute-start(bf16[16,1280]{1,0:T(8,128)(2,1)S(1)} %rim_rows.1), channel_id=1, source_target_pairs={{0,8},{8,16},{16,24},{24,32},{32,40},{40,48},{48,56},{56,64},{64,7... | collective-permute-start | bytes 122888 | tf_op jit(solution)/shard_map/ppermute | solution.py:486
  4.1 1.4 %collective-permute-done.rim_ref.rimbc_ref = bf16[16,1280]{1,0:T(8,128)(2,1)S(1)} collective-permute-done((bf16[16,1280]{1,0:T(8,128)(2,1)S(1)}, bf16[16,1280]{1,0:T(8,128)(2,1)S(1)}, u32[]{:S(2)}, u32[]{:S(2)}) %collective-permute-start) | collective-permute-done | bytes 40992 | tf_op jit(solution)/shard_map/ppermute | solution.py:486
  5.5 6.6 %states.1 = (bf16[32,72,128]{2,1,0:T(8,128)(2,1)}, f32[8,16,256]{2,1,0:T(8,128)}, bf16[256,256]{1,0:T(8,128)(2,1)}) custom-call(bf16[256,1024]{1,0:T(8,128)(2,1)} %x_ref.5, bf16[16,1280]{1,0:T(8,128)(2,1)S(1)} %collective-permute-done.rim_ref.rimbc_ref, bf16[256,1024]{1,0:T(8,128)(2,1)} %gy_ref.5, f32[4,1024]{1,0:T(4,128)} %wx_ref.3, ...), custom_call_target="tpu_custom_call" | custom-call | flops 700000000 | bytes 21000000 | tf_op jit(solution)/shard_map/states/pallas_call | solution.py:554
  12.0 9.6 %all-to-all-start = ((bf16[32,72,128]{2,1,0:T(8,128)(2,1)}), bf16[32,72,128]{2,1,0:T(8,128)(2,1)S(1)}, u32[]{:S(2)}, u32[]{:S(2)}) async-start(bf16[32,72,128]{2,1,0:T(8,128)(2,1)} %get-tuple-element.35), calls=%async_computation | async-start | bytes 1179648 | tf_op jit(solution)/shard_map/all_to_all | solution.py:581
  21.6 7.0 %slopes.1 = (bf16[3,1024,256]{2,1,0:T(8,128)(2,1)}, f32[1024,256]{1,0:T(8,128)}, bf16[2,1024,256]{2,1,0:T(8,128)(2,1)}, f32[1024,128]{1,0:T(8,128)}, bf16[2,256,...) custom-call(bf16[256,1024]{1,0:T(8,128)(2,1)} %x_ref.5, bf16[16,1280]{1,0:T(8,128)(2,1)} %copy-done, ...), custom_call_target="tpu_custom_call" | custom-call | flops 600000000 | bytes 18000000 | tf_op jit(solution)/shard_map/slopes/pallas_call | solution.py:583
  28.7 5.3 %all-to-all-done.in_ref = bf16[32,72,128]{2,1,0:T(8,128)(2,1)S(1)} async-done(((bf16[32,72,128]{2,1,0:T(8,128)(2,1)}), bf16[32,72,128]{2,1,0:T(8,128)(2,1)S(1)}, u32[]{:S(2)}, u32[]{:S(2)}) %all-to-all-start) | async-done | bytes 589856 | tf_op jit(solution)/shard_map/all_to_all | solution.py:581
  34.0 1.0 %state_scan.1 = bf16[32,64,128]{2,1,0:T(8,128)(2,1)} custom-call(bf16[32,72,128]{2,1,0:T(8,128)(2,1)S(1)} %all-to-all-done.in_ref), custom_call_target="tpu_custom_call" | custom-call | flops 100000000 | bytes 3000000 | tf_op jit(solution)/shard_map/state_scan/pallas_call | solution.py:605
  34.9 4.1 %all-to-all-start.1 = ((bf16[32,64,128]{2,1,0:T(8,128)(2,1)}), bf16[32,64,128]{2,1,0:T(8,128)(2,1)S(1)}, u32[]{:S(2)}, u32[]{:S(2)}) async-start(bf16[32,64,128]{2,1,0:T(8,128)(2,1)} %state_scan.1), calls=%async_computation.1 | async-start | bytes 1048576 | tf_op jit(solution)/shard_map/all_to_all | solution.py:614
  39.0 6.1 %in_block.1 = (f32[3,1024,256]{2,1,0:T(8,128)}, f32[3,16,256]{2,1,0:T(8,128)}, f32[256,256]{1,0:T(8,128)}) custom-call(bf16[3,1024,256]{2,1,0:T(8,128)(2,1)} %get-tuple-element.39.low_ref, bf16[256,1024]{1,0:T(8,128)(2,1)} %gy_ref.5, f32[8,16,256]{2,1,0:T(8,128)} %get-tuple-element.36.rows_ref, bf16[256,256]{1,0:T(8,128)(2,1)} %get-tuple-element.40.bctok_ref, ...), custom_call_target="tpu_custom_call" | custom-call | flops 800000000 | bytes 24000000 | tf_op jit(solution)/shard_map/in_block/pallas_call | solution.py:616
  45.1 5.5 %all-to-all-done.1.state_ref = bf16[32,64,128]{2,1,0:T(8,128)(2,1)S(1)} async-done(((bf16[32,64,128]{2,1,0:T(8,128)(2,1)}), bf16[32,64,128]{2,1,0:T(8,128)(2,1)S(1)}, u32[]{:S(2)}, u32[]{:S(2)}) %all-to-all-start.1) | async-done | bytes 524320 | tf_op jit(solution)/shard_map/all_to_all | solution.py:614
  50.7 3.3 %bc_part.1 = bf16[8,40,256]{2,1,0:T(8,128)(2,1)} custom-call(bf16[32,64,128]{2,1,0:T(8,128)(2,1)S(1)} %all-to-all-done.1.state_ref, bf16[2,1024,256]{2,1,0:T(8,128)(2,1)} %get-tuple-element.49.scaled_ref, f32[256,256]{1,0:T(8,128)} %get-tuple-element.50.dbc_ref, f32[256,256]{1,0:T(8,128)} %get-tuple-element.51.bcslope_ref, ...), custom_call_target="tpu_custom_call" | custom-call | flops 400000000 | bytes 12000000 | tf_op jit(solution)/shard_map/bc_part/pallas_call | solution.py:639
  54.0 6.6 %all-to-all-start.2 = ((bf16[8,40,256]{2,1,0:T(8,128)(2,1)}), bf16[8,40,256]{2,1,0:T(8,128)(2,1)S(1)}, u32[]{:S(2)}, u32[]{:S(2)}) async-start(bf16[8,40,256]{2,1,0:T(8,128)(2,1)} %bc_part.1), calls=%async_computation.2 | async-start | bytes 327680 | tf_op jit(solution)/shard_map/all_to_all | solution.py:652
  60.5 6.9 %x_part.1 = (bf16[256,1024]{1,0:T(8,128)(2,1)}, bf16[256,1024]{1,0:T(8,128)(2,1)}, f32[40,1024]{1,0:T(8,128)}, f32[16,256]{1,0:T(8,128)}, f32[8,128]{1,0:T(8,128)}) custom-call(bf16[32,64,128]{2,1,0:T(8,128)(2,1)S(1)} %all-to-all-done.1.state_ref, bf16[3,1024,256]{2,1,0:T(8,128)(2,1)} %get-tuple-element.39.low_ref, ...), custom_call_target="tpu_custom_call" | custom-call | flops 1000000000 | bytes 30000000 | tf_op jit(solution)/shard_map/x_part/pallas_call | solution.py:655
  67.4 1.6 %all-to-all-done.2.got_ref = bf16[8,40,256]{2,1,0:T(8,128)(2,1)S(1)} async-done(((bf16[8,40,256]{2,1,0:T(8,128)(2,1)}), bf16[8,40,256]{2,1,0:T(8,128)(2,1)S(1)}, u32[]{:S(2)}, u32[]{:S(2)}) %all-to-all-start.2) | async-done | bytes 163872 | tf_op jit(solution)/shard_map/all_to_all | solution.py:652
  69.0 0.9 %pack_sums.1 = (f32[4,1408]{1,0:T(4,128)S(1)}, f32[32,256]{1,0:T(8,128)S(1)}, f32[8,1280]{1,0:T(8,128)S(1)}) custom-call(bf16[8,40,256]{2,1,0:T(8,128)(2,1)S(1)} %all-to-all-done.2.got_ref, f32[40,1024]{1,0:T(8,128)} %get-tuple-element.48.sides_ref, f32[8,128]{1,0:T(8,128)} %get-tuple-element.53.gh_ref), custom_call_target="tpu_custom_call" | custom-call | flops 100000000 | bytes 3000000 | tf_op jit(solution)/shard_map/pack_sums/pallas_call | solution.py:678
  69.9 2.3 %collective-permute-start.2 = (f32[4,1408]{1,0:T(4,128)S(1)}, f32[4,1408]{1,0:T(4,128)S(1)}, u32[]{:S(2)}, u32[]{:S(2)}) collective-permute-start(f32[4,1408]{1,0:T(4,128)S(1)} %get-tuple-element.59), channel_id=1, source_target_pairs={{0,8},{8,0},{16,24},{24,16},{32,40},{40,32},{48,56},{56,48},{64,72... | collective-permute-start | bytes 67592 | tf_op jit(solution)/shard_map/ppermute | solution.py:493
  72.3 0.8 collective-permute-done.2
  73.2 0.5 collective-permute-start.4
  73.7 2.0 %collective-permute-start.3 = (f32[4,1408]{1,0:T(4,128)S(1)}, f32[4,1408]{1,0:T(4,128)S(1)}, u32[]{:S(2)}, u32[]{:S(2)}) collective-permute-start(f32[4,1408]{1,0:T(4,128)S(1)} %add.12), channel_id=1, source_target_pairs={{0,32},{8,40},{16,48},{24,56},{32,0},{40,8},{48,16},{56,24},{64,96... | collective-permute-start | bytes 67592 | tf_op jit(solution)/shard_map/ppermute | solution.py:493
  75.7 1.3 %collective-permute-done.4 = f32[4,1408]{1,0:T(4,128)S(1)} collective-permute-done((f32[4,1408]{1,0:T(4,128)S(1)}, f32[4,1408]{1,0:T(4,128)S(1)}, u32[]{:S(2)}, u32[]{:S(2)}) %collective-permute-start.4) | collective-permute-done | bytes 22560 | tf_op jit(solution)/shard_map/ppermute | solution.py:493
  77.0 0.4 collective-permute-start.5
  77.4 0.2 collective-permute-start.1
  77.5 0.3 collective-permute-done.3
  77.9 0.4 collective-permute-done.5
  78.2 0.3 collective-permute-start.7
  78.5 1.7 %collective-permute-start.6 = (f32[4,1408]{1,0:T(4,128)S(1)}, f32[4,1408]{1,0:T(4,128)S(1)}, u32[]{:S(2)}, u32[]{:S(2)}) collective-permute-start(f32[4,1408]{1,0:T(4,128)S(1)} %add_add_fusion.a_ref), channel_id=1, source_target_pairs={{0,128},{8,136},{16,144},{24,152},{32,160},{40,168},{48,176},{56,1... | collective-permute-start | bytes 67592 | tf_op jit(solution)/shard_map/ppermute | solution.py:493
  80.2 2.0 %collective-permute-done.7.c_ref = f32[4,1408]{1,0:T(4,128)S(1)} collective-permute-done((f32[4,1408]{1,0:T(4,128)S(1)}, f32[4,1408]{1,0:T(4,128)S(1)}, u32[]{:S(2)}, u32[]{:S(2)}) %collective-permute-start.7) | collective-permute-done | bytes 22560 | tf_op jit(solution)/shard_map/ppermute | solution.py:493
  82.2 2.6 %collective-permute-start.8 = (f32[4,1408]{1,0:T(4,128)S(1)}, f32[4,1408]{1,0:T(4,128)S(1)}, u32[]{:S(2)}, u32[]{:S(2)}) collective-permute-start(f32[4,1408]{1,0:T(4,128)S(1)} %collective-permute-done.7.c_ref), channel_id=1, source_target_pairs={{0,8},{8,0},{16,24},{24,16},{32,40},{40,32},{48,56},{56,48},{64,72... | collective-permute-start | bytes 67592 | tf_op jit(solution)/shard_map/ppermute | solution.py:493
  84.7 0.0 collective-permute-done.1.spill_ref
  84.7 1.6 %last_rows.1 = (bf16[256,1024]{1,0:T(8,128)(2,1)}, f32[32,256]{1,0:T(8,128)}) custom-call(bf16[256,1024]{1,0:T(8,128)(2,1)} %get-tuple-element.47.gx_ref, f32[40,1024]{1,0:T(8,128)} %get-tuple-element.48.sides_ref, f32[32,256]{1,0:T(8,128)S(1)} %get-tuple-element.54.own_ref, ...), custom_call_target="tpu_custom_call", output_to_operand_aliasing={{0}: (0, {})} | custom-call | flops 100000000 | bytes 3000000 | tf_op jit(solution)/shard_map/last_rows/pallas_call | solution.py:692
  86.3 0.6 finish_sums.1
  (6 shorter events, 0.0 us)
Async XLA Ops:
  1.4 4.0 %collective-permute-start = (bf16[16,1280]{1,0:T(8,128)(2,1)S(1)}, bf16[16,1280]{1,0:T(8,128)(2,1)S(1)}, u32[]{:S(2)}, u32[]{:S(2)}) collective-permute-start(bf16[16,1280]{1,0:T(8,128)(2,1)S(1)} %rim_rows.1), channel_id=1, source_target_pairs={{0,8},{8,16},{16,24},{24,32},{32,40},{40,48},{48,56},{56,64},{64,7... | collective-permute-start | bytes 122888 | tf_op jit(solution)/shard_map/ppermute | solution.py:486
  5.5 16.2 %copy-start = (bf16[16,1280]{1,0:T(8,128)(2,1)}, bf16[16,1280]{1,0:T(8,128)(2,1)S(1)}, u32[]{:S(2)}) copy-start(bf16[16,1280]{1,0:T(8,128)(2,1)S(1)} %collective-permute-done.rim_ref.rimbc_ref) | copy-start | bytes 122884
  12.0 21.9 %all-to-all-start = ((bf16[32,72,128]{2,1,0:T(8,128)(2,1)}), bf16[32,72,128]{2,1,0:T(8,128)(2,1)S(1)}, u32[]{:S(2)}, u32[]{:S(2)}) async-start(bf16[32,72,128]{2,1,0:T(8,128)(2,1)} %get-tuple-element.35), calls=%async_computation | async-start | bytes 1179648 | tf_op jit(solution)/shard_map/all_to_all | solution.py:581
  34.9 15.7 %all-to-all-start.1 = ((bf16[32,64,128]{2,1,0:T(8,128)(2,1)}), bf16[32,64,128]{2,1,0:T(8,128)(2,1)S(1)}, u32[]{:S(2)}, u32[]{:S(2)}) async-start(bf16[32,64,128]{2,1,0:T(8,128)(2,1)} %state_scan.1), calls=%async_computation.1 | async-start | bytes 1048576 | tf_op jit(solution)/shard_map/all_to_all | solution.py:614
  54.0 15.0 %all-to-all-start.2 = ((bf16[8,40,256]{2,1,0:T(8,128)(2,1)}), bf16[8,40,256]{2,1,0:T(8,128)(2,1)S(1)}, u32[]{:S(2)}, u32[]{:S(2)}) async-start(bf16[8,40,256]{2,1,0:T(8,128)(2,1)} %bc_part.1), calls=%async_computation.2 | async-start | bytes 327680 | tf_op jit(solution)/shard_map/all_to_all | solution.py:652
  69.9 3.2 %collective-permute-start.2 = (f32[4,1408]{1,0:T(4,128)S(1)}, f32[4,1408]{1,0:T(4,128)S(1)}, u32[]{:S(2)}, u32[]{:S(2)}) collective-permute-start(f32[4,1408]{1,0:T(4,128)S(1)} %get-tuple-element.59), channel_id=1, source_target_pairs={{0,8},{8,0},{16,24},{24,16},{32,40},{40,32},{48,56},{56,48},{64,72... | collective-permute-start | bytes 67592 | tf_op jit(solution)/shard_map/ppermute | solution.py:493
  73.2 3.9 %collective-permute-start.4 = (f32[4,1408]{1,0:T(4,128)S(1)}, f32[4,1408]{1,0:T(4,128)S(1)}, u32[]{:S(2)}, u32[]{:S(2)}) collective-permute-start(f32[4,1408]{1,0:T(4,128)S(1)} %add.12), channel_id=1, source_target_pairs={{0,48},{8,24},{16,0},{24,40},{32,16},{40,56},{48,32},{56,8},{64,11... | collective-permute-start | bytes 67592 | tf_op jit(solution)/shard_map/ppermute | solution.py:493
  73.7 4.2 %collective-permute-start.3 = (f32[4,1408]{1,0:T(4,128)S(1)}, f32[4,1408]{1,0:T(4,128)S(1)}, u32[]{:S(2)}, u32[]{:S(2)}) collective-permute-start(f32[4,1408]{1,0:T(4,128)S(1)} %add.12), channel_id=1, source_target_pairs={{0,32},{8,40},{16,48},{24,56},{32,0},{40,8},{48,16},{56,24},{64,96... | collective-permute-start | bytes 67592 | tf_op jit(solution)/shard_map/ppermute | solution.py:493
  77.0 1.2 %collective-permute-start.5 = (f32[4,1408]{1,0:T(4,128)S(1)}, f32[4,1408]{1,0:T(4,128)S(1)}, u32[]{:S(2)}, u32[]{:S(2)}) collective-permute-start(f32[4,1408]{1,0:T(4,128)S(1)} %collective-permute-done.4), channel_id=1, source_target_pairs={{0,8},{8,0},{16,24},{24,16},{32,40},{40,32},{48,56},{56,48},{64,72... | collective-permute-start | bytes 67592 | tf_op jit(solution)/shard_map/ppermute | solution.py:493
  77.4 7.4 %collective-permute-start.1 = (f32[8,1280]{1,0:T(8,128)S(1)}, f32[8,1280]{1,0:T(8,128)S(1)}, u32[]{:S(2)}, u32[]{:S(2)}) collective-permute-start(f32[8,1280]{1,0:T(8,128)S(1)} %get-tuple-element.55), channel_id=1, source_target_pairs={{0,248},{8,0},{16,8},{24,16},{32,24},{40,32},{48,40},{56,48},{64,5... | collective-permute-start | bytes 122888 | tf_op jit(solution)/shard_map/ppermute | solution.py:486
  78.2 3.9 %collective-permute-start.7 = (f32[4,1408]{1,0:T(4,128)S(1)}, f32[4,1408]{1,0:T(4,128)S(1)}, u32[]{:S(2)}, u32[]{:S(2)}) collective-permute-start(f32[4,1408]{1,0:T(4,128)S(1)} %add_add_fusion.a_ref), channel_id=1, source_target_pairs={{0,192},{8,72},{16,208},{24,88},{32,224},{40,104},{48,240},{56,120... | collective-permute-start | bytes 67592 | tf_op jit(solution)/shard_map/ppermute | solution.py:493
  78.5 7.8 %collective-permute-start.6 = (f32[4,1408]{1,0:T(4,128)S(1)}, f32[4,1408]{1,0:T(4,128)S(1)}, u32[]{:S(2)}, u32[]{:S(2)}) collective-permute-start(f32[4,1408]{1,0:T(4,128)S(1)} %add_add_fusion.a_ref), channel_id=1, source_target_pairs={{0,128},{8,136},{16,144},{24,152},{32,160},{40,168},{48,176},{56,1... | collective-permute-start | bytes 67592 | tf_op jit(solution)/shard_map/ppermute | solution.py:493
  82.2 4.1 %collective-permute-start.8 = (f32[4,1408]{1,0:T(4,128)S(1)}, f32[4,1408]{1,0:T(4,128)S(1)}, u32[]{:S(2)}, u32[]{:S(2)}) collective-permute-start(f32[4,1408]{1,0:T(4,128)S(1)} %collective-permute-done.7.c_ref), channel_id=1, source_target_pairs={{0,8},{8,0},{16,24},{24,16},{32,40},{40,32},{48,56},{56,48},{64,72... | collective-permute-start | bytes 67592 | tf_op jit(solution)/shard_map/ppermute | solution.py:493

commit v7 on v6

--- a/solution.py
+++ b/solution.py
@@ -353,7 +353,7 @@
     grad_act = dbc_ref[...] + jnp.concatenate([grad_b, grad_c], axis=0)
     grad, sides = conv_back(
         grad_act * bcslope_ref[...], bclow_ref[0].astype(F32), bcsides_ref[...],
-        bcsides_ref[...], masks_of(rows_ref),
+        bcsides_ref[...], [rows_ref[0, k : k + 1, :] for k in range(4)],
     )
     token = mm_nt(eye(BLK, BF16), grad.astype(BF16)).astype(BF16)
     row = iota((8, 128), 0)
@@ -641,7 +641,8 @@
         grid=(1,),
         in_specs=[
             one((peers, 64, NS)), one((2, channels, rows)), square, square,
-            whole((2, 256, rows)), whole((256, 128)), row_spec,
+            one((1, 256, rows)), whole((256, 128)),
+            pl.BlockSpec((1, heads, rows), lambda i: (MASK, 0, 0)),
         ],
         out_specs=whole((shares, share + 8, 256)),
         out_shape=shaped((shares, share + 8, 256), BF16),

time: 87.7 us -> 87.7 us (level)
  no operation moved by 1% of the time
where the time goes in v7:
time: 87.7 us; the launch traced here: 86.9 us
  Pallas kernels  34.7 us (40%)
  starting transfers between devices  32.7 us (37%)
  waiting for transfers between devices  18.7 us (21%)
    ppermute x7, starting transfers between devices, moved(): return lax.ppermute(value, 'ctx', [(i, to(i)) for i in range(peers)])  9.71 us
    all_to_all x1, starting transfers between devices, local(): got = lax.all_to_all(pay, 'ctx', 0, 0, tiled=True)  9.58 us
    pallas_call x1, Pallas kernels, local(): pl.pallas_call(slope_kernel, grid=(steps,), in_specs=[columns(rows), colu...  7.04 us
    pallas_call x1, Pallas kernels, local(): pl.pallas_call(x_kernel, grid=(steps,), in_specs=[state_spec, stack(3), s...  6.89 us
    pallas_call x1, Pallas kernels, local(): pl.pallas_call(state_kernel, grid=(steps,), in_specs=[columns(rows), colu...  6.58 us
    all_to_all x1, starting transfers between devices, local(): got_bc = lax.all_to_all(pay_bc, 'head', 0, 0, tiled=True)  6.56 us
    pallas_call x1, Pallas kernels, local(): pl.pallas_call(block_kernel, grid=(steps,), in_specs=[stack(2), columns(r...  6.13 us
    all_to_all x1, waiting for transfers between devices, local(): states = lax.all_to_all(carried, 'ctx', 0, 0, tiled=True)  5.54 us
  transfers between devices with their start and end apart: 12, of which 9 were waited for; matrix products, arithmetic and copies ran while one was open for 0% of the time, Pallas kernels for 25%

profile of v7, /device:TPU:1, one launch (start us, length us, event | category | flops | bytes accessed | tf_op | source)
XLA Modules:
  0.0 86.9 jit_solution(8434356459102141669)
XLA Ops:
  0.6 0.8 rim_rows.1
  1.4 2.7 %collective-permute-start = (bf16[16,1280]{1,0:T(8,128)(2,1)S(1)}, bf16[16,1280]{1,0:T(8,128)(2,1)S(1)}, u32[]{:S(2)}, u32[]{:S(2)}) collective-permute-start(bf16[16,1280]{1,0:T(8,128)(2,1)S(1)} %rim_rows.1), channel_id=1, source_target_pairs={{0,8},{8,16},{16,24},{24,32},{32,40},{40,48},{48,56},{56,64},{64,7... | collective-permute-start | bytes 122888 | tf_op jit(solution)/shard_map/ppermute | solution.py:486
  4.1 1.4 %collective-permute-done.rim_ref.rimbc_ref = bf16[16,1280]{1,0:T(8,128)(2,1)S(1)} collective-permute-done((bf16[16,1280]{1,0:T(8,128)(2,1)S(1)}, bf16[16,1280]{1,0:T(8,128)(2,1)S(1)}, u32[]{:S(2)}, u32[]{:S(2)}) %collective-permute-start) | collective-permute-done | bytes 40992 | tf_op jit(solution)/shard_map/ppermute | solution.py:486
  5.5 6.6 %states.1 = (bf16[32,72,128]{2,1,0:T(8,128)(2,1)}, f32[8,16,256]{2,1,0:T(8,128)}, bf16[256,256]{1,0:T(8,128)(2,1)}) custom-call(bf16[256,1024]{1,0:T(8,128)(2,1)} %x_ref.5, bf16[16,1280]{1,0:T(8,128)(2,1)S(1)} %collective-permute-done.rim_ref.rimbc_ref, bf16[256,1024]{1,0:T(8,128)(2,1)} %gy_ref.5, f32[4,1024]{1,0:T(4,128)} %wx_ref.3, ...), custom_call_target="tpu_custom_call" | custom-call | flops 700000000 | bytes 21000000 | tf_op jit(solution)/shard_map/states/pallas_call | solution.py:554
  12.0 9.6 %all-to-all-start = ((bf16[32,72,128]{2,1,0:T(8,128)(2,1)}), bf16[32,72,128]{2,1,0:T(8,128)(2,1)S(1)}, u32[]{:S(2)}, u32[]{:S(2)}) async-start(bf16[32,72,128]{2,1,0:T(8,128)(2,1)} %get-tuple-element.35), calls=%async_computation | async-start | bytes 1179648 | tf_op jit(solution)/shard_map/all_to_all | solution.py:581
  21.6 7.0 %slopes.1 = (bf16[3,1024,256]{2,1,0:T(8,128)(2,1)}, f32[1024,256]{1,0:T(8,128)}, bf16[2,1024,256]{2,1,0:T(8,128)(2,1)}, f32[1024,128]{1,0:T(8,128)}, bf16[2,256,...) custom-call(bf16[256,1024]{1,0:T(8,128)(2,1)} %x_ref.5, bf16[16,1280]{1,0:T(8,128)(2,1)} %copy-done, ...), custom_call_target="tpu_custom_call" | custom-call | flops 600000000 | bytes 18000000 | tf_op jit(solution)/shard_map/slopes/pallas_call | solution.py:583
  28.7 5.3 %all-to-all-done.in_ref = bf16[32,72,128]{2,1,0:T(8,128)(2,1)S(1)} async-done(((bf16[32,72,128]{2,1,0:T(8,128)(2,1)}), bf16[32,72,128]{2,1,0:T(8,128)(2,1)S(1)}, u32[]{:S(2)}, u32[]{:S(2)}) %all-to-all-start) | async-done | bytes 589856 | tf_op jit(solution)/shard_map/all_to_all | solution.py:581
  34.0 1.0 %state_scan.1 = bf16[32,64,128]{2,1,0:T(8,128)(2,1)} custom-call(bf16[32,72,128]{2,1,0:T(8,128)(2,1)S(1)} %all-to-all-done.in_ref), custom_call_target="tpu_custom_call" | custom-call | flops 100000000 | bytes 3000000 | tf_op jit(solution)/shard_map/state_scan/pallas_call | solution.py:605
  34.9 4.1 %all-to-all-start.1 = ((bf16[32,64,128]{2,1,0:T(8,128)(2,1)}), bf16[32,64,128]{2,1,0:T(8,128)(2,1)S(1)}, u32[]{:S(2)}, u32[]{:S(2)}) async-start(bf16[32,64,128]{2,1,0:T(8,128)(2,1)} %state_scan.1), calls=%async_computation.1 | async-start | bytes 1048576 | tf_op jit(solution)/shard_map/all_to_all | solution.py:614
  39.0 6.1 %in_block.1 = (f32[3,1024,256]{2,1,0:T(8,128)}, f32[3,16,256]{2,1,0:T(8,128)}, f32[256,256]{1,0:T(8,128)}) custom-call(bf16[3,1024,256]{2,1,0:T(8,128)(2,1)} %get-tuple-element.39.low_ref, bf16[256,1024]{1,0:T(8,128)(2,1)} %gy_ref.5, f32[8,16,256]{2,1,0:T(8,128)} %get-tuple-element.36.rows_ref, bf16[256,256]{1,0:T(8,128)(2,1)} %get-tuple-element.40.bctok_ref, ...), custom_call_target="tpu_custom_call" | custom-call | flops 800000000 | bytes 24000000 | tf_op jit(solution)/shard_map/in_block/pallas_call | solution.py:616
  45.1 5.5 %all-to-all-done.1.state_ref = bf16[32,64,128]{2,1,0:T(8,128)(2,1)S(1)} async-done(((bf16[32,64,128]{2,1,0:T(8,128)(2,1)}), bf16[32,64,128]{2,1,0:T(8,128)(2,1)S(1)}, u32[]{:S(2)}, u32[]{:S(2)}) %all-to-all-start.1) | async-done | bytes 524320 | tf_op jit(solution)/shard_map/all_to_all | solution.py:614
  50.7 3.3 %bc_part.1 = bf16[8,40,256]{2,1,0:T(8,128)(2,1)} custom-call(bf16[32,64,128]{2,1,0:T(8,128)(2,1)S(1)} %all-to-all-done.1.state_ref, bf16[2,1024,256]{2,1,0:T(8,128)(2,1)} %get-tuple-element.49.scaled_ref, f32[256,256]{1,0:T(8,128)} %get-tuple-element.50.dbc_ref, f32[256,256]{1,0:T(8,128)} %get-tuple-element.51.bcslope_ref, ...), custom_call_target="tpu_custom_call" | custom-call | flops 400000000 | bytes 12000000 | tf_op jit(solution)/shard_map/bc_part/pallas_call | solution.py:639
  53.9 6.6 %all-to-all-start.2 = ((bf16[8,40,256]{2,1,0:T(8,128)(2,1)}), bf16[8,40,256]{2,1,0:T(8,128)(2,1)S(1)}, u32[]{:S(2)}, u32[]{:S(2)}) async-start(bf16[8,40,256]{2,1,0:T(8,128)(2,1)} %bc_part.1), calls=%async_computation.2 | async-start | bytes 327680 | tf_op jit(solution)/shard_map/all_to_all | solution.py:653
  60.5 6.9 %x_part.1 = (bf16[256,1024]{1,0:T(8,128)(2,1)}, bf16[256,1024]{1,0:T(8,128)(2,1)}, f32[40,1024]{1,0:T(8,128)}, f32[16,256]{1,0:T(8,128)}, f32[8,128]{1,0:T(8,128)}) custom-call(bf16[32,64,128]{2,1,0:T(8,128)(2,1)S(1)} %all-to-all-done.1.state_ref, bf16[3,1024,256]{2,1,0:T(8,128)(2,1)} %get-tuple-element.39.low_ref, ...), custom_call_target="tpu_custom_call" | custom-call | flops 1000000000 | bytes 30000000 | tf_op jit(solution)/shard_map/x_part/pallas_call | solution.py:656
  67.4 1.6 %all-to-all-done.2.got_ref = bf16[8,40,256]{2,1,0:T(8,128)(2,1)S(1)} async-done(((bf16[8,40,256]{2,1,0:T(8,128)(2,1)}), bf16[8,40,256]{2,1,0:T(8,128)(2,1)S(1)}, u32[]{:S(2)}, u32[]{:S(2)}) %all-to-all-start.2) | async-done | bytes 163872 | tf_op jit(solution)/shard_map/all_to_all | solution.py:653
  69.0 0.9 %pack_sums.1 = (f32[4,1408]{1,0:T(4,128)S(1)}, f32[32,256]{1,0:T(8,128)S(1)}, f32[8,1280]{1,0:T(8,128)S(1)}) custom-call(bf16[8,40,256]{2,1,0:T(8,128)(2,1)S(1)} %all-to-all-done.2.got_ref, f32[40,1024]{1,0:T(8,128)} %get-tuple-element.48.sides_ref, f32[8,128]{1,0:T(8,128)} %get-tuple-element.53.gh_ref), custom_call_target="tpu_custom_call" | custom-call | flops 100000000 | bytes 3000000 | tf_op jit(solution)/shard_map/pack_sums/pallas_call | solution.py:679
  69.9 2.3 %collective-permute-start.2 = (f32[4,1408]{1,0:T(4,128)S(1)}, f32[4,1408]{1,0:T(4,128)S(1)}, u32[]{:S(2)}, u32[]{:S(2)}) collective-permute-start(f32[4,1408]{1,0:T(4,128)S(1)} %get-tuple-element.59), channel_id=1, source_target_pairs={{0,8},{8,0},{16,24},{24,16},{32,40},{40,32},{48,56},{56,48},{64,72... | collective-permute-start | bytes 67592 | tf_op jit(solution)/shard_map/ppermute | solution.py:493
  72.2 0.8 collective-permute-done.2
  73.1 0.5 collective-permute-start.4
  73.6 2.0 %collective-permute-start.3 = (f32[4,1408]{1,0:T(4,128)S(1)}, f32[4,1408]{1,0:T(4,128)S(1)}, u32[]{:S(2)}, u32[]{:S(2)}) collective-permute-start(f32[4,1408]{1,0:T(4,128)S(1)} %add.12), channel_id=1, source_target_pairs={{0,32},{8,40},{16,48},{24,56},{32,0},{40,8},{48,16},{56,24},{64,96... | collective-permute-start | bytes 67592 | tf_op jit(solution)/shard_map/ppermute | solution.py:493
  75.6 1.3 %collective-permute-done.4 = f32[4,1408]{1,0:T(4,128)S(1)} collective-permute-done((f32[4,1408]{1,0:T(4,128)S(1)}, f32[4,1408]{1,0:T(4,128)S(1)}, u32[]{:S(2)}, u32[]{:S(2)}) %collective-permute-start.4) | collective-permute-done | bytes 22560 | tf_op jit(solution)/shard_map/ppermute | solution.py:493
  77.0 0.4 collective-permute-start.5
  77.3 0.2 collective-permute-start.1
  77.5 0.3 collective-permute-done.3
  77.8 0.4 collective-permute-done.5
  78.2 0.3 collective-permute-start.7
  78.4 1.7 %collective-permute-start.6 = (f32[4,1408]{1,0:T(4,128)S(1)}, f32[4,1408]{1,0:T(4,128)S(1)}, u32[]{:S(2)}, u32[]{:S(2)}) collective-permute-start(f32[4,1408]{1,0:T(4,128)S(1)} %add_add_fusion.a_ref), channel_id=1, source_target_pairs={{0,128},{8,136},{16,144},{24,152},{32,160},{40,168},{48,176},{56,1... | collective-permute-start | bytes 67592 | tf_op jit(solution)/shard_map/ppermute | solution.py:493
  80.1 2.0 %collective-permute-done.7.c_ref = f32[4,1408]{1,0:T(4,128)S(1)} collective-permute-done((f32[4,1408]{1,0:T(4,128)S(1)}, f32[4,1408]{1,0:T(4,128)S(1)}, u32[]{:S(2)}, u32[]{:S(2)}) %collective-permute-start.7) | collective-permute-done | bytes 22560 | tf_op jit(solution)/shard_map/ppermute | solution.py:493
  82.1 2.6 %collective-permute-start.8 = (f32[4,1408]{1,0:T(4,128)S(1)}, f32[4,1408]{1,0:T(4,128)S(1)}, u32[]{:S(2)}, u32[]{:S(2)}) collective-permute-start(f32[4,1408]{1,0:T(4,128)S(1)} %collective-permute-done.7.c_ref), channel_id=1, source_target_pairs={{0,8},{8,0},{16,24},{24,16},{32,40},{40,32},{48,56},{56,48},{64,72... | collective-permute-start | bytes 67592 | tf_op jit(solution)/shard_map/ppermute | solution.py:493
  84.7 0.0 collective-permute-done.1.spill_ref
  84.7 1.6 %last_rows.1 = (bf16[256,1024]{1,0:T(8,128)(2,1)}, f32[32,256]{1,0:T(8,128)}) custom-call(bf16[256,1024]{1,0:T(8,128)(2,1)} %get-tuple-element.47.gx_ref, f32[40,1024]{1,0:T(8,128)} %get-tuple-element.48.sides_ref, f32[32,256]{1,0:T(8,128)S(1)} %get-tuple-element.54.own_ref, ...), custom_call_target="tpu_custom_call", output_to_operand_aliasing={{0}: (0, {})} | custom-call | flops 100000000 | bytes 3000000 | tf_op jit(solution)/shard_map/last_rows/pallas_call | solution.py:693
  86.2 0.6 finish_sums.1
  (6 shorter events, 0.0 us)
Async XLA Ops:
  1.4 4.0 %collective-permute-start = (bf16[16,1280]{1,0:T(8,128)(2,1)S(1)}, bf16[16,1280]{1,0:T(8,128)(2,1)S(1)}, u32[]{:S(2)}, u32[]{:S(2)}) collective-permute-start(bf16[16,1280]{1,0:T(8,128)(2,1)S(1)} %rim_rows.1), channel_id=1, source_target_pairs={{0,8},{8,16},{16,24},{24,32},{32,40},{40,48},{48,56},{56,64},{64,7... | collective-permute-start | bytes 122888 | tf_op jit(solution)/shard_map/ppermute | solution.py:486
  5.5 16.2 %copy-start = (bf16[16,1280]{1,0:T(8,128)(2,1)}, bf16[16,1280]{1,0:T(8,128)(2,1)S(1)}, u32[]{:S(2)}) copy-start(bf16[16,1280]{1,0:T(8,128)(2,1)S(1)} %collective-permute-done.rim_ref.rimbc_ref) | copy-start | bytes 122884
  12.0 21.9 %all-to-all-start = ((bf16[32,72,128]{2,1,0:T(8,128)(2,1)}), bf16[32,72,128]{2,1,0:T(8,128)(2,1)S(1)}, u32[]{:S(2)}, u32[]{:S(2)}) async-start(bf16[32,72,128]{2,1,0:T(8,128)(2,1)} %get-tuple-element.35), calls=%async_computation | async-start | bytes 1179648 | tf_op jit(solution)/shard_map/all_to_all | solution.py:581
  34.9 15.7 %all-to-all-start.1 = ((bf16[32,64,128]{2,1,0:T(8,128)(2,1)}), bf16[32,64,128]{2,1,0:T(8,128)(2,1)S(1)}, u32[]{:S(2)}, u32[]{:S(2)}) async-start(bf16[32,64,128]{2,1,0:T(8,128)(2,1)} %state_scan.1), calls=%async_computation.1 | async-start | bytes 1048576 | tf_op jit(solution)/shard_map/all_to_all | solution.py:614
  53.9 15.0 %all-to-all-start.2 = ((bf16[8,40,256]{2,1,0:T(8,128)(2,1)}), bf16[8,40,256]{2,1,0:T(8,128)(2,1)S(1)}, u32[]{:S(2)}, u32[]{:S(2)}) async-start(bf16[8,40,256]{2,1,0:T(8,128)(2,1)} %bc_part.1), calls=%async_computation.2 | async-start | bytes 327680 | tf_op jit(solution)/shard_map/all_to_all | solution.py:653
  69.9 3.2 %collective-permute-start.2 = (f32[4,1408]{1,0:T(4,128)S(1)}, f32[4,1408]{1,0:T(4,128)S(1)}, u32[]{:S(2)}, u32[]{:S(2)}) collective-permute-start(f32[4,1408]{1,0:T(4,128)S(1)} %get-tuple-element.59), channel_id=1, source_target_pairs={{0,8},{8,0},{16,24},{24,16},{32,40},{40,32},{48,56},{56,48},{64,72... | collective-permute-start | bytes 67592 | tf_op jit(solution)/shard_map/ppermute | solution.py:493
  73.1 3.9 %collective-permute-start.4 = (f32[4,1408]{1,0:T(4,128)S(1)}, f32[4,1408]{1,0:T(4,128)S(1)}, u32[]{:S(2)}, u32[]{:S(2)}) collective-permute-start(f32[4,1408]{1,0:T(4,128)S(1)} %add.12), channel_id=1, source_target_pairs={{0,48},{8,24},{16,0},{24,40},{32,16},{40,56},{48,32},{56,8},{64,11... | collective-permute-start | bytes 67592 | tf_op jit(solution)/shard_map/ppermute | solution.py:493
  73.6 4.2 %collective-permute-start.3 = (f32[4,1408]{1,0:T(4,128)S(1)}, f32[4,1408]{1,0:T(4,128)S(1)}, u32[]{:S(2)}, u32[]{:S(2)}) collective-permute-start(f32[4,1408]{1,0:T(4,128)S(1)} %add.12), channel_id=1, source_target_pairs={{0,32},{8,40},{16,48},{24,56},{32,0},{40,8},{48,16},{56,24},{64,96... | collective-permute-start | bytes 67592 | tf_op jit(solution)/shard_map/ppermute | solution.py:493
  77.0 1.2 %collective-permute-start.5 = (f32[4,1408]{1,0:T(4,128)S(1)}, f32[4,1408]{1,0:T(4,128)S(1)}, u32[]{:S(2)}, u32[]{:S(2)}) collective-permute-start(f32[4,1408]{1,0:T(4,128)S(1)} %collective-permute-done.4), channel_id=1, source_target_pairs={{0,8},{8,0},{16,24},{24,16},{32,40},{40,32},{48,56},{56,48},{64,72... | collective-permute-start | bytes 67592 | tf_op jit(solution)/shard_map/ppermute | solution.py:493
  77.3 7.4 %collective-permute-start.1 = (f32[8,1280]{1,0:T(8,128)S(1)}, f32[8,1280]{1,0:T(8,128)S(1)}, u32[]{:S(2)}, u32[]{:S(2)}) collective-permute-start(f32[8,1280]{1,0:T(8,128)S(1)} %get-tuple-element.55), channel_id=1, source_target_pairs={{0,248},{8,0},{16,8},{24,16},{32,24},{40,32},{48,40},{56,48},{64,5... | collective-permute-start | bytes 122888 | tf_op jit(solution)/shard_map/ppermute | solution.py:486
  78.2 3.9 %collective-permute-start.7 = (f32[4,1408]{1,0:T(4,128)S(1)}, f32[4,1408]{1,0:T(4,128)S(1)}, u32[]{:S(2)}, u32[]{:S(2)}) collective-permute-start(f32[4,1408]{1,0:T(4,128)S(1)} %add_add_fusion.a_ref), channel_id=1, source_target_pairs={{0,192},{8,72},{16,208},{24,88},{32,224},{40,104},{48,240},{56,120... | collective-permute-start | bytes 67592 | tf_op jit(solution)/shard_map/ppermute | solution.py:493
  78.4 7.8 %collective-permute-start.6 = (f32[4,1408]{1,0:T(4,128)S(1)}, f32[4,1408]{1,0:T(4,128)S(1)}, u32[]{:S(2)}, u32[]{:S(2)}) collective-permute-start(f32[4,1408]{1,0:T(4,128)S(1)} %add_add_fusion.a_ref), channel_id=1, source_target_pairs={{0,128},{8,136},{16,144},{24,152},{32,160},{40,168},{48,176},{56,1... | collective-permute-start | bytes 67592 | tf_op jit(solution)/shard_map/ppermute | solution.py:493
  82.1 4.1 %collective-permute-start.8 = (f32[4,1408]{1,0:T(4,128)S(1)}, f32[4,1408]{1,0:T(4,128)S(1)}, u32[]{:S(2)}, u32[]{:S(2)}) collective-permute-start(f32[4,1408]{1,0:T(4,128)S(1)} %collective-permute-done.7.c_ref), channel_id=1, source_target_pairs={{0,8},{8,0},{16,24},{24,16},{32,40},{40,32},{48,56},{56,48},{64,72... | collective-permute-start | bytes 67592 | tf_op jit(solution)/shard_map/ppermute | solution.py:493
